TPU v7x, 512 devices: a whole 4x4x16 slice. The times are simulated.
512 devices in a mesh: dp: 8 (over z_hi, core), expert: 64 (over x, z_lo, y).
Axes of the slice: x: 4, y: 4, z: 16 (z_hi: 4, z_lo: 4; z = z_hi * 4 + z_lo), core: 2. Of those that a mesh axis runs over, the one named last changes fastest.
Arguments:
- tokens: bfloat16 [98304, 1024], P(('dp', 'expert')), may hold values from -6 to 6
- out_grad: bfloat16 [98304, 1024], P(('dp', 'expert')), may hold values from -2.5 to 2.5
- gates: bfloat16 [98304, 2], P(('dp', 'expert')), may hold values from 0.099609375 to 0.8984375
- expert_ids: int32 [98304, 2], P(('dp', 'expert')), may hold values from 0 to 63, all different within a row; in each aligned block of 192 rows (0 to 191, 192 to 383, ...) at most 9 rows name the same one
- w_in: bfloat16 [64, 1024, 1024], P('expert', None, 'dp'), may hold values from -0.1875 to 0.1875
- w_out: bfloat16 [64, 1024, 1024], P('expert', None, 'dp'), may hold values from -0.1875 to 0.1875
Outputs:
- d_tokens: bfloat16 [98304, 1024], P(('dp', 'expert'))
- gate_grad: bfloat16 [98304, 2], P(('dp', 'expert'))
- grad_in: float32 [64, 1024, 1024], P('expert', None, 'dp')
- grad_out: float32 [64, 1024, 1024], P('expert', None, 'dp')
Inputs may be any that keep to these rules, and one draw needn't show every extreme that they name: `expert_ids`: each row names two different experts. Among the 192 rows of one device no expert is named more than 9 times, and in every draw some device names some expert exactly 9 times.
All inputs are finite; a program needn't handle non-finite values.
Results may differ from a plain program's by a relative error of at most 0.022.
Values may be sent and summed in bfloat16 or wider, within the bound.
No kernel may reach another device: no remote copies, remote signals or barrier semaphores. Data moves between devices by JAX's collectives and lax.ppermute only.
A program may use at most 64 MiB of HBM per device.

v0:
```python
import jax
import jax.numpy as jnp
from jax import lax
from jax.sharding import PartitionSpec as P

gelu_scale = 0.7978845608028654
cubic_coef = 0.044715


def gelu_value(values):
    return (
        0.5
        * values
        * (1.0 + jnp.tanh(gelu_scale * (values + cubic_coef * values * values * values)))
    )


def gelu_slope(values):
    tanh_inner = jnp.tanh(gelu_scale * (values + cubic_coef * values * values * values))
    return 0.5 * (1.0 + tanh_inner) + 0.5 * values * (
        1.0 - tanh_inner * tanh_inner
    ) * gelu_scale * (1.0 + 3.0 * cubic_coef * values * values)


def slot_positions(expert_ids, experts, capacity):
    flat_ids = expert_ids.reshape(-1)
    onehot = (flat_ids[:, None] == jnp.arange(experts, dtype=jnp.int32)[None, :]).astype(jnp.int32)
    earlier = jnp.cumsum(onehot, axis=0) - onehot
    return flat_ids * capacity + jnp.sum(earlier * onehot, axis=1)


def column_terms(rows_x, rows_dy, gate_column, w_first, w_second):
    pre_act = jnp.dot(rows_x, w_first, preferred_element_type=jnp.float32)
    activated = gelu_value(pre_act).astype(jnp.bfloat16)
    dy_proj = jnp.dot(rows_dy, w_second, preferred_element_type=jnp.float32)
    d_pre = (gate_column * dy_proj * gelu_slope(pre_act)).astype(jnp.bfloat16)
    scaled = (gate_column * activated.astype(jnp.float32)).astype(jnp.bfloat16)
    dx_part = lax.dot_general(
        d_pre, w_first, (((1,), (1,)), ((), ())), preferred_element_type=jnp.float32
    )
    gate_part = lax.dot_general(
        activated, w_second, (((1,), (1,)), ((), ())), preferred_element_type=jnp.float32
    )
    return (dx_part, gate_part, d_pre, scaled)


def gate_value(gate_part, rows_dy):
    result = jnp.sum(rows_dy.astype(jnp.float32) * gate_part, axis=1)
    return result


def shards(tokens, out_grad, gates, expert_ids, w_in, w_out):
    tok_rows = tokens.shape[0]
    model_width = tokens.shape[1]
    experts = lax.axis_size("expert")
    capacity = 3 * tok_rows // experts
    slot_count = experts * capacity
    target = slot_positions(expert_ids, experts, capacity)
    source_row = (
        jnp.zeros((slot_count,), jnp.int32)
        .at[target]
        .set(jnp.arange(2 * tok_rows, dtype=jnp.int32) // 2)
    )
    filled = jnp.zeros((slot_count,), jnp.bool_).at[target].set(True)
    send_x = jnp.where(filled[:, None], tokens[source_row], jnp.zeros((), jnp.bfloat16)).reshape(
        experts, capacity, model_width
    )
    send_dy = jnp.where(filled[:, None], out_grad[source_row], jnp.zeros((), jnp.bfloat16)).reshape(
        experts, capacity, model_width
    )
    send_gate = (
        jnp.zeros((slot_count,), jnp.bfloat16)
        .at[target]
        .set(gates.reshape(-1))
        .reshape(experts, capacity)
    )
    got_x, got_dy, got_gate = (
        lax.all_to_all(send_x, "expert", split_axis=0, concat_axis=0, tiled=True),
        lax.all_to_all(send_dy, "expert", split_axis=0, concat_axis=0, tiled=True),
        lax.all_to_all(send_gate, "expert", split_axis=0, concat_axis=0, tiled=True),
    )
    rows_x = got_x.reshape(slot_count, model_width)
    rows_dy = got_dy.reshape(slot_count, model_width)
    gate_column = got_gate.reshape(slot_count, 1).astype(jnp.float32)
    full_in, full_out = (
        lax.all_gather(w_in, "dp", axis=2, tiled=True),
        lax.all_gather(w_out, "dp", axis=2, tiled=True),
    )
    dx_part, gate_part, d_pre, scaled = column_terms(
        rows_x, rows_dy, gate_column, full_in[0], full_out[0]
    )
    dx_rows = dx_part.astype(jnp.bfloat16).reshape(experts, capacity, model_width)
    gate_rows = gate_value(gate_part, rows_dy).astype(jnp.bfloat16).reshape(experts, capacity)
    back_dx, back_gate = (
        lax.all_to_all(dx_rows, "expert", split_axis=0, concat_axis=0, tiled=True),
        lax.all_to_all(gate_rows, "expert", split_axis=0, concat_axis=0, tiled=True),
    )
    grad_first = lax.dot_general(
        rows_x, d_pre, (((0,), (0,)), ((), ())), preferred_element_type=jnp.float32
    )
    grad_second = lax.dot_general(
        rows_dy, scaled, (((0,), (0,)), ((), ())), preferred_element_type=jnp.float32
    )
    grad_in, grad_out = (
        lax.psum_scatter(
            grad_first[None].astype(jnp.bfloat16), "dp", scatter_dimension=2, tiled=True
        ).astype(jnp.float32),
        lax.psum_scatter(
            grad_second[None].astype(jnp.bfloat16), "dp", scatter_dimension=2, tiled=True
        ).astype(jnp.float32),
    )
    picked = back_dx.reshape(slot_count, model_width)[target].reshape(tok_rows, 2, model_width)
    d_tokens = jnp.sum(picked.astype(jnp.float32), axis=1).astype(jnp.bfloat16)
    gate_grad = back_gate.reshape(slot_count)[target].reshape(tok_rows, 2)
    return (d_tokens, gate_grad, grad_in, grad_out)


def solution(mesh):
    in_specs = (
        P(("dp", "expert"), None),
        P(("dp", "expert"), None),
        P(("dp", "expert"), None),
        P(("dp", "expert"), None),
        P("expert", None, "dp"),
        P("expert", None, "dp"),
    )
    out_specs = (
        P(("dp", "expert"), None),
        P(("dp", "expert"), None),
        P("expert", None, "dp"),
        P("expert", None, "dp"),
    )
    return jax.shard_map(shards, mesh=mesh, in_specs=in_specs, out_specs=out_specs, check_vma=False)
```

profile of v0, /device:TPU:6, one launch (start us, length us, event | category | flops | bytes accessed | tf_op | source)
XLA Modules:
  0.0 441.6 jit_solution(18355745456563152464)
XLA Ops:
  7.2 0.7 broadcast_multiply_fusion
  7.9 0.8 copy.17
  8.7 0.1 eq.29
  8.9 0.1 eq.25
  9.0 0.8 copy.20
  9.8 0.2 reshape.171
  10.0 0.1 copy.16
  10.1 0.1 mul.88
  10.3 0.9 reduce-window.6
  11.2 0.2 slice_reduce_fusion
  11.6 3.0 scatter_custom_fusion
  14.6 0.8 all_to_all.25
  15.3 12.2 %all-to-all-start = ((bf16[64,1,9]{2,1,0:T(2,128)(2,1)}), bf16[64,1,9]{2,1,0:T(2,128)(2,1)S(1)}, u32[]{:S(2)}, u32[]{:S(2)}) async-start(bf16[64,1,9]{2,1,0:T(2,128)(2,1)} %all_to_all.25), calls=%async_computation | async-start | bytes 65536 | tf_op jit(solution)/shard_map/all_to_all | solution.py:80
  27.6 2.9 scatter_custom_fusion.2
  30.6 2.0 scatter_custom_fusion.1
  32.5 0.1 broadcast_in_dim.44
  32.7 3.4 gather_fusion.1
  36.1 2.4 gather.19
  38.5 3.4 gather_fusion
  41.9 3.3 gather.17
  45.2 4.0 broadcast_select_fusion.1
  49.2 10.7 %all-to-all-start.1 = ((bf16[64,9,1024]{2,1,0:T(8,128)(2,1)}), bf16[64,9,1024]{2,1,0:T(8,128)(2,1)S(1)}, u32[]{:S(2)}, u32[]{:S(2)}) async-start(bf16[64,9,1024]{2,1,0:T(8,128)(2,1)} %get-tuple-element.12), calls=%async_computation.1 | async-start | bytes 4194304 | tf_op jit(solution)/shard_map/all_to_all | solution.py:79
  59.9 0.7 all-gather.5.cloned.1.call-update
  60.6 76.0 %all-to-all-done.1 = bf16[64,9,1024]{2,1,0:T(8,128)(2,1)S(1)} async-done(((bf16[64,9,1024]{2,1,0:T(8,128)(2,1)}), bf16[64,9,1024]{2,1,0:T(8,128)(2,1)S(1)}, u32[]{:S(2)}, u32[]{:S(2)}) %all-to-all-start.1) | async-done | bytes 1179680 | tf_op jit(solution)/shard_map/all_to_all | solution.py:79
  136.6 10.5 %all-to-all-start.2 = ((bf16[64,9,1024]{2,1,0:T(8,128)(2,1)}), bf16[64,9,1024]{2,1,0:T(8,128)(2,1)}, u32[]{:S(2)}, u32[]{:S(2)}) async-start(bf16[64,9,1024]{2,1,0:T(8,128)(2,1)} %get-tuple-element.13), calls=%async_computation.2 | async-start | bytes 4194304 | tf_op jit(solution)/shard_map/all_to_all | solution.py:78
  147.2 0.7 all-gather.3.cloned.1.call-update
  148.0 0.1 reshape.134
  148.2 1.4 reshape.127
  149.5 70.7 %all-to-all-done.2 = bf16[64,9,1024]{2,1,0:T(8,128)(2,1)} async-done(((bf16[64,9,1024]{2,1,0:T(8,128)(2,1)}), bf16[64,9,1024]{2,1,0:T(8,128)(2,1)}, u32[]{:S(2)}, u32[]{:S(2)}) %all-to-all-start.2) | async-done | bytes 1179680 | tf_op jit(solution)/shard_map/all_to_all | solution.py:78
  220.2 2.5 reshape.128
  222.8 4.9 %fusion.9 = f32[576,1024]{1,0:T(8,128)} fusion(bf16[576,1024]{1,0:T(8,128)(2,1)S(1)} %reshape.128, bf16[1,1024,1024]{2,1,0:T(8,128)(2,1)} %all-gather.5.cloned.1.call-done), kind=kOutput, calls=%fused_computation.23 | convolution fusion | flops 1207959552 | bytes 5636096 | tf_op jit(solution)/shard_map/dot_general | solution.py:33
  227.7 4.8 %fusion.6 = bf16[576,1024]{1,0:T(8,128)(2,1)S(1)} fusion(f32[576,1024]{1,0:T(8,128)} %fusion.9, bf16[576,1024]{1,0:T(8,128)(2,1)S(1)} %copy-done.2, bf16[1,1024,1024]{2,1,0:T(8,128)(2,1)} %all-gather.3.cloned.1.call-done, f32[576]{0:T(1024)S(1)} %reshape.134), kind=kOutput, calls=%fused_computation.15 | convolution fusion | flops 1219756032 | bytes 6818048 | tf_op jit(solution)/shard_map/dot_general | solution.py:35
  232.5 1.0 copy-done.6
  233.5 1.8 convert_bitcast_fusion.1
  235.3 7.7 %copy.24 = bf16[1,1024,1024]{1,0,2:T(2,128)(2,1)} copy(bf16[1,1024,1024]{2,1,0:T(8,128)(2,1)S(1)} %convert_bitcast_fusion.1) | data formatting | bytes 4194304
  243.1 4.4 copy.35
  247.5 1.2 copy-done.3
  248.7 4.0 multiply_reduce_fusion
  252.7 0.8 convert_element_type.89
  253.5 18.0 %all-to-all-start.4 = ((bf16[64,1,9]{2,1,0:T(2,128)(2,1)}), bf16[64,1,9]{2,1,0:T(2,128)(2,1)S(1)}, u32[]{:S(2)}, u32[]{:S(2)}) async-start(bf16[64,1,9]{2,1,0:T(2,128)(2,1)} %convert_element_type.89), calls=%async_computation.4 | async-start | bytes 65536 | tf_op jit(solution)/shard_map/all_to_all | solution.py:96
  271.5 3.4 fusion.17
  274.9 1.6 reshape.129
  276.5 3.0 all-to-all-done.4
  279.5 7.8 %all-to-all-start.3 = ((bf16[64,9,1024]{2,1,0:T(8,128)(2,1)}), bf16[64,9,1024]{2,1,0:T(8,128)(2,1)}, u32[]{:S(2)}, u32[]{:S(2)}) async-start(bf16[64,9,1024]{2,1,0:T(8,128)(2,1)} %reshape.129), calls=%async_computation.3 | async-start | bytes 4194304 | tf_op jit(solution)/shard_map/all_to_all | solution.py:95
  287.3 0.3 reduce-scatter.9.cloned.1.call-start
  287.6 4.3 convert_bitcast_fusion
  292.0 7.7 %copy.26 = bf16[1,1024,1024]{1,0,2:T(2,128)(2,1)} copy(bf16[1,1024,1024]{2,1,0:T(8,128)(2,1)S(1)} %convert_bitcast_fusion) | data formatting | bytes 4194304
  299.7 4.3 copy.34
  304.2 0.1 reshape.132
  304.3 2.8 gather_fusion.3
  307.2 0.2 reshape.133
  307.3 0.7 copy.23
  308.0 19.5 %reduce-scatter.7.cloned.1.call-done = bf16[128,1024]{1,0:T(8,128)(2,1)} async-done(((bf16[1024,1024]{1,0:T(8,128)(2,1)}), bf16[128,1024]{1,0:T(8,128)(2,1)}) %reduce-scatter.7.cloned.1.call-update) | async-done | bytes 262160
  327.5 1.2 reshape_bitcast_fusion.1
  328.7 0.4 copy.25
  329.2 0.8 convert_element_type.82
  330.0 94.8 %reduce-scatter.9.cloned.1.call-done = bf16[128,1024]{1,0:T(8,128)(2,1)} async-done(((bf16[1024,1024]{1,0:T(8,128)(2,1)}), bf16[128,1024]{1,0:T(8,128)(2,1)}) %reduce-scatter.9.cloned.1.call-update) | async-done | bytes 262160
  424.8 1.2 reshape_bitcast_fusion
  426.0 0.4 copy.27
  426.5 0.8 convert_element_type.87
  427.3 2.5 reshape.130
  429.9 2.1 gather_fusion.2
  431.9 0.3 reshape.131
  432.2 2.8 reduce_sum.34
  (32 shorter events, 0.6 us)
Async XLA Ops:
  7.2 25.5 %copy-start = (bf16[192,1024]{1,0:T(8,128)(2,1)S(1)}, bf16[192,1024]{1,0:T(8,128)(2,1)}, u32[]{:S(2)}) copy-start(bf16[192,1024]{1,0:T(8,128)(2,1)} %param.6) | copy-start | bytes 1179652
  15.3 33.8 %all-to-all-start = ((bf16[64,1,9]{2,1,0:T(2,128)(2,1)}), bf16[64,1,9]{2,1,0:T(2,128)(2,1)S(1)}, u32[]{:S(2)}, u32[]{:S(2)}) async-start(bf16[64,1,9]{2,1,0:T(2,128)(2,1)} %all_to_all.25), calls=%async_computation | async-start | bytes 65536 | tf_op jit(solution)/shard_map/all_to_all | solution.py:80
  36.1 2.4 copy-start.1
  49.2 87.4 %all-to-all-start.1 = ((bf16[64,9,1024]{2,1,0:T(8,128)(2,1)}), bf16[64,9,1024]{2,1,0:T(8,128)(2,1)S(1)}, u32[]{:S(2)}, u32[]{:S(2)}) async-start(bf16[64,9,1024]{2,1,0:T(8,128)(2,1)} %get-tuple-element.12), calls=%async_computation.1 | async-start | bytes 4194304 | tf_op jit(solution)/shard_map/all_to_all | solution.py:79
  59.8 163.0 %all-gather.5.cloned.1.call-start = ((), (), s32[]{:S(2)}) async-start(), calls=%async_computation.8 | async-start | bytes 2359296 | tf_op jit(solution)/shard_map/all_gather | solution.py:86
  136.6 83.6 %all-to-all-start.2 = ((bf16[64,9,1024]{2,1,0:T(8,128)(2,1)}), bf16[64,9,1024]{2,1,0:T(8,128)(2,1)}, u32[]{:S(2)}, u32[]{:S(2)}) async-start(bf16[64,9,1024]{2,1,0:T(8,128)(2,1)} %get-tuple-element.13), calls=%async_computation.2 | async-start | bytes 4194304 | tf_op jit(solution)/shard_map/all_to_all | solution.py:78
  147.1 80.5 %all-gather.3.cloned.1.call-start = ((), (), s32[]{:S(2)}) async-start(), calls=%async_computation.7 | async-start | bytes 2359296 | tf_op jit(solution)/shard_map/all_gather | solution.py:87
  147.9 179.6 %reduce-scatter.7.cloned.1.call-start = ((), (), s32[]{:S(2)}) async-start(), calls=%async_computation.9 | async-start | bytes 2359296
  222.8 4.9 %copy-start.4 = (bf16[576,1024]{1,0:T(8,128)(2,1)}, bf16[576,1024]{1,0:T(8,128)(2,1)S(1)}, u32[]{:S(2)}) copy-start(bf16[576,1024]{1,0:T(8,128)(2,1)S(1)} %reshape.128) | copy-start | bytes 3538948
  222.8 4.9 %copy-start.2 = (bf16[576,1024]{1,0:T(8,128)(2,1)S(1)}, bf16[576,1024]{1,0:T(8,128)(2,1)}, u32[]{:S(2)}) copy-start(bf16[576,1024]{1,0:T(8,128)(2,1)} %reshape.127) | copy-start | bytes 3538948
  227.7 5.8 %copy-start.5 = (bf16[576,1024]{1,0:T(8,128)(2,1)S(1)}, bf16[576,1024]{1,0:T(8,128)(2,1)}, u32[]{:S(2)}) copy-start(bf16[576,1024]{1,0:T(8,128)(2,1)} %copy-done.4) | copy-start | bytes 3538948
  232.5 1.0 copy-start.6
  247.4 1.3 copy-start.3
  253.5 26.0 %all-to-all-start.4 = ((bf16[64,1,9]{2,1,0:T(2,128)(2,1)}), bf16[64,1,9]{2,1,0:T(2,128)(2,1)S(1)}, u32[]{:S(2)}, u32[]{:S(2)}) async-start(bf16[64,1,9]{2,1,0:T(2,128)(2,1)} %convert_element_type.89), calls=%async_computation.4 | async-start | bytes 65536 | tf_op jit(solution)/shard_map/all_to_all | solution.py:96
  279.5 147.8 %all-to-all-start.3 = ((bf16[64,9,1024]{2,1,0:T(8,128)(2,1)}), bf16[64,9,1024]{2,1,0:T(8,128)(2,1)}, u32[]{:S(2)}, u32[]{:S(2)}) async-start(bf16[64,9,1024]{2,1,0:T(8,128)(2,1)} %reshape.129), calls=%async_computation.3 | async-start | bytes 4194304 | tf_op jit(solution)/shard_map/all_to_all | solution.py:95
  287.3 137.5 %reduce-scatter.9.cloned.1.call-start = ((), (), s32[]{:S(2)}) async-start(), calls=%async_computation.10 | async-start | bytes 2359296
Sparse Core Ops, SparseCore 0:
  62.8 68.1 all-gather.4
  150.1 70.8 all-gather.2
  247.6 79.8 reduce-scatter.6
  330.2 94.5 reduce-scatter.8
where the time goes:
time: 447 us; the launch traced here: 442 us
  waiting for transfers between devices  265 us (59%)
  local copies, waits for them, and re-layouts  68.7 us (15%)
  starting transfers between devices  59.6 us (13%)
  matrix products  23.2 us (5%)
  between operations  14.1 us (3%)
  other arithmetic  10.5 us (2%)
    unnamed x6, waiting for transfers between devices  116 us
    all_to_all x1, waiting for transfers between devices, shards(): lax.all_to_all(send_dy, 'expert', split_axis=0, concat_axis=0, tiled=True)  76 us
    all_to_all x1, waiting for transfers between devices, shards(): lax.all_to_all(send_x, 'expert', split_axis=0, concat_axis=0, tiled=True)  70.7 us
    unnamed x25, local copies, waits for them, and re-layouts  32.1 us
    all_to_all x1, starting transfers between devices, shards(): lax.all_to_all(gate_rows, 'expert', split_axis=0, concat_axis=0, tiled=True)  18 us
    all_to_all x1, starting transfers between devices, shards(): lax.all_to_all(send_gate, 'expert', split_axis=0, concat_axis=0, tiled=True)  12.2 us
    all_to_all x1, starting transfers between devices, shards(): lax.all_to_all(send_dy, 'expert', split_axis=0, concat_axis=0, tiled=True)  10.7 us
    all_to_all x1, starting transfers between devices, shards(): lax.all_to_all(send_x, 'expert', split_axis=0, concat_axis=0, tiled=True)  10.5 us
  transfers between devices with their start and end apart: 9, of which 5 were waited for; matrix products, arithmetic and copies ran while one was open for 15% of the time, Pallas kernels for 0%

commit v1 on v0

v1 whole, which is shorter than its diff:
```python
import jax
import jax.numpy as jnp
from jax import lax
from jax.experimental import pallas as pl
from jax.experimental.pallas import tpu as pltpu
from jax.sharding import PartitionSpec as P

gelu_scale = 0.7978845608028654
cubic_coef = 0.044715
bf16 = jnp.bfloat16
f32 = jnp.float32
LANES = 128
VMEM_BYTES = 56 << 20


def call(body, out_shape, name, scratch=()):
    return pl.pallas_call(
        body,
        out_shape=out_shape,
        scratch_shapes=scratch,
        name=name,
        compiler_params=pltpu.CompilerParams(vmem_limit_bytes=VMEM_BYTES),
    )


def slot_targets(ids_ref, experts, capacity):
    tokens = ids_ref.shape[1]
    first = ids_ref[0:1, :]
    second = ids_ref[1:2, :]
    expert = lax.broadcasted_iota(jnp.int32, (experts, tokens), 0)
    is_first = (expert == first).astype(f32)
    is_second = (expert == second).astype(f32)
    before = (
        lax.broadcasted_iota(jnp.int32, (tokens, tokens), 0)
        < lax.broadcasted_iota(jnp.int32, (tokens, tokens), 1)
    ).astype(f32)
    earlier = jnp.dot(
        (is_first + is_second).astype(bf16), before.astype(bf16), preferred_element_type=f32
    )
    slot_first = jnp.sum(earlier * is_first, axis=0, keepdims=True).astype(jnp.int32)
    slot_second = jnp.sum(earlier * is_second, axis=0, keepdims=True).astype(jnp.int32)
    return first * capacity + slot_first, second * capacity + slot_second


def one_hots(ids_ref, experts, capacity):
    tokens = ids_ref.shape[1]
    first, second = slot_targets(ids_ref, experts, capacity)
    slot = lax.broadcasted_iota(jnp.int32, (experts * capacity, tokens), 0)
    return (slot == first).astype(f32), (slot == second).astype(f32)


def dispatch_body(experts, capacity, ids_ref, gates_ref, x_ref, dy_ref, out_ref, wide_ref):
    width = x_ref.shape[1] // LANES
    slots = experts * capacity
    pick_first, pick_second = one_hots(ids_ref, experts, capacity)
    gates = gates_ref[...].astype(f32)
    pick = (pick_first + pick_second).astype(bf16)
    gated = (pick_first * gates[0:1, :] + pick_second * gates[1:2, :]).astype(bf16)
    rows_x = jnp.dot(pick, x_ref[...], preferred_element_type=f32)
    rows_dy = jnp.dot(gated, dy_ref[...], preferred_element_type=f32)
    for j in range(width):
        cols = slice(j * LANES, (j + 1) * LANES)
        wide_ref[pl.ds(j, slots, stride=2 * width), :] = rows_x[:, cols]
        wide_ref[pl.ds(width + j, slots, stride=2 * width), :] = rows_dy[:, cols]
    out_ref[...] = wide_ref[...].astype(bf16)


def gelu_parts(pre):
    inner = jnp.tanh(gelu_scale * (pre + cubic_coef * pre * pre * pre))
    value = 0.5 * pre * (1.0 + inner)
    slope = 0.5 * (1.0 + inner) + 0.5 * pre * (1.0 - inner * inner) * gelu_scale * (
        1.0 + 3.0 * cubic_coef * pre * pre
    )
    return value, slope


def units(x, dy, w_first, w_second):
    pre = jnp.dot(x, w_first, preferred_element_type=f32)
    dy_proj = jnp.dot(dy, w_second, preferred_element_type=f32)
    value, slope = gelu_parts(pre)
    activated = value.astype(bf16)
    d_pre = (dy_proj * slope).astype(bf16)
    gate = activated.astype(f32) * dy_proj
    grad_first = lax.dot_general(
        d_pre, x, (((0,), (0,)), ((), ())), preferred_element_type=f32
    )
    grad_second = lax.dot_general(
        activated, dy, (((0,), (0,)), ((), ())), preferred_element_type=f32
    )
    return d_pre, gate, grad_first, grad_second


def own_body(
    mine_ref, other_ref, wi_ref, wo_ref, x_ref, dy_ref, dpre_ref, gate_ref, gi_ref, go_ref, wide_ref
):
    slots = x_ref.shape[0] // 2
    width = x_ref.shape[1] // LANES
    for half, ref in enumerate((mine_ref, other_ref)):
        wide_ref[...] = ref[...].astype(f32)
        rows = slice(half * slots, (half + 1) * slots)
        for j in range(width):
            cols = slice(j * LANES, (j + 1) * LANES)
            x_ref[rows, cols] = wide_ref[pl.ds(j, slots, stride=2 * width), :].astype(bf16)
            dy_ref[rows, cols] = wide_ref[pl.ds(width + j, slots, stride=2 * width), :].astype(bf16)
    d_pre, gate, grad_first, grad_second = units(x_ref[...], dy_ref[...], wi_ref[...], wo_ref[...])
    dpre_ref[...] = d_pre
    gate_ref[...] = gate
    gi_ref[...] = grad_first
    go_ref[...] = grad_second


def near_body(
    x_ref, dy_ref, wim_ref, wom_ref, wip_ref, wop_ref, gate_in_ref,
    dpre_ref, gate_ref, gim_ref, gom_ref, gip_ref, gop_ref,
):
    w_first = jnp.concatenate([wim_ref[...], wip_ref[...]], axis=1)
    w_second = jnp.concatenate([wom_ref[...], wop_ref[...]], axis=1)
    d_pre, gate, grad_first, grad_second = units(x_ref[...], dy_ref[...], w_first, w_second)
    dpre_ref[...] = d_pre
    gate_ref[...] = gate_in_ref[...] + gate[:, :LANES] + gate[:, LANES:]
    gim_ref[...] = grad_first[:LANES].astype(bf16)
    gip_ref[...] = grad_first[LANES:].astype(bf16)
    gom_ref[...] = grad_second[:LANES].astype(bf16)
    gop_ref[...] = grad_second[LANES:].astype(bf16)


def far_body(x_ref, dy_ref, wi_ref, wo_ref, gate_in_ref, dpre_ref, gate_ref, gi_ref, go_ref):
    d_pre, gate, grad_first, grad_second = units(x_ref[...], dy_ref[...], wi_ref[...], wo_ref[...])
    dpre_ref[...] = d_pre
    gate_ref[...] = gate_in_ref[...] + gate
    gi_ref[...] = grad_first.astype(bf16)
    go_ref[...] = grad_second.astype(bf16)


def dx_body(
    dpre0_ref, dpre1_ref, dpre2_ref, w0_ref, wm_ref, wp_ref, wf_ref, gate_ref,
    keep_ref, keep_gate_ref, give_ref,
):
    slots = keep_ref.shape[0]
    width = keep_ref.shape[1]
    d_pre = jnp.concatenate([dpre0_ref[...], dpre1_ref[...], dpre2_ref[...]], axis=1)
    weights = jnp.concatenate([w0_ref[...], wm_ref[...], wp_ref[...], wf_ref[...]], axis=1)
    dx = lax.dot_general(d_pre, weights, (((1,), (1,)), ((), ())), preferred_element_type=f32)
    gate = jnp.sum(gate_ref[...], axis=1, keepdims=True)
    keep_ref[...] = dx[:slots]
    keep_gate_ref[...] = jnp.broadcast_to(gate[:slots], keep_gate_ref.shape)
    give_ref[:, :width] = dx[slots:].astype(bf16)
    coarse = gate[slots:].astype(bf16)
    fine = (gate[slots:] - coarse.astype(f32)).astype(bf16)
    lane = lax.broadcasted_iota(jnp.int32, (slots, LANES), 1)
    give_ref[:, width:] = jnp.where(
        lane == 0, coarse.astype(f32), jnp.where(lane == 1, fine.astype(f32), 0.0)
    ).astype(bf16)


def pack_body(experts, capacity, keep_ref, keep_gate_ref, took_ref, out_ref, rows_ref, wide_ref):
    slots = keep_ref.shape[0]
    width = keep_ref.shape[1]
    tiles = width // LANES
    step = (capacity + 1) * tiles
    for j in range(tiles):
        cols = slice(j * LANES, (j + 1) * LANES)
        total = keep_ref[:, cols] + took_ref[:, cols].astype(f32)
        rows_ref[j] = total.astype(bf16).astype(f32)
    gate = keep_gate_ref[:, 0:1] + jnp.sum(took_ref[:, width:].astype(f32), axis=1, keepdims=True)
    row = lax.broadcasted_iota(jnp.int32, (slots, LANES), 0)
    lane = lax.broadcasted_iota(jnp.int32, (slots, LANES), 1)
    spread = jnp.where(row % capacity == lane, gate, 0.0).astype(bf16)
    expert = lax.broadcasted_iota(jnp.int32, (experts, slots), 0)
    slot = lax.broadcasted_iota(jnp.int32, (experts, slots), 1)
    owner = (slot // capacity == expert).astype(f32).astype(bf16)
    table = jnp.dot(owner, spread, preferred_element_type=f32)
    for c in range(capacity):
        for j in range(tiles):
            wide_ref[pl.ds(c * tiles + j, experts, stride=step), :] = rows_ref[
                j, pl.ds(c, experts, stride=capacity), :
            ]
    for j in range(tiles):
        wide_ref[pl.ds(capacity * tiles + j, experts, stride=step), :] = (
            table if j == 0 else jnp.zeros_like(table)
        )
    out_ref[...] = wide_ref[...].astype(bf16)


def combine_body(
    experts, capacity, ids_ref, gates_ref, back_ref, dtok_ref, dgate_ref, wide_ref, rows_ref
):
    slots = experts * capacity
    tiles = dtok_ref.shape[1] // LANES
    step = (capacity + 1) * tiles
    wide_ref[...] = back_ref[...].astype(f32)
    for c in range(capacity):
        for j in range(tiles):
            rows_ref[j, pl.ds(c, experts, stride=capacity), :] = wide_ref[
                pl.ds(c * tiles + j, experts, stride=step), :
            ]
    table = wide_ref[pl.ds(capacity * tiles, experts, stride=step), :].astype(bf16)
    pick_first, pick_second = one_hots(ids_ref, experts, capacity)
    pick = (pick_first + pick_second).astype(bf16)
    for j in range(tiles):
        dtok_ref[:, j * LANES : (j + 1) * LANES] = lax.dot_general(
            pick, rows_ref[j].astype(bf16), (((0,), (0,)), ((), ())), preferred_element_type=f32
        ).astype(bf16)
    expert = lax.broadcasted_iota(jnp.int32, (slots, experts), 1)
    slot = lax.broadcasted_iota(jnp.int32, (slots, experts), 0)
    owner = (slot // capacity == expert).astype(f32).astype(bf16)
    by_slot = jnp.dot(owner, table, preferred_element_type=f32)
    row = lax.broadcasted_iota(jnp.int32, (slots, LANES), 0)
    lane = lax.broadcasted_iota(jnp.int32, (slots, LANES), 1)
    gate = jnp.sum(jnp.where(row % capacity == lane, by_slot, 0.0), axis=1, keepdims=True)
    gates = gates_ref[...].astype(f32)
    sums = jnp.concatenate(
        [
            jnp.sum(pick_first * gate, axis=0, keepdims=True),
            jnp.sum(pick_second * gate, axis=0, keepdims=True),
        ],
        axis=0,
    )
    dgate_ref[...] = (sums / gates).astype(bf16)


def add_body(a_ref, b_ref, c_ref, d_ref, first_ref, second_ref):
    first_ref[...] = (a_ref[...].astype(f32) + b_ref[...].astype(f32)).astype(bf16)
    second_ref[...] = (c_ref[...].astype(f32) + d_ref[...].astype(f32)).astype(bf16)


def finish_body(own_i, a_i, c_i, own_o, a_o, c_o, gi_ref, go_ref):
    gi_ref[...] = (own_i[...] + a_i[...].astype(f32) + c_i[...].astype(f32)).T
    go_ref[...] = (own_o[...] + a_o[...].astype(f32) + c_o[...].astype(f32)).T


def shards(tokens, out_grad, gates, expert_ids, w_in, w_out):
    tok_rows, width = tokens.shape
    experts = lax.axis_size("expert")
    replicas = lax.axis_size("dp")
    capacity = 3 * tok_rows // experts
    slots = experts * capacity
    tiles = width // LANES
    shard = w_in.shape[2]
    up = [(i, (i + 2) % replicas) for i in range(replicas)]
    down = [(i, (i - 2) % replicas) for i in range(replicas)]
    swap = [(i, i ^ 1) for i in range(replicas)]
    sds = jax.ShapeDtypeStruct

    def send(value, perm):
        return lax.ppermute(value, "dp", perm)

    wi = w_in.reshape(width, shard)
    wo = w_out.reshape(width, shard)
    ids = expert_ids.T
    gates_row = gates.T

    wi_m = send(wi, up)
    wo_p = send(wo, down)
    wi_p = send(wi, down)
    wo_m = send(wo, up)
    wi_f = send(wi_m, up)
    wo_f = send(wo_p, down)

    payload = call(
        lambda *refs: dispatch_body(experts, capacity, *refs),
        sds((slots * 2 * tiles, LANES), bf16),
        "dispatch",
        [pltpu.VMEM((slots * 2 * tiles, LANES), f32)],
    )(ids, gates_row, tokens, out_grad)
    mine = lax.all_to_all(
        payload.reshape(experts, capacity * 2 * tiles, LANES),
        "expert", split_axis=0, concat_axis=0, tiled=True,
    ).reshape(slots * 2 * tiles, LANES)
    other = send(mine, swap)

    rows = sds((2 * slots, width), bf16)
    gate_shape = sds((2 * slots, LANES), f32)
    grad = sds((shard, width), bf16)
    x, dy, dpre0, gate0, own_i, own_o = call(
        own_body,
        (rows, rows, sds((2 * slots, shard), bf16), gate_shape,
         sds((shard, width), f32), sds((shard, width), f32)),
        "own_units",
        [pltpu.VMEM((slots * 2 * tiles, LANES), f32)],
    )(mine, other, wi, wo)
    dpre1, gate1, gi_m, go_m, gi_p, go_p = call(
        near_body,
        (sds((2 * slots, 2 * shard), bf16), gate_shape, grad, grad, grad, grad),
        "near_units",
    )(x, dy, wi_m, wo_m, wi_p, wo_p, gate0)
    a_o = send(go_p, up)
    a_i = send(gi_m, down)
    dpre2, gate2, gi_f, go_f = call(
        far_body,
        (sds((2 * slots, shard), bf16), gate_shape, grad, grad),
        "far_units",
    )(x, dy, wi_f, wo_f, gate1)
    b_i = send(gi_f, up)
    b_o = send(go_f, down)
    keep, keep_gate, give = call(
        dx_body,
        (sds((slots, width), f32), sds((slots, LANES), f32), sds((slots, width + LANES), bf16)),
        "input_gradient",
    )(dpre0, dpre1, dpre2, wi, wi_m, wi_p, wi_f, gate2)
    took = send(give, swap)
    back = call(
        lambda *refs: pack_body(experts, capacity, *refs),
        sds((experts * (capacity + 1) * tiles, LANES), bf16),
        "pack",
        [
            pltpu.VMEM((tiles, slots, LANES), f32),
            pltpu.VMEM((experts * (capacity + 1) * tiles, LANES), f32),
        ],
    )(keep, keep_gate, took)
    back = lax.all_to_all(
        back.reshape(experts, (capacity + 1) * tiles, LANES),
        "expert", split_axis=0, concat_axis=0, tiled=True,
    ).reshape(experts * (capacity + 1) * tiles, LANES)
    sum_i, sum_o = call(add_body, (grad, grad), "add_far")(gi_p, b_i, go_m, b_o)
    c_i = send(sum_i, up)
    c_o = send(sum_o, down)
    d_tokens, gate_grad = call(
        lambda *refs: combine_body(experts, capacity, *refs),
        (sds((tok_rows, width), bf16), sds((2, tok_rows), bf16)),
        "combine",
        [
            pltpu.VMEM((experts * (capacity + 1) * tiles, LANES), f32),
            pltpu.VMEM((tiles, slots, LANES), f32),
        ],
    )(ids, gates_row, back)
    total = sds((width, shard), f32)
    grad_in, grad_out = call(finish_body, (total, total), "finish")(
        own_i, a_i, c_i, own_o, a_o, c_o
    )
    return d_tokens, gate_grad.T, grad_in[None], grad_out[None]


def solution(mesh):
    by_token = P(("dp", "expert"), None)
    by_expert = P("expert", None, "dp")
    return jax.shard_map(
        shards,
        mesh=mesh,
        in_specs=(by_token, by_token, by_token, by_token, by_expert, by_expert),
        out_specs=(by_token, by_token, by_expert, by_expert),
        check_vma=False,
    )
```

time: 447 us -> 311 us (0.70)
  the two profiles are of different devices: /device:TPU:6 before, /device:TPU:39 now
where the time goes in v1:
time: 311 us; the launch traced here: 310 us
  waiting for transfers between devices  100 us (32%)
  starting transfers between devices  90 us (29%)
  blocking collectives  65.3 us (21%)
  Pallas kernels  46.7 us (15%)
  local copies, waits for them, and re-layouts  6.61 us (2%)
    ppermute x14, waiting for transfers between devices, send(): return lax.ppermute(value, 'dp', perm)  100 us
    ppermute x14, starting transfers between devices, send(): return lax.ppermute(value, 'dp', perm)  66.2 us
    all_to_all x1, blocking collectives, shards(): lax.all_to_all(payload.reshape(experts, capacity * 2 * tiles, LANES), 'ex...  65.3 us
    all_to_all x1, starting transfers between devices, shards(): lax.all_to_all(back.reshape(experts, (capacity + 1) * tiles, LANES), 'exp...  23.8 us
    pallas_call x1, Pallas kernels, shards(): call(own_body, (rows, rows, sds((2 * slots, shard), bf16), gate_shape, sd...  10.8 us
    pallas_call x1, Pallas kernels, shards(): call(near_body, (sds((2 * slots, 2 * shard), bf16), gate_shape, grad, gra...  7.09 us
    unnamed x44, local copies, waits for them, and re-layouts  6.61 us
  transfers between devices with their start and end apart: 15, of which 7 were waited for; matrix products, arithmetic and copies ran while one was open for 0% of the time, Pallas kernels for 7%

profile of v1, /device:TPU:39, one launch (start us, length us, event | category | flops | bytes accessed | tf_op | source)
XLA Modules:
  0.0 309.7 jit_solution(17848776329222301074)
XLA Ops:
  0.6 4.7 %dispatch.1 = bf16[9216,128]{1,0:T(8,128)(2,1)} custom-call(s32[2,192]{1,0:T(2,128)} %bitcast.23, bf16[2,192]{1,0:T(2,128)(2,1)} %bitcast.25, bf16[192,1024]{1,0:T(8,128)(2,1)} %refs_2_.1, bf16[192,1024]{1,0:T(8,128)(2,1)} %refs_3_.1), custom_call_target="tpu_custom_call" | custom-call | tf_op jit(solution)/shard_map/dispatch/pallas_call | solution.py:260
  5.3 65.3 %all_to_all.10 = bf16[64,144,128]{2,1,0:T(8,128)(2,1)S(1)} all-to-all(bf16[64,144,128]{2,1,0:T(8,128)(2,1)} %bitcast.13), channel_id=1, replica_groups=mesh['dp'=8,'expert'=64] {'expert'}, dimensions={0} | all-to-all | bytes 4718592 | tf_op jit(solution)/shard_map/all_to_all | solution.py:266
  70.6 3.7 %collective-permute-start = (bf16[9216,128]{1,0:T(8,128)(2,1)S(1)}, bf16[9216,128]{1,0:T(8,128)(2,1)S(1)}, u32[]{:S(2)}, u32[]{:S(2)}) collective-permute-start(bf16[9216,128]{1,0:T(8,128)(2,1)S(1)} %bitcast.11), channel_id=1, source_target_pairs={{0,64},{64,0},{128,192},{192,128},{256,320},{320,256},{384,448},{4... | collective-permute-start | bytes 7077896 | tf_op jit(solution)/shard_map/ppermute | solution.py:246
  74.4 0.0 copy-done.4
  74.4 8.8 %collective-permute-start.1 = (bf16[1024,128]{1,0:T(8,128)(2,1)S(1)}, bf16[1024,128]{1,0:T(8,128)(2,1)S(1)}, u32[]{:S(2)}, u32[]{:S(2)}) collective-permute-start(bf16[1024,128]{1,0:T(8,128)(2,1)S(1)} %bitcast.18), channel_id=1, source_target_pairs={{0,128},{64,192},{128,256},{192,320},{256,384},{320,448},{384,0},{... | collective-permute-start | bytes 786440 | tf_op jit(solution)/shard_map/ppermute | solution.py:246
  83.2 0.0 copy-done.8
  83.2 2.9 collective-permute-start.4
  86.1 7.3 %collective-permute-start.3 = (bf16[1024,128]{1,0:T(8,128)(2,1)S(1)}, bf16[1024,128]{1,0:T(8,128)(2,1)S(1)}, u32[]{:S(2)}, u32[]{:S(2)}) collective-permute-start(bf16[1024,128]{1,0:T(8,128)(2,1)S(1)} %bitcast.19), channel_id=1, source_target_pairs={{0,384},{64,448},{128,0},{192,64},{256,128},{320,192},{384,256},{4... | collective-permute-start | bytes 786440 | tf_op jit(solution)/shard_map/ppermute | solution.py:246
  93.4 1.9 collective-permute-start.2
  95.3 6.7 %collective-permute-done.1.wim_ref.wm_ref = bf16[1024,128]{1,0:T(8,128)(2,1)S(1)} collective-permute-done((bf16[1024,128]{1,0:T(8,128)(2,1)S(1)}, bf16[1024,128]{1,0:T(8,128)(2,1)S(1)}, u32[]{:S(2)}, u32[]{:S(2)}) %collective-permute-start.1) | collective-permute-done | bytes 262176 | tf_op jit(solution)/shard_map/ppermute | solution.py:246
  102.0 7.2 %collective-permute-start.5 = (bf16[1024,128]{1,0:T(8,128)(2,1)S(1)}, bf16[1024,128]{1,0:T(8,128)(2,1)S(1)}, u32[]{:S(2)}, u32[]{:S(2)}) collective-permute-start(bf16[1024,128]{1,0:T(8,128)(2,1)S(1)} %collective-permute-done.1.wim_ref.wm_ref), channel_id=1, source_target_pairs={{0,128},{64,192},{128,256},{192,320},{256,384},{320,448},{384,0},{... | collective-permute-start | bytes 786440 | tf_op jit(solution)/shard_map/ppermute | solution.py:246
  109.2 16.3 %collective-permute-done.4.wop_ref = bf16[1024,128]{1,0:T(8,128)(2,1)S(1)} collective-permute-done((bf16[1024,128]{1,0:T(8,128)(2,1)S(1)}, bf16[1024,128]{1,0:T(8,128)(2,1)S(1)}, u32[]{:S(2)}, u32[]{:S(2)}) %collective-permute-start.4) | collective-permute-done | bytes 262176 | tf_op jit(solution)/shard_map/ppermute | solution.py:246
  125.5 3.1 collective-permute-start.6
  128.6 0.0 collective-permute-done.other_ref
  128.6 0.0 copy-done
  128.6 0.0 copy-start.2
  128.6 1.4 copy-done.2
  130.1 10.8 %own_units.1 = (bf16[1152,1024]{1,0:T(8,128)(2,1)}, bf16[1152,1024]{1,0:T(8,128)(2,1)}, bf16[1152,128]{1,0:T(8,128)(2,1)}, f32[1152,128]{1,0:T(8,128)}, f32[128,1024]{1,0:T(8,128)}, /*index=5*/f32[128,1024]{1,0:T(8,128)}) custom-call(bf16[9216,128]{1,0:T(8,128)(2,1)} %bitcast.12, bf16[9216,128]{1,0:T(8,128)(2,1)} %copy-done.2, bf16[1024,128]{1,0:T(8,128)(2,1)} %bitcast.16, ...), custom_call_target="tpu_custom_call" | custom-call | tf_op jit(solution)/shard_map/own_units/pallas_call | solution.py:275
  140.9 0.0 collective-permute-done.3.wip_ref.wp_ref
  140.9 0.0 collective-permute-done.2.wom_ref
  140.9 0.0 copy-start.10
  140.9 0.0 copy-done.5
  140.9 0.0 copy-done.9
  140.9 0.7 copy-done.6
  141.6 0.0 copy-done.10
  141.6 7.1 %near_units.1 = (bf16[1152,256]{1,0:T(8,128)(2,1)}, f32[1152,128]{1,0:T(8,128)}, bf16[128,1024]{1,0:T(8,128)(2,1)}, bf16[128,1024]{1,0:T(8,128)(2,1)}, bf16[128,...) custom-call(bf16[1152,1024]{1,0:T(8,128)(2,1)} %get-tuple-element.30.x_ref, bf16[1152,1024]{1,0:T(8,128)(2,1)} %get-tuple-element.31.dy_ref, ...), custom_call_target="tpu_custom_call" | custom-call | tf_op jit(solution)/shard_map/near_units/pallas_call | solution.py:282
  148.7 0.0 collective-permute-done.5.wi_ref.wf_ref
  148.7 0.9 collective-permute-done.6.wo_ref
  149.7 0.0 copy-done.7
  149.7 0.7 copy-done.11
  150.4 5.7 %far_units.1 = (bf16[1152,128]{1,0:T(8,128)(2,1)}, f32[1152,128]{1,0:T(8,128)}, bf16[128,1024]{1,0:T(8,128)(2,1)}, bf16[128,1024]{1,0:T(8,128)(2,1)}) custom-call(bf16[1152,1024]{1,0:T(8,128)(2,1)} %get-tuple-element.30.x_ref, bf16[1152,1024]{1,0:T(8,128)(2,1)} %get-tuple-element.31.dy_ref, bf16[1024,128]{1,0:T(8,128)(2,1)} %copy-done.7, ...), custom_call_target="tpu_custom_call" | custom-call | tf_op jit(solution)/shard_map/far_units/pallas_call | solution.py:289
  156.0 5.2 %input_gradient.1 = (f32[576,1024]{1,0:T(8,128)}, f32[576,128]{1,0:T(8,128)}, bf16[576,1152]{1,0:T(8,128)(2,1)}) custom-call(bf16[1152,128]{1,0:T(8,128)(2,1)} %get-tuple-element.29.dpre0_ref, bf16[1152,256]{1,0:T(8,128)(2,1)} %get-tuple-element.33.dpre1_ref, bf16[1152,128]{1,0:T(8,128)(2,1)} %get-tuple-element.35.dpre2_ref, bf16[1024,128]{1,0:T(8,128)(2,1)} %bitcast.17, ...), custom_call_target="tpu_custom_call" | custom-call | tf_op jit(solution)/shard_map/input_gradient/pallas_call | solution.py:296
  161.2 3.5 %collective-permute-start.7 = (bf16[576,1152]{1,0:T(8,128)(2,1)}, bf16[576,1152]{1,0:T(8,128)(2,1)S(1)}, u32[]{:S(2)}, u32[]{:S(2)}) collective-permute-start(bf16[576,1152]{1,0:T(8,128)(2,1)} %get-tuple-element.39), channel_id=1, source_target_pairs={{0,64},{64,0},{128,192},{192,128},{256,320},{320,256},{384,448},{4... | collective-permute-start | bytes 3981320 | tf_op jit(solution)/shard_map/ppermute | solution.py:246
  164.7 2.9 collective-permute-done.7.refs_2_
  167.6 1.1 copy-done.3
  168.7 4.7 %pack.1 = bf16[5120,128]{1,0:T(8,128)(2,1)} custom-call(f32[576,1024]{1,0:T(8,128)} %get-tuple-element.37.refs_0_, f32[576,128]{1,0:T(8,128)} %get-tuple-element.38.refs_1_, bf16[576,1152]{1,0:T(8,128)(2,1)} %copy-done.3), custom_call_target="tpu_custom_call" | custom-call | tf_op jit(solution)/shard_map/pack/pallas_call | solution.py:302
  173.4 23.8 %all-to-all-start.1 = ((bf16[64,80,128]{2,1,0:T(8,128)(2,1)}), bf16[64,80,128]{2,1,0:T(8,128)(2,1)S(1)}, u32[]{:S(2)}, u32[]{:S(2)}) async-start(bf16[64,80,128]{2,1,0:T(8,128)(2,1)} %bitcast.14), calls=%async_computation.1 | async-start | bytes 2621440 | tf_op jit(solution)/shard_map/all_to_all | solution.py:311
  197.2 0.0 copy-done.21
  197.3 7.6 %collective-permute-start.10 = (bf16[128,1024]{1,0:T(8,128)(2,1)S(1)}, bf16[128,1024]{1,0:T(8,128)(2,1)S(1)}, u32[]{:S(2)}, u32[]{:S(2)}) collective-permute-start(bf16[128,1024]{1,0:T(8,128)(2,1)S(1)} %copy-done.21), channel_id=1, source_target_pairs={{0,384},{64,448},{128,0},{192,64},{256,128},{320,192},{384,256},{4... | collective-permute-start | bytes 786440 | tf_op jit(solution)/shard_map/ppermute | solution.py:246
  204.8 0.0 copy-done.20
  204.8 1.9 collective-permute-start.9
  206.7 0.0 copy-done.19
  206.8 4.7 %collective-permute-start.12 = (bf16[128,1024]{1,0:T(8,128)(2,1)S(1)}, bf16[128,1024]{1,0:T(8,128)(2,1)S(1)}, u32[]{:S(2)}, u32[]{:S(2)}) collective-permute-start(bf16[128,1024]{1,0:T(8,128)(2,1)S(1)} %copy-done.19), channel_id=1, source_target_pairs={{0,128},{64,192},{128,256},{192,320},{256,384},{320,448},{384,0},{... | collective-permute-start | bytes 786440 | tf_op jit(solution)/shard_map/ppermute | solution.py:246
  211.4 0.0 copy-done.18
  211.4 4.5 %collective-permute-start.8 = (bf16[128,1024]{1,0:T(8,128)(2,1)S(1)}, bf16[128,1024]{1,0:T(8,128)(2,1)S(1)}, u32[]{:S(2)}, u32[]{:S(2)}) collective-permute-start(bf16[128,1024]{1,0:T(8,128)(2,1)S(1)} %copy-done.18), channel_id=1, source_target_pairs={{0,384},{64,448},{128,0},{192,64},{256,128},{320,192},{384,256},{4... | collective-permute-start | bytes 786440 | tf_op jit(solution)/shard_map/ppermute | solution.py:246
  216.0 16.9 %collective-permute-done.10.d_ref = bf16[128,1024]{1,0:T(8,128)(2,1)S(1)} collective-permute-done((bf16[128,1024]{1,0:T(8,128)(2,1)S(1)}, bf16[128,1024]{1,0:T(8,128)(2,1)S(1)}, u32[]{:S(2)}, u32[]{:S(2)}) %collective-permute-start.10) | collective-permute-done | bytes 262176 | tf_op jit(solution)/shard_map/ppermute | solution.py:246
  232.8 49.4 %collective-permute-done.9.b_ref = bf16[128,1024]{1,0:T(8,128)(2,1)S(1)} collective-permute-done((bf16[128,1024]{1,0:T(8,128)(2,1)S(1)}, bf16[128,1024]{1,0:T(8,128)(2,1)S(1)}, u32[]{:S(2)}, u32[]{:S(2)}) %collective-permute-start.9) | collective-permute-done | bytes 262176 | tf_op jit(solution)/shard_map/ppermute | solution.py:246
  282.2 0.0 copy-done.12
  282.2 0.7 copy-done.13
  282.9 2.0 add_far.1
  284.9 1.9 collective-permute-start.11
  286.9 7.3 %collective-permute-start.13 = (bf16[128,1024]{1,0:T(8,128)(2,1)}, bf16[128,1024]{1,0:T(8,128)(2,1)S(1)}, u32[]{:S(2)}, u32[]{:S(2)}) collective-permute-start(bf16[128,1024]{1,0:T(8,128)(2,1)} %get-tuple-element.51), channel_id=1, source_target_pairs={{0,384},{64,448},{128,0},{192,64},{256,128},{320,192},{384,256},{4... | collective-permute-start | bytes 786440 | tf_op jit(solution)/shard_map/ppermute | solution.py:246
  294.1 0.0 collective-permute-done.12.a_o
  294.1 0.0 copy-start.14
  294.1 0.0 collective-permute-done.8.a_i
  294.2 0.0 copy-start.15
  294.2 7.2 %collective-permute-done.11.c_i = bf16[128,1024]{1,0:T(8,128)(2,1)S(1)} collective-permute-done((bf16[128,1024]{1,0:T(8,128)(2,1)}, bf16[128,1024]{1,0:T(8,128)(2,1)S(1)}, u32[]{:S(2)}, u32[]{:S(2)}) %collective-permute-start.11) | collective-permute-done | bytes 262176 | tf_op jit(solution)/shard_map/ppermute | solution.py:246
  301.4 0.0 collective-permute-done.13.c_o
  301.4 0.7 copy-done.16
  302.0 0.1 copy-done.17
  302.2 2.7 finish.1
  304.8 0.0 all-to-all-done.1
  304.9 1.1 copy-done.1
  305.9 3.8 %combine.1 = (bf16[192,1024]{1,0:T(8,128)(2,1)}, bf16[2,192]{1,0:T(2,128)(2,1)}) custom-call(s32[2,192]{1,0:T(2,128)} %bitcast.24, bf16[2,192]{1,0:T(2,128)(2,1)} %bitcast.26, bf16[5120,128]{1,0:T(8,128)(2,1)} %bitcast.15), custom_call_target="tpu_custom_call" | custom-call | tf_op jit(solution)/shard_map/combine/pallas_call | solution.py:318
  (20 shorter events, 0.0 us)
Async XLA Ops:
  5.3 69.1 %copy-start.4 = (bf16[1,1024,128]{2,1,0:T(8,128)(2,1)S(1)}, bf16[1,1024,128]{2,1,0:T(8,128)(2,1)}, u32[]{:S(2)}) copy-start(bf16[1,1024,128]{2,1,0:T(8,128)(2,1)} %param.10) | copy-start | bytes 786436
  5.3 77.9 %copy-start.8 = (bf16[1,1024,128]{2,1,0:T(8,128)(2,1)S(1)}, bf16[1,1024,128]{2,1,0:T(8,128)(2,1)}, u32[]{:S(2)}) copy-start(bf16[1,1024,128]{2,1,0:T(8,128)(2,1)} %param.11) | copy-start | bytes 786436
  70.6 58.0 %copy-start = (bf16[64,144,128]{2,1,0:T(8,128)(2,1)}, bf16[64,144,128]{2,1,0:T(8,128)(2,1)S(1)}, u32[]{:S(2)}) copy-start(bf16[64,144,128]{2,1,0:T(8,128)(2,1)S(1)} %all_to_all.10) | copy-start | bytes 7077892
  70.6 58.0 %collective-permute-start = (bf16[9216,128]{1,0:T(8,128)(2,1)S(1)}, bf16[9216,128]{1,0:T(8,128)(2,1)S(1)}, u32[]{:S(2)}, u32[]{:S(2)}) collective-permute-start(bf16[9216,128]{1,0:T(8,128)(2,1)S(1)} %bitcast.11), channel_id=1, source_target_pairs={{0,64},{64,0},{128,192},{192,128},{256,320},{320,256},{384,448},{4... | collective-permute-start | bytes 7077896 | tf_op jit(solution)/shard_map/ppermute | solution.py:246
  74.4 27.6 %collective-permute-start.1 = (bf16[1024,128]{1,0:T(8,128)(2,1)S(1)}, bf16[1024,128]{1,0:T(8,128)(2,1)S(1)}, u32[]{:S(2)}, u32[]{:S(2)}) collective-permute-start(bf16[1024,128]{1,0:T(8,128)(2,1)S(1)} %bitcast.18), channel_id=1, source_target_pairs={{0,128},{64,192},{128,256},{192,320},{256,384},{320,448},{384,0},{... | collective-permute-start | bytes 786440 | tf_op jit(solution)/shard_map/ppermute | solution.py:246
  83.2 42.3 %collective-permute-start.4 = (bf16[1024,128]{1,0:T(8,128)(2,1)S(1)}, bf16[1024,128]{1,0:T(8,128)(2,1)S(1)}, u32[]{:S(2)}, u32[]{:S(2)}) collective-permute-start(bf16[1024,128]{1,0:T(8,128)(2,1)S(1)} %bitcast.21), channel_id=1, source_target_pairs={{0,384},{64,448},{128,0},{192,64},{256,128},{320,192},{384,256},{4... | collective-permute-start | bytes 786440 | tf_op jit(solution)/shard_map/ppermute | solution.py:246
  86.1 54.8 %collective-permute-start.3 = (bf16[1024,128]{1,0:T(8,128)(2,1)S(1)}, bf16[1024,128]{1,0:T(8,128)(2,1)S(1)}, u32[]{:S(2)}, u32[]{:S(2)}) collective-permute-start(bf16[1024,128]{1,0:T(8,128)(2,1)S(1)} %bitcast.19), channel_id=1, source_target_pairs={{0,384},{64,448},{128,0},{192,64},{256,128},{320,192},{384,256},{4... | collective-permute-start | bytes 786440 | tf_op jit(solution)/shard_map/ppermute | solution.py:246
  93.4 47.5 %collective-permute-start.2 = (bf16[1024,128]{1,0:T(8,128)(2,1)S(1)}, bf16[1024,128]{1,0:T(8,128)(2,1)S(1)}, u32[]{:S(2)}, u32[]{:S(2)}) collective-permute-start(bf16[1024,128]{1,0:T(8,128)(2,1)S(1)} %bitcast.22), channel_id=1, source_target_pairs={{0,128},{64,192},{128,256},{192,320},{256,384},{320,448},{384,0},{... | collective-permute-start | bytes 786440 | tf_op jit(solution)/shard_map/ppermute | solution.py:246
  102.0 38.9 %copy-start.5 = (bf16[1024,128]{1,0:T(8,128)(2,1)}, bf16[1024,128]{1,0:T(8,128)(2,1)S(1)}, u32[]{:S(2)}) copy-start(bf16[1024,128]{1,0:T(8,128)(2,1)S(1)} %collective-permute-done.1.wim_ref.wm_ref) | copy-start | bytes 786436
  102.0 46.8 %collective-permute-start.5 = (bf16[1024,128]{1,0:T(8,128)(2,1)S(1)}, bf16[1024,128]{1,0:T(8,128)(2,1)S(1)}, u32[]{:S(2)}, u32[]{:S(2)}) collective-permute-start(bf16[1024,128]{1,0:T(8,128)(2,1)S(1)} %collective-permute-done.1.wim_ref.wm_ref), channel_id=1, source_target_pairs={{0,128},{64,192},{128,256},{192,320},{256,384},{320,448},{384,0},{... | collective-permute-start | bytes 786440 | tf_op jit(solution)/shard_map/ppermute | solution.py:246
  125.5 15.4 %copy-start.9 = (bf16[1024,128]{1,0:T(8,128)(2,1)}, bf16[1024,128]{1,0:T(8,128)(2,1)S(1)}, u32[]{:S(2)}) copy-start(bf16[1024,128]{1,0:T(8,128)(2,1)S(1)} %collective-permute-done.4.wop_ref) | copy-start | bytes 786436
  125.5 24.2 %collective-permute-start.6 = (bf16[1024,128]{1,0:T(8,128)(2,1)S(1)}, bf16[1024,128]{1,0:T(8,128)(2,1)S(1)}, u32[]{:S(2)}, u32[]{:S(2)}) collective-permute-start(bf16[1024,128]{1,0:T(8,128)(2,1)S(1)} %collective-permute-done.4.wop_ref), channel_id=1, source_target_pairs={{0,384},{64,448},{128,0},{192,64},{256,128},{320,192},{384,256},{4... | collective-permute-start | bytes 786440 | tf_op jit(solution)/shard_map/ppermute | solution.py:246
  128.6 1.4 copy-start.2
  140.9 0.8 copy-start.6
  140.9 0.8 copy-start.10
  148.7 0.9 copy-start.7
  149.7 0.7 copy-start.11
  161.2 6.3 %collective-permute-start.7 = (bf16[576,1152]{1,0:T(8,128)(2,1)}, bf16[576,1152]{1,0:T(8,128)(2,1)S(1)}, u32[]{:S(2)}, u32[]{:S(2)}) collective-permute-start(bf16[576,1152]{1,0:T(8,128)(2,1)} %get-tuple-element.39), channel_id=1, source_target_pairs={{0,64},{64,0},{128,192},{192,128},{256,320},{320,256},{384,448},{4... | collective-permute-start | bytes 3981320 | tf_op jit(solution)/shard_map/ppermute | solution.py:246
  167.6 1.1 copy-start.3
  173.4 23.9 %copy-start.21 = (bf16[128,1024]{1,0:T(8,128)(2,1)S(1)}, bf16[128,1024]{1,0:T(8,128)(2,1)}, u32[]{:S(2)}) copy-start(bf16[128,1024]{1,0:T(8,128)(2,1)} %get-tuple-element.47) | copy-start | bytes 786436
  173.4 31.4 %copy-start.20 = (bf16[128,1024]{1,0:T(8,128)(2,1)S(1)}, bf16[128,1024]{1,0:T(8,128)(2,1)}, u32[]{:S(2)}) copy-start(bf16[128,1024]{1,0:T(8,128)(2,1)} %get-tuple-element.45) | copy-start | bytes 786436
  173.4 33.4 %copy-start.19 = (bf16[128,1024]{1,0:T(8,128)(2,1)S(1)}, bf16[128,1024]{1,0:T(8,128)(2,1)}, u32[]{:S(2)}) copy-start(bf16[128,1024]{1,0:T(8,128)(2,1)} %get-tuple-element.50) | copy-start | bytes 786436
  173.4 38.0 %copy-start.18 = (bf16[128,1024]{1,0:T(8,128)(2,1)S(1)}, bf16[128,1024]{1,0:T(8,128)(2,1)}, u32[]{:S(2)}) copy-start(bf16[128,1024]{1,0:T(8,128)(2,1)} %get-tuple-element.43) | copy-start | bytes 786436
  173.4 131.4 %all-to-all-start.1 = ((bf16[64,80,128]{2,1,0:T(8,128)(2,1)}), bf16[64,80,128]{2,1,0:T(8,128)(2,1)S(1)}, u32[]{:S(2)}, u32[]{:S(2)}) async-start(bf16[64,80,128]{2,1,0:T(8,128)(2,1)} %bitcast.14), calls=%async_computation.1 | async-start | bytes 2621440 | tf_op jit(solution)/shard_map/all_to_all | solution.py:311
  197.3 35.6 %collective-permute-start.10 = (bf16[128,1024]{1,0:T(8,128)(2,1)S(1)}, bf16[128,1024]{1,0:T(8,128)(2,1)S(1)}, u32[]{:S(2)}, u32[]{:S(2)}) collective-permute-start(bf16[128,1024]{1,0:T(8,128)(2,1)S(1)} %copy-done.21), channel_id=1, source_target_pairs={{0,384},{64,448},{128,0},{192,64},{256,128},{320,192},{384,256},{4... | collective-permute-start | bytes 786440 | tf_op jit(solution)/shard_map/ppermute | solution.py:246
  204.8 77.4 %collective-permute-start.9 = (bf16[128,1024]{1,0:T(8,128)(2,1)S(1)}, bf16[128,1024]{1,0:T(8,128)(2,1)S(1)}, u32[]{:S(2)}, u32[]{:S(2)}) collective-permute-start(bf16[128,1024]{1,0:T(8,128)(2,1)S(1)} %copy-done.20), channel_id=1, source_target_pairs={{0,128},{64,192},{128,256},{192,320},{256,384},{320,448},{384,0},{... | collective-permute-start | bytes 786440 | tf_op jit(solution)/shard_map/ppermute | solution.py:246
  206.8 87.4 %collective-permute-start.12 = (bf16[128,1024]{1,0:T(8,128)(2,1)S(1)}, bf16[128,1024]{1,0:T(8,128)(2,1)S(1)}, u32[]{:S(2)}, u32[]{:S(2)}) collective-permute-start(bf16[128,1024]{1,0:T(8,128)(2,1)S(1)} %copy-done.19), channel_id=1, source_target_pairs={{0,128},{64,192},{128,256},{192,320},{256,384},{320,448},{384,0},{... | collective-permute-start | bytes 786440 | tf_op jit(solution)/shard_map/ppermute | solution.py:246
  211.4 82.7 %collective-permute-start.8 = (bf16[128,1024]{1,0:T(8,128)(2,1)S(1)}, bf16[128,1024]{1,0:T(8,128)(2,1)S(1)}, u32[]{:S(2)}, u32[]{:S(2)}) collective-permute-start(bf16[128,1024]{1,0:T(8,128)(2,1)S(1)} %copy-done.18), channel_id=1, source_target_pairs={{0,384},{64,448},{128,0},{192,64},{256,128},{320,192},{384,256},{4... | collective-permute-start | bytes 786440 | tf_op jit(solution)/shard_map/ppermute | solution.py:246
  232.8 49.4 %copy-start.12 = (bf16[128,1024]{1,0:T(8,128)(2,1)}, bf16[128,1024]{1,0:T(8,128)(2,1)S(1)}, u32[]{:S(2)}) copy-start(bf16[128,1024]{1,0:T(8,128)(2,1)S(1)} %collective-permute-done.10.d_ref) | copy-start | bytes 786436
  282.2 0.7 copy-start.13
  284.9 16.4 %collective-permute-start.11 = (bf16[128,1024]{1,0:T(8,128)(2,1)}, bf16[128,1024]{1,0:T(8,128)(2,1)S(1)}, u32[]{:S(2)}, u32[]{:S(2)}) collective-permute-start(bf16[128,1024]{1,0:T(8,128)(2,1)} %get-tuple-element.48), channel_id=1, source_target_pairs={{0,128},{64,192},{128,256},{192,320},{256,384},{320,448},{384,0},{... | collective-permute-start | bytes 786440 | tf_op jit(solution)/shard_map/ppermute | solution.py:246
  286.9 14.5 %collective-permute-start.13 = (bf16[128,1024]{1,0:T(8,128)(2,1)}, bf16[128,1024]{1,0:T(8,128)(2,1)S(1)}, u32[]{:S(2)}, u32[]{:S(2)}) collective-permute-start(bf16[128,1024]{1,0:T(8,128)(2,1)} %get-tuple-element.51), channel_id=1, source_target_pairs={{0,384},{64,448},{128,0},{192,64},{256,128},{320,192},{384,256},{4... | collective-permute-start | bytes 786440 | tf_op jit(solution)/shard_map/ppermute | solution.py:246
  294.1 7.2 %copy-start.14 = (bf16[128,1024]{1,0:T(8,128)(2,1)}, bf16[128,1024]{1,0:T(8,128)(2,1)S(1)}, u32[]{:S(2)}) copy-start(bf16[128,1024]{1,0:T(8,128)(2,1)S(1)} %collective-permute-done.12.a_o) | copy-start | bytes 786436
  294.2 7.2 %copy-start.15 = (bf16[128,1024]{1,0:T(8,128)(2,1)}, bf16[128,1024]{1,0:T(8,128)(2,1)S(1)}, u32[]{:S(2)}) copy-start(bf16[128,1024]{1,0:T(8,128)(2,1)S(1)} %collective-permute-done.8.a_i) | copy-start | bytes 786436
  301.4 0.7 copy-start.16
  301.4 0.8 copy-start.17
  304.8 1.1 copy-start.1

commit v2 on v1

--- a/solution.py
+++ b/solution.py
@@ -110,11 +110,12 @@
 
 
 def near_body(
-    x_ref, dy_ref, wim_ref, wom_ref, wip_ref, wop_ref, gate_in_ref,
+    x_ref, dy_ref, wm_ref, wp_ref, gate_in_ref,
     dpre_ref, gate_ref, gim_ref, gom_ref, gip_ref, gop_ref,
 ):
-    w_first = jnp.concatenate([wim_ref[...], wip_ref[...]], axis=1)
-    w_second = jnp.concatenate([wom_ref[...], wop_ref[...]], axis=1)
+    width = x_ref.shape[1]
+    w_first = jnp.concatenate([wm_ref[:width], wp_ref[:width]], axis=1)
+    w_second = jnp.concatenate([wm_ref[width:], wp_ref[width:]], axis=1)
     d_pre, gate, grad_first, grad_second = units(x_ref[...], dy_ref[...], w_first, w_second)
     dpre_ref[...] = d_pre
     gate_ref[...] = gate_in_ref[...] + gate[:, :LANES] + gate[:, LANES:]
@@ -139,7 +140,7 @@
     slots = keep_ref.shape[0]
     width = keep_ref.shape[1]
     d_pre = jnp.concatenate([dpre0_ref[...], dpre1_ref[...], dpre2_ref[...]], axis=1)
-    weights = jnp.concatenate([w0_ref[...], wm_ref[...], wp_ref[...], wf_ref[...]], axis=1)
+    weights = jnp.concatenate([w0_ref[...], wm_ref[:width], wp_ref[:width], wf_ref[...]], axis=1)
     dx = lax.dot_general(d_pre, weights, (((1,), (1,)), ((), ())), preferred_element_type=f32)
     gate = jnp.sum(gate_ref[...], axis=1, keepdims=True)
     keep_ref[...] = dx[:slots]
@@ -219,14 +220,16 @@
     dgate_ref[...] = (sums / gates).astype(bf16)
 
 
-def add_body(a_ref, b_ref, c_ref, d_ref, first_ref, second_ref):
-    first_ref[...] = (a_ref[...].astype(f32) + b_ref[...].astype(f32)).astype(bf16)
-    second_ref[...] = (c_ref[...].astype(f32) + d_ref[...].astype(f32)).astype(bf16)
-
-
-def finish_body(own_i, a_i, c_i, own_o, a_o, c_o, gi_ref, go_ref):
-    gi_ref[...] = (own_i[...] + a_i[...].astype(f32) + c_i[...].astype(f32)).T
-    go_ref[...] = (own_o[...] + a_o[...].astype(f32) + c_o[...].astype(f32)).T
+def add_body(near_i, far_i, near_o, far_o, own_i, a_i, own_o, a_o, si_ref, so_ref, ti_ref, to_ref):
+    si_ref[...] = (near_i[...].astype(f32) + far_i[...].astype(f32)).astype(bf16)
+    so_ref[...] = (near_o[...].astype(f32) + far_o[...].astype(f32)).astype(bf16)
+    ti_ref[...] = own_i[...] + a_i[...].astype(f32)
+    to_ref[...] = own_o[...] + a_o[...].astype(f32)
+
+
+def finish_body(total_i, c_i, total_o, c_o, gi_ref, go_ref):
+    gi_ref[...] = (total_i[...] + c_i[...].astype(f32)).T
+    go_ref[...] = (total_o[...] + c_o[...].astype(f32)).T
 
 
 def shards(tokens, out_grad, gates, expert_ids, w_in, w_out):
@@ -250,12 +253,9 @@
     ids = expert_ids.T
     gates_row = gates.T
 
-    wi_m = send(wi, up)
-    wo_p = send(wo, down)
-    wi_p = send(wi, down)
-    wo_m = send(wo, up)
-    wi_f = send(wi_m, up)
-    wo_f = send(wo_p, down)
+    both = jnp.concatenate([wi, wo], axis=0)
+    w_m = send(both, up)
+    w_p = send(both, down)
 
     payload = call(
         lambda *refs: dispatch_body(experts, capacity, *refs),
@@ -267,6 +267,9 @@
         payload.reshape(experts, capacity * 2 * tiles, LANES),
         "expert", split_axis=0, concat_axis=0, tiled=True,
     ).reshape(slots * 2 * tiles, LANES)
+    wi_f = send(w_m[:width], up)
+    wo_f = send(w_p[width:], down)
+    mine, w_m, w_p = lax.optimization_barrier((mine, w_m, w_p))
     other = send(mine, swap)
 
     rows = sds((2 * slots, width), bf16)
@@ -283,7 +286,7 @@
         near_body,
         (sds((2 * slots, 2 * shard), bf16), gate_shape, grad, grad, grad, grad),
         "near_units",
-    )(x, dy, wi_m, wo_m, wi_p, wo_p, gate0)
+    )(x, dy, w_m, w_p, gate0)
     a_o = send(go_p, up)
     a_i = send(gi_m, down)
     dpre2, gate2, gi_f, go_f = call(
@@ -293,11 +296,12 @@
     )(x, dy, wi_f, wo_f, gate1)
     b_i = send(gi_f, up)
     b_o = send(go_f, down)
+    gate2, a_i, a_o = lax.optimization_barrier((gate2, a_i, a_o))
     keep, keep_gate, give = call(
         dx_body,
         (sds((slots, width), f32), sds((slots, LANES), f32), sds((slots, width + LANES), bf16)),
         "input_gradient",
-    )(dpre0, dpre1, dpre2, wi, wi_m, wi_p, wi_f, gate2)
+    )(dpre0, dpre1, dpre2, wi, w_m, w_p, wi_f, gate2)
     took = send(give, swap)
     back = call(
         lambda *refs: pack_body(experts, capacity, *refs),
@@ -308,11 +312,15 @@
             pltpu.VMEM((experts * (capacity + 1) * tiles, LANES), f32),
         ],
     )(keep, keep_gate, took)
+    part = sds((shard, width), f32)
+    sum_i, sum_o, part_i, part_o = call(add_body, (grad, grad, part, part), "add_far")(
+        gi_p, b_i, go_m, b_o, own_i, a_i, own_o, a_o
+    )
+    back, sum_i, sum_o = lax.optimization_barrier((back, sum_i, sum_o))
     back = lax.all_to_all(
         back.reshape(experts, (capacity + 1) * tiles, LANES),
         "expert", split_axis=0, concat_axis=0, tiled=True,
     ).reshape(experts * (capacity + 1) * tiles, LANES)
-    sum_i, sum_o = call(add_body, (grad, grad), "add_far")(gi_p, b_i, go_m, b_o)
     c_i = send(sum_i, up)
     c_o = send(sum_o, down)
     d_tokens, gate_grad = call(
@@ -326,7 +334,7 @@
     )(ids, gates_row, back)
     total = sds((width, shard), f32)
     grad_in, grad_out = call(finish_body, (total, total), "finish")(
-        own_i, a_i, c_i, own_o, a_o, c_o
+        part_i, c_i, part_o, c_o
     )
     return d_tokens, gate_grad.T, grad_in[None], grad_out[None]
 

time: 311 us -> 297 us (0.955)
  the two profiles are of different devices: /device:TPU:39 before, /device:TPU:38 now
where the time goes in v2:
time: 297 us; the launch traced here: 296 us
  waiting for transfers between devices  161 us (54%)
  starting transfers between devices  80.4 us (27%)
  Pallas kernels  47.4 us (16%)
  local copies, waits for them, and re-layouts  5.99 us (2%)
    ppermute x12, waiting for transfers between devices, send(): return lax.ppermute(value, 'dp', perm)  161 us
    ppermute x12, starting transfers between devices, send(): return lax.ppermute(value, 'dp', perm)  55.6 us
    all_to_all x1, starting transfers between devices, shards(): lax.all_to_all(back.reshape(experts, (capacity + 1) * tiles, LANES), 'exp...  12.8 us
    all_to_all x1, starting transfers between devices, shards(): lax.all_to_all(payload.reshape(experts, capacity * 2 * tiles, LANES), 'ex...  11.9 us
    pallas_call x1, Pallas kernels, shards(): call(own_body, (rows, rows, sds((2 * slots, shard), bf16), gate_shape, sd...  10.8 us
    pallas_call x1, Pallas kernels, shards(): call(near_body, (sds((2 * slots, 2 * shard), bf16), gate_shape, grad, gra...  7.1 us
    unnamed x40, local copies, waits for them, and re-layouts  5.95 us
  transfers between devices with their start and end apart: 14, of which 5 were waited for; matrix products, arithmetic and copies ran while one was open for 0% of the time, Pallas kernels for 10%

profile of v2, /device:TPU:38, one launch (start us, length us, event | category | flops | bytes accessed | tf_op | source)
XLA Modules:
  0.0 295.9 jit_solution(5645096236242219853)
XLA Ops:
  0.6 4.7 %dispatch.1 = bf16[9216,128]{1,0:T(8,128)(2,1)} custom-call(s32[2,192]{1,0:T(2,128)} %bitcast.21, bf16[2,192]{1,0:T(2,128)(2,1)} %bitcast.23, bf16[192,1024]{1,0:T(8,128)(2,1)} %refs_2_.1, bf16[192,1024]{1,0:T(8,128)(2,1)} %refs_3_.1), custom_call_target="tpu_custom_call" | custom-call | tf_op jit(solution)/shard_map/dispatch/pallas_call | solution.py:260
  5.3 0.0 copy-start.4
  5.3 0.0 copy-start.8
  5.3 11.9 %all-to-all-start = ((bf16[64,144,128]{2,1,0:T(8,128)(2,1)}), bf16[64,144,128]{2,1,0:T(8,128)(2,1)S(1)}, u32[]{:S(2)}, u32[]{:S(2)}) async-start(bf16[64,144,128]{2,1,0:T(8,128)(2,1)} %bitcast.13), calls=%async_computation | async-start | bytes 4718592 | tf_op jit(solution)/shard_map/all_to_all | solution.py:266
  17.3 0.0 copy-done.4
  17.3 0.0 copy-done.8
  17.3 9.1 %collective-permute-start = (bf16[2048,128]{1,0:T(8,128)(2,1)S(1)}, bf16[2048,128]{1,0:T(8,128)(2,1)S(1)}, u32[]{:S(2)}, u32[]{:S(2)}) collective-permute-start(bf16[2048,128]{1,0:T(8,128)(2,1)S(1)} %pad_maximum_fusion), channel_id=1, source_target_pairs={{0,128},{64,192},{128,256},{192,320},{256,384},{320,448},{384,0},{... | collective-permute-start | bytes 1572872 | tf_op jit(solution)/shard_map/ppermute | solution.py:249
  26.4 2.8 collective-permute-start.1
  29.3 92.0 %collective-permute-done.wm_ref = bf16[2048,128]{1,0:T(8,128)(2,1)S(1)} collective-permute-done((bf16[2048,128]{1,0:T(8,128)(2,1)S(1)}, bf16[2048,128]{1,0:T(8,128)(2,1)S(1)}, u32[]{:S(2)}, u32[]{:S(2)}) %collective-permute-start) | collective-permute-done | bytes 524320 | tf_op jit(solution)/shard_map/ppermute | solution.py:249
  121.3 0.0 copy-start.2
  121.3 0.0 collective-permute-done.1.wp_ref
  121.3 0.0 all-to-all-done
  121.3 0.0 copy-start
  121.3 1.9 collective-permute-start.2
  123.2 1.9 collective-permute-start.3
  125.2 8.0 %collective-permute-start.4 = (bf16[1024,128]{1,0:T(8,128)(2,1)S(1)}, bf16[1024,128]{1,0:T(8,128)(2,1)S(1)}, u32[]{:S(2)}, u32[]{:S(2)}) collective-permute-start(bf16[1024,128]{1,0:T(8,128)(2,1)S(1)} %slice.9), channel_id=1, source_target_pairs={{0,384},{64,448},{128,0},{192,64},{256,128},{320,192},{384,256},{4... | collective-permute-start | bytes 786440 | tf_op jit(solution)/shard_map/ppermute | solution.py:249
  133.2 0.0 collective-permute-done.2.other_ref
  133.2 0.0 copy-done
  133.2 0.0 copy-start.5
  133.2 1.4 copy-done.5
  134.7 10.8 %own_units.1 = (bf16[1152,1024]{1,0:T(8,128)(2,1)}, bf16[1152,1024]{1,0:T(8,128)(2,1)}, bf16[1152,128]{1,0:T(8,128)(2,1)}, f32[1152,128]{1,0:T(8,128)}, f32[128,1024]{1,0:T(8,128)}, /*index=5*/f32[128,1024]{1,0:T(8,128)}) custom-call(bf16[9216,128]{1,0:T(8,128)(2,1)} %bitcast.12, bf16[9216,128]{1,0:T(8,128)(2,1)} %copy-done.5, bf16[1024,128]{1,0:T(8,128)(2,1)} %bitcast.16, ...), custom_call_target="tpu_custom_call" | custom-call | tf_op jit(solution)/shard_map/own_units/pallas_call | solution.py:278
  145.5 0.0 copy-done.2
  145.5 0.0 copy-done.3
  145.5 7.1 %near_units.1 = (bf16[1152,256]{1,0:T(8,128)(2,1)}, f32[1152,128]{1,0:T(8,128)}, bf16[128,1024]{1,0:T(8,128)(2,1)}, bf16[128,1024]{1,0:T(8,128)(2,1)}, bf16[128,...) custom-call(bf16[1152,1024]{1,0:T(8,128)(2,1)} %get-tuple-element.42.x_ref, bf16[1152,1024]{1,0:T(8,128)(2,1)} %get-tuple-element.43.dy_ref, ...), custom_call_target="tpu_custom_call" | custom-call | tf_op jit(solution)/shard_map/near_units/pallas_call | solution.py:285
  152.6 5.4 %collective-permute-start.5 = (bf16[128,1024]{1,0:T(8,128)(2,1)}, bf16[128,1024]{1,0:T(8,128)(2,1)S(1)}, u32[]{:S(2)}, u32[]{:S(2)}) collective-permute-start(bf16[128,1024]{1,0:T(8,128)(2,1)} %get-tuple-element.51), channel_id=1, source_target_pairs={{0,384},{64,448},{128,0},{192,64},{256,128},{320,192},{384,256},{4... | collective-permute-start | bytes 786440 | tf_op jit(solution)/shard_map/ppermute | solution.py:249
  158.0 4.6 %collective-permute-start.6 = (bf16[128,1024]{1,0:T(8,128)(2,1)}, bf16[128,1024]{1,0:T(8,128)(2,1)S(1)}, u32[]{:S(2)}, u32[]{:S(2)}) collective-permute-start(bf16[128,1024]{1,0:T(8,128)(2,1)} %get-tuple-element.52), channel_id=1, source_target_pairs={{0,128},{64,192},{128,256},{192,320},{256,384},{320,448},{384,0},{... | collective-permute-start | bytes 786440 | tf_op jit(solution)/shard_map/ppermute | solution.py:249
  162.6 0.0 collective-permute-done.3.wi_ref.wf_ref
  162.6 0.0 copy-start.7
  162.6 0.0 collective-permute-done.4.wo_ref
  162.6 0.0 copy-start.11
  162.6 0.7 copy-done.7
  163.3 0.1 copy-done.11
  163.4 5.7 %far_units.1 = (bf16[1152,128]{1,0:T(8,128)(2,1)}, f32[1152,128]{1,0:T(8,128)}, bf16[128,1024]{1,0:T(8,128)(2,1)}, bf16[128,1024]{1,0:T(8,128)(2,1)}) custom-call(bf16[1152,1024]{1,0:T(8,128)(2,1)} %get-tuple-element.42.x_ref, bf16[1152,1024]{1,0:T(8,128)(2,1)} %get-tuple-element.43.dy_ref, bf16[1024,128]{1,0:T(8,128)(2,1)} %copy-done.7, ...), custom_call_target="tpu_custom_call" | custom-call | tf_op jit(solution)/shard_map/far_units/pallas_call | solution.py:292
  169.1 6.3 %collective-permute-done.5.a_i = bf16[128,1024]{1,0:T(8,128)(2,1)S(1)} collective-permute-done((bf16[128,1024]{1,0:T(8,128)(2,1)}, bf16[128,1024]{1,0:T(8,128)(2,1)S(1)}, u32[]{:S(2)}, u32[]{:S(2)}) %collective-permute-start.5) | collective-permute-done | bytes 262176 | tf_op jit(solution)/shard_map/ppermute | solution.py:249
  175.4 0.0 collective-permute-done.6.a_o
  175.4 5.3 %input_gradient.1 = (f32[576,1024]{1,0:T(8,128)}, f32[576,128]{1,0:T(8,128)}, bf16[576,1152]{1,0:T(8,128)(2,1)}) custom-call(bf16[1152,128]{1,0:T(8,128)(2,1)} %get-tuple-element.41.dpre0_ref, bf16[1152,256]{1,0:T(8,128)(2,1)} %get-tuple-element.47.dpre1_ref, bf16[1152,128]{1,0:T(8,128)(2,1)} %get-tuple-element.49.dpre2_ref, bf16[1024,128]{1,0:T(8,128)(2,1)} %bitcast.17, ...), custom_call_target="tpu_custom_call" | custom-call | tf_op jit(solution)/shard_map/input_gradient/pallas_call | solution.py:300
  180.7 1.9 collective-permute-start.7
  182.6 0.0 copy-done.17
  182.6 2.6 collective-permute-start.8
  185.2 0.0 copy-done.16
  185.3 7.1 %collective-permute-start.9 = (bf16[128,1024]{1,0:T(8,128)(2,1)S(1)}, bf16[128,1024]{1,0:T(8,128)(2,1)S(1)}, u32[]{:S(2)}, u32[]{:S(2)}) collective-permute-start(bf16[128,1024]{1,0:T(8,128)(2,1)S(1)} %copy-done.16), channel_id=1, source_target_pairs={{0,384},{64,448},{128,0},{192,64},{256,128},{320,192},{384,256},{4... | collective-permute-start | bytes 786440 | tf_op jit(solution)/shard_map/ppermute | solution.py:249
  192.4 5.8 %collective-permute-done.8.far_i = bf16[128,1024]{1,0:T(8,128)(2,1)S(1)} collective-permute-done((bf16[128,1024]{1,0:T(8,128)(2,1)S(1)}, bf16[128,1024]{1,0:T(8,128)(2,1)S(1)}, u32[]{:S(2)}, u32[]{:S(2)}) %collective-permute-start.8) | collective-permute-done | bytes 262176 | tf_op jit(solution)/shard_map/ppermute | solution.py:249
  198.1 10.5 %collective-permute-done.9.far_o = bf16[128,1024]{1,0:T(8,128)(2,1)S(1)} collective-permute-done((bf16[128,1024]{1,0:T(8,128)(2,1)S(1)}, bf16[128,1024]{1,0:T(8,128)(2,1)S(1)}, u32[]{:S(2)}, u32[]{:S(2)}) %collective-permute-start.9) | collective-permute-done | bytes 262176 | tf_op jit(solution)/shard_map/ppermute | solution.py:249
  208.6 0.0 copy-done.9
  208.6 0.0 copy-done.10
  208.6 0.0 copy-done.12
  208.6 0.7 copy-done.13
  209.3 2.9 add_far.1
  212.2 0.0 collective-permute-done.7.refs_2_
  212.2 1.1 copy-done.6
  213.3 4.7 %pack.1 = bf16[5120,128]{1,0:T(8,128)(2,1)} custom-call(f32[576,1024]{1,0:T(8,128)} %get-tuple-element.54.refs_0_, f32[576,128]{1,0:T(8,128)} %get-tuple-element.55.refs_1_, bf16[576,1152]{1,0:T(8,128)(2,1)} %copy-done.6), custom_call_target="tpu_custom_call" | custom-call | tf_op jit(solution)/shard_map/pack/pallas_call | solution.py:306
  218.0 12.8 %all-to-all-start.1 = ((bf16[64,80,128]{2,1,0:T(8,128)(2,1)}), bf16[64,80,128]{2,1,0:T(8,128)(2,1)S(1)}, u32[]{:S(2)}, u32[]{:S(2)}) async-start(bf16[64,80,128]{2,1,0:T(8,128)(2,1)} %bitcast.14), calls=%async_computation.1 | async-start | bytes 2621440 | tf_op jit(solution)/shard_map/all_to_all | solution.py:320
  230.9 0.0 copy-done.19
  230.9 8.3 %collective-permute-start.10 = (bf16[128,1024]{1,0:T(8,128)(2,1)S(1)}, bf16[128,1024]{1,0:T(8,128)(2,1)S(1)}, u32[]{:S(2)}, u32[]{:S(2)}) collective-permute-start(bf16[128,1024]{1,0:T(8,128)(2,1)S(1)} %copy-done.19), channel_id=1, source_target_pairs={{0,128},{64,192},{128,256},{192,320},{256,384},{320,448},{384,0},{... | collective-permute-start | bytes 786440 | tf_op jit(solution)/shard_map/ppermute | solution.py:249
  239.2 0.0 copy-done.18
  239.2 1.9 collective-permute-start.11
  241.2 46.5 %collective-permute-done.10.c_i = bf16[128,1024]{1,0:T(8,128)(2,1)S(1)} collective-permute-done((bf16[128,1024]{1,0:T(8,128)(2,1)S(1)}, bf16[128,1024]{1,0:T(8,128)(2,1)S(1)}, u32[]{:S(2)}, u32[]{:S(2)}) %collective-permute-start.10) | collective-permute-done | bytes 262176 | tf_op jit(solution)/shard_map/ppermute | solution.py:249
  287.7 0.0 collective-permute-done.11.c_o
  287.7 0.7 copy-done.14
  288.4 0.1 copy-done.15
  288.5 2.5 finish.1
  291.0 0.0 all-to-all-done.1
  291.0 1.1 copy-done.1
  292.1 3.8 %combine.1 = (bf16[192,1024]{1,0:T(8,128)(2,1)}, bf16[2,192]{1,0:T(2,128)(2,1)}) custom-call(s32[2,192]{1,0:T(2,128)} %bitcast.22, bf16[2,192]{1,0:T(2,128)(2,1)} %bitcast.24, bf16[5120,128]{1,0:T(8,128)(2,1)} %bitcast.15), custom_call_target="tpu_custom_call" | custom-call | tf_op jit(solution)/shard_map/combine/pallas_call | solution.py:326
  (16 shorter events, 0.1 us)
Async XLA Ops:
  5.3 12.0 %copy-start.4 = (bf16[1,1024,128]{2,1,0:T(8,128)(2,1)S(1)}, bf16[1,1024,128]{2,1,0:T(8,128)(2,1)}, u32[]{:S(2)}) copy-start(bf16[1,1024,128]{2,1,0:T(8,128)(2,1)} %param.10) | copy-start | bytes 786436
  5.3 12.0 %copy-start.8 = (bf16[1,1024,128]{2,1,0:T(8,128)(2,1)S(1)}, bf16[1,1024,128]{2,1,0:T(8,128)(2,1)}, u32[]{:S(2)}) copy-start(bf16[1,1024,128]{2,1,0:T(8,128)(2,1)} %param.11) | copy-start | bytes 786436
  5.3 116.0 %all-to-all-start = ((bf16[64,144,128]{2,1,0:T(8,128)(2,1)}), bf16[64,144,128]{2,1,0:T(8,128)(2,1)S(1)}, u32[]{:S(2)}, u32[]{:S(2)}) async-start(bf16[64,144,128]{2,1,0:T(8,128)(2,1)} %bitcast.13), calls=%async_computation | async-start | bytes 4718592 | tf_op jit(solution)/shard_map/all_to_all | solution.py:266
  17.3 103.9 %collective-permute-start = (bf16[2048,128]{1,0:T(8,128)(2,1)S(1)}, bf16[2048,128]{1,0:T(8,128)(2,1)S(1)}, u32[]{:S(2)}, u32[]{:S(2)}) collective-permute-start(bf16[2048,128]{1,0:T(8,128)(2,1)S(1)} %pad_maximum_fusion), channel_id=1, source_target_pairs={{0,128},{64,192},{128,256},{192,320},{256,384},{320,448},{384,0},{... | collective-permute-start | bytes 1572872 | tf_op jit(solution)/shard_map/ppermute | solution.py:249
  26.4 94.8 %collective-permute-start.1 = (bf16[2048,128]{1,0:T(8,128)(2,1)S(1)}, bf16[2048,128]{1,0:T(8,128)(2,1)S(1)}, u32[]{:S(2)}, u32[]{:S(2)}) collective-permute-start(bf16[2048,128]{1,0:T(8,128)(2,1)S(1)} %pad_maximum_fusion), channel_id=1, source_target_pairs={{0,384},{64,448},{128,0},{192,64},{256,128},{320,192},{384,256},{4... | collective-permute-start | bytes 1572872 | tf_op jit(solution)/shard_map/ppermute | solution.py:249
  121.3 24.2 %copy-start.2 = (bf16[2048,128]{1,0:T(8,128)(2,1)}, bf16[2048,128]{1,0:T(8,128)(2,1)S(1)}, u32[]{:S(2)}) copy-start(bf16[2048,128]{1,0:T(8,128)(2,1)S(1)} %collective-permute-done.wm_ref) | copy-start | bytes 1572868
  121.3 24.2 %copy-start.3 = (bf16[2048,128]{1,0:T(8,128)(2,1)}, bf16[2048,128]{1,0:T(8,128)(2,1)S(1)}, u32[]{:S(2)}) copy-start(bf16[2048,128]{1,0:T(8,128)(2,1)S(1)} %collective-permute-done.1.wp_ref) | copy-start | bytes 1572868
  121.3 12.0 %copy-start = (bf16[64,144,128]{2,1,0:T(8,128)(2,1)}, bf16[64,144,128]{2,1,0:T(8,128)(2,1)S(1)}, u32[]{:S(2)}) copy-start(bf16[64,144,128]{2,1,0:T(8,128)(2,1)S(1)} %all-to-all-done) | copy-start | bytes 7077892
  121.3 11.9 %collective-permute-start.2 = (bf16[9216,128]{1,0:T(8,128)(2,1)S(1)}, bf16[9216,128]{1,0:T(8,128)(2,1)S(1)}, u32[]{:S(2)}, u32[]{:S(2)}) collective-permute-start(bf16[9216,128]{1,0:T(8,128)(2,1)S(1)} %bitcast.11), channel_id=1, source_target_pairs={{0,64},{64,0},{128,192},{192,128},{256,320},{320,256},{384,448},{4... | collective-permute-start | bytes 7077896 | tf_op jit(solution)/shard_map/ppermute | solution.py:249
  123.2 39.3 %collective-permute-start.3 = (bf16[1024,128]{1,0:T(8,128)(2,1)S(1)}, bf16[1024,128]{1,0:T(8,128)(2,1)S(1)}, u32[]{:S(2)}, u32[]{:S(2)}) collective-permute-start(bf16[1024,128]{1,0:T(8,128)(2,1)S(1)} %slice.8), channel_id=1, source_target_pairs={{0,128},{64,192},{128,256},{192,320},{256,384},{320,448},{384,0},{... | collective-permute-start | bytes 786440 | tf_op jit(solution)/shard_map/ppermute | solution.py:249
  125.2 37.4 %collective-permute-start.4 = (bf16[1024,128]{1,0:T(8,128)(2,1)S(1)}, bf16[1024,128]{1,0:T(8,128)(2,1)S(1)}, u32[]{:S(2)}, u32[]{:S(2)}) collective-permute-start(bf16[1024,128]{1,0:T(8,128)(2,1)S(1)} %slice.9), channel_id=1, source_target_pairs={{0,384},{64,448},{128,0},{192,64},{256,128},{320,192},{384,256},{4... | collective-permute-start | bytes 786440 | tf_op jit(solution)/shard_map/ppermute | solution.py:249
  133.2 1.5 copy-start.5
  152.6 22.8 %collective-permute-start.5 = (bf16[128,1024]{1,0:T(8,128)(2,1)}, bf16[128,1024]{1,0:T(8,128)(2,1)S(1)}, u32[]{:S(2)}, u32[]{:S(2)}) collective-permute-start(bf16[128,1024]{1,0:T(8,128)(2,1)} %get-tuple-element.51), channel_id=1, source_target_pairs={{0,384},{64,448},{128,0},{192,64},{256,128},{320,192},{384,256},{4... | collective-permute-start | bytes 786440 | tf_op jit(solution)/shard_map/ppermute | solution.py:249
  158.0 17.4 %collective-permute-start.6 = (bf16[128,1024]{1,0:T(8,128)(2,1)}, bf16[128,1024]{1,0:T(8,128)(2,1)S(1)}, u32[]{:S(2)}, u32[]{:S(2)}) collective-permute-start(bf16[128,1024]{1,0:T(8,128)(2,1)} %get-tuple-element.52), channel_id=1, source_target_pairs={{0,128},{64,192},{128,256},{192,320},{256,384},{320,448},{384,0},{... | collective-permute-start | bytes 786440 | tf_op jit(solution)/shard_map/ppermute | solution.py:249
  162.6 0.7 copy-start.7
  162.6 0.8 copy-start.11
  169.1 13.5 %copy-start.17 = (bf16[128,1024]{1,0:T(8,128)(2,1)S(1)}, bf16[128,1024]{1,0:T(8,128)(2,1)}, u32[]{:S(2)}) copy-start(bf16[128,1024]{1,0:T(8,128)(2,1)} %get-tuple-element.58) | copy-start | bytes 786436
  169.1 16.2 %copy-start.16 = (bf16[128,1024]{1,0:T(8,128)(2,1)S(1)}, bf16[128,1024]{1,0:T(8,128)(2,1)}, u32[]{:S(2)}) copy-start(bf16[128,1024]{1,0:T(8,128)(2,1)} %get-tuple-element.60) | copy-start | bytes 786436
  175.4 33.2 %copy-start.9 = (bf16[128,1024]{1,0:T(8,128)(2,1)}, bf16[128,1024]{1,0:T(8,128)(2,1)S(1)}, u32[]{:S(2)}) copy-start(bf16[128,1024]{1,0:T(8,128)(2,1)S(1)} %collective-permute-done.5.a_i) | copy-start | bytes 786436
  175.4 33.2 %copy-start.10 = (bf16[128,1024]{1,0:T(8,128)(2,1)}, bf16[128,1024]{1,0:T(8,128)(2,1)S(1)}, u32[]{:S(2)}) copy-start(bf16[128,1024]{1,0:T(8,128)(2,1)S(1)} %collective-permute-done.6.a_o) | copy-start | bytes 786436
  180.7 31.6 %collective-permute-start.7 = (bf16[576,1152]{1,0:T(8,128)(2,1)}, bf16[576,1152]{1,0:T(8,128)(2,1)S(1)}, u32[]{:S(2)}, u32[]{:S(2)}) collective-permute-start(bf16[576,1152]{1,0:T(8,128)(2,1)} %get-tuple-element.56), channel_id=1, source_target_pairs={{0,64},{64,0},{128,192},{192,128},{256,320},{320,256},{384,448},{4... | collective-permute-start | bytes 3981320 | tf_op jit(solution)/shard_map/ppermute | solution.py:249
  182.6 15.5 %collective-permute-start.8 = (bf16[128,1024]{1,0:T(8,128)(2,1)S(1)}, bf16[128,1024]{1,0:T(8,128)(2,1)S(1)}, u32[]{:S(2)}, u32[]{:S(2)}) collective-permute-start(bf16[128,1024]{1,0:T(8,128)(2,1)S(1)} %copy-done.17), channel_id=1, source_target_pairs={{0,128},{64,192},{128,256},{192,320},{256,384},{320,448},{384,0},{... | collective-permute-start | bytes 786440 | tf_op jit(solution)/shard_map/ppermute | solution.py:249
  185.3 23.4 %collective-permute-start.9 = (bf16[128,1024]{1,0:T(8,128)(2,1)S(1)}, bf16[128,1024]{1,0:T(8,128)(2,1)S(1)}, u32[]{:S(2)}, u32[]{:S(2)}) collective-permute-start(bf16[128,1024]{1,0:T(8,128)(2,1)S(1)} %copy-done.16), channel_id=1, source_target_pairs={{0,384},{64,448},{128,0},{192,64},{256,128},{320,192},{384,256},{4... | collective-permute-start | bytes 786440 | tf_op jit(solution)/shard_map/ppermute | solution.py:249
  198.1 10.5 %copy-start.12 = (bf16[128,1024]{1,0:T(8,128)(2,1)}, bf16[128,1024]{1,0:T(8,128)(2,1)S(1)}, u32[]{:S(2)}) copy-start(bf16[128,1024]{1,0:T(8,128)(2,1)S(1)} %collective-permute-done.8.far_i) | copy-start | bytes 786436
  208.6 0.7 copy-start.13
  212.2 1.1 copy-start.6
  218.0 12.9 %copy-start.19 = (bf16[128,1024]{1,0:T(8,128)(2,1)S(1)}, bf16[128,1024]{1,0:T(8,128)(2,1)}, u32[]{:S(2)}) copy-start(bf16[128,1024]{1,0:T(8,128)(2,1)} %get-tuple-element.71) | copy-start | bytes 786436
  218.0 21.2 %copy-start.18 = (bf16[128,1024]{1,0:T(8,128)(2,1)S(1)}, bf16[128,1024]{1,0:T(8,128)(2,1)}, u32[]{:S(2)}) copy-start(bf16[128,1024]{1,0:T(8,128)(2,1)} %get-tuple-element.73) | copy-start | bytes 786436
  218.0 72.9 %all-to-all-start.1 = ((bf16[64,80,128]{2,1,0:T(8,128)(2,1)}), bf16[64,80,128]{2,1,0:T(8,128)(2,1)S(1)}, u32[]{:S(2)}, u32[]{:S(2)}) async-start(bf16[64,80,128]{2,1,0:T(8,128)(2,1)} %bitcast.14), calls=%async_computation.1 | async-start | bytes 2621440 | tf_op jit(solution)/shard_map/all_to_all | solution.py:320
  230.9 56.8 %collective-permute-start.10 = (bf16[128,1024]{1,0:T(8,128)(2,1)S(1)}, bf16[128,1024]{1,0:T(8,128)(2,1)S(1)}, u32[]{:S(2)}, u32[]{:S(2)}) collective-permute-start(bf16[128,1024]{1,0:T(8,128)(2,1)S(1)} %copy-done.19), channel_id=1, source_target_pairs={{0,128},{64,192},{128,256},{192,320},{256,384},{320,448},{384,0},{... | collective-permute-start | bytes 786440 | tf_op jit(solution)/shard_map/ppermute | solution.py:249
  239.2 48.5 %collective-permute-start.11 = (bf16[128,1024]{1,0:T(8,128)(2,1)S(1)}, bf16[128,1024]{1,0:T(8,128)(2,1)S(1)}, u32[]{:S(2)}, u32[]{:S(2)}) collective-permute-start(bf16[128,1024]{1,0:T(8,128)(2,1)S(1)} %copy-done.18), channel_id=1, source_target_pairs={{0,384},{64,448},{128,0},{192,64},{256,128},{320,192},{384,256},{4... | collective-permute-start | bytes 786440 | tf_op jit(solution)/shard_map/ppermute | solution.py:249
  287.7 0.7 copy-start.14
  287.7 0.8 copy-start.15
  291.0 1.1 copy-start.1

commit v3 on v1

--- a/solution.py
+++ b/solution.py
@@ -74,25 +74,7 @@
     return value, slope
 
 
-def units(x, dy, w_first, w_second):
-    pre = jnp.dot(x, w_first, preferred_element_type=f32)
-    dy_proj = jnp.dot(dy, w_second, preferred_element_type=f32)
-    value, slope = gelu_parts(pre)
-    activated = value.astype(bf16)
-    d_pre = (dy_proj * slope).astype(bf16)
-    gate = activated.astype(f32) * dy_proj
-    grad_first = lax.dot_general(
-        d_pre, x, (((0,), (0,)), ((), ())), preferred_element_type=f32
-    )
-    grad_second = lax.dot_general(
-        activated, dy, (((0,), (0,)), ((), ())), preferred_element_type=f32
-    )
-    return d_pre, gate, grad_first, grad_second
-
-
-def own_body(
-    mine_ref, other_ref, wi_ref, wo_ref, x_ref, dy_ref, dpre_ref, gate_ref, gi_ref, go_ref, wide_ref
-):
+def unpack_body(mine_ref, other_ref, x_ref, dy_ref, wide_ref):
     slots = x_ref.shape[0] // 2
     width = x_ref.shape[1] // LANES
     for half, ref in enumerate((mine_ref, other_ref)):
@@ -102,44 +84,39 @@
             cols = slice(j * LANES, (j + 1) * LANES)
             x_ref[rows, cols] = wide_ref[pl.ds(j, slots, stride=2 * width), :].astype(bf16)
             dy_ref[rows, cols] = wide_ref[pl.ds(width + j, slots, stride=2 * width), :].astype(bf16)
-    d_pre, gate, grad_first, grad_second = units(x_ref[...], dy_ref[...], wi_ref[...], wo_ref[...])
-    dpre_ref[...] = d_pre
-    gate_ref[...] = gate
-    gi_ref[...] = grad_first
-    go_ref[...] = grad_second
-
-
-def near_body(
-    x_ref, dy_ref, wim_ref, wom_ref, wip_ref, wop_ref, gate_in_ref,
-    dpre_ref, gate_ref, gim_ref, gom_ref, gip_ref, gop_ref,
-):
-    w_first = jnp.concatenate([wim_ref[...], wip_ref[...]], axis=1)
-    w_second = jnp.concatenate([wom_ref[...], wop_ref[...]], axis=1)
-    d_pre, gate, grad_first, grad_second = units(x_ref[...], dy_ref[...], w_first, w_second)
-    dpre_ref[...] = d_pre
-    gate_ref[...] = gate_in_ref[...] + gate[:, :LANES] + gate[:, LANES:]
-    gim_ref[...] = grad_first[:LANES].astype(bf16)
-    gip_ref[...] = grad_first[LANES:].astype(bf16)
-    gom_ref[...] = grad_second[:LANES].astype(bf16)
-    gop_ref[...] = grad_second[LANES:].astype(bf16)
-
-
-def far_body(x_ref, dy_ref, wi_ref, wo_ref, gate_in_ref, dpre_ref, gate_ref, gi_ref, go_ref):
-    d_pre, gate, grad_first, grad_second = units(x_ref[...], dy_ref[...], wi_ref[...], wo_ref[...])
-    dpre_ref[...] = d_pre
-    gate_ref[...] = gate_in_ref[...] + gate
-    gi_ref[...] = grad_first.astype(bf16)
-    go_ref[...] = grad_second.astype(bf16)
-
-
-def dx_body(
-    dpre0_ref, dpre1_ref, dpre2_ref, w0_ref, wm_ref, wp_ref, wf_ref, gate_ref,
-    keep_ref, keep_gate_ref, give_ref,
-):
+
+
+def units_body(x_ref, dy_ref, w_ref, dpre_ref, gate_ref, grad_ref):
+    blocks = w_ref.shape[0]
+    width = x_ref.shape[1]
+    x = x_ref[...]
+    dy = dy_ref[...]
+    gates = []
+    for pair in range(0, blocks, 2):
+        w_first = jnp.concatenate([w_ref[pair, :width], w_ref[pair + 1, :width]], axis=1)
+        w_second = jnp.concatenate([w_ref[pair, width:], w_ref[pair + 1, width:]], axis=1)
+        pre = jnp.dot(x, w_first, preferred_element_type=f32)
+        dy_proj = jnp.dot(dy, w_second, preferred_element_type=f32)
+        value, slope = gelu_parts(pre)
+        activated = value.astype(bf16)
+        d_pre = (dy_proj * slope).astype(bf16)
+        gate = activated.astype(f32) * dy_proj
+        gates += [gate[:, :LANES], gate[:, LANES:]]
+        dpre_ref[:, pair * LANES : (pair + 2) * LANES] = d_pre
+        for row, left, right in ((0, d_pre, x), (LANES, activated, dy)):
+            grad = lax.dot_general(
+                left, right, (((0,), (0,)), ((), ())), preferred_element_type=f32
+            ).astype(bf16)
+            grad_ref[pair, row : row + LANES] = grad[:LANES]
+            grad_ref[pair + 1, row : row + LANES] = grad[LANES:]
+    gate_ref[...] = sum(gates[1:], gates[0])
+
+
+def dx_body(dpre_ref, w_ref, gate_ref, keep_ref, keep_gate_ref, give_ref):
     slots = keep_ref.shape[0]
     width = keep_ref.shape[1]
-    d_pre = jnp.concatenate([dpre0_ref[...], dpre1_ref[...], dpre2_ref[...]], axis=1)
-    weights = jnp.concatenate([w0_ref[...], wm_ref[...], wp_ref[...], wf_ref[...]], axis=1)
+    d_pre = dpre_ref[...]
+    weights = jnp.concatenate([w_ref[i, :width] for i in range(w_ref.shape[0])], axis=1)
     dx = lax.dot_general(d_pre, weights, (((1,), (1,)), ((), ())), preferred_element_type=f32)
     gate = jnp.sum(gate_ref[...], axis=1, keepdims=True)
     keep_ref[...] = dx[:slots]
@@ -219,14 +196,10 @@
     dgate_ref[...] = (sums / gates).astype(bf16)
 
 
-def add_body(a_ref, b_ref, c_ref, d_ref, first_ref, second_ref):
-    first_ref[...] = (a_ref[...].astype(f32) + b_ref[...].astype(f32)).astype(bf16)
-    second_ref[...] = (c_ref[...].astype(f32) + d_ref[...].astype(f32)).astype(bf16)
-
-
-def finish_body(own_i, a_i, c_i, own_o, a_o, c_o, gi_ref, go_ref):
-    gi_ref[...] = (own_i[...] + a_i[...].astype(f32) + c_i[...].astype(f32)).T
-    go_ref[...] = (own_o[...] + a_o[...].astype(f32) + c_o[...].astype(f32)).T
+def finish_body(total_ref, gi_ref, go_ref):
+    total = total_ref[...].astype(f32)
+    gi_ref[...] = total[:LANES].T
+    go_ref[...] = total[LANES:].T
 
 
 def shards(tokens, out_grad, gates, expert_ids, w_in, w_out):
@@ -237,8 +210,7 @@
     slots = experts * capacity
     tiles = width // LANES
     shard = w_in.shape[2]
-    up = [(i, (i + 2) % replicas) for i in range(replicas)]
-    down = [(i, (i - 2) % replicas) for i in range(replicas)]
+    same_core = [[i for i in range(replicas) if i % 2 == c] for c in range(2)]
     swap = [(i, i ^ 1) for i in range(replicas)]
     sds = jax.ShapeDtypeStruct
 
@@ -250,12 +222,9 @@
     ids = expert_ids.T
     gates_row = gates.T
 
-    wi_m = send(wi, up)
-    wo_p = send(wo, down)
-    wi_p = send(wi, down)
-    wo_m = send(wo, up)
-    wi_f = send(wi_m, up)
-    wo_f = send(wo_p, down)
+    weights = lax.all_gather(
+        jnp.concatenate([wi, wo], axis=0), "dp", axis=0, tiled=False, axis_index_groups=same_core
+    )
 
     payload = call(
         lambda *refs: dispatch_body(experts, capacity, *refs),
@@ -268,36 +237,29 @@
         "expert", split_axis=0, concat_axis=0, tiled=True,
     ).reshape(slots * 2 * tiles, LANES)
     other = send(mine, swap)
-
     rows = sds((2 * slots, width), bf16)
-    gate_shape = sds((2 * slots, LANES), f32)
-    grad = sds((shard, width), bf16)
-    x, dy, dpre0, gate0, own_i, own_o = call(
-        own_body,
-        (rows, rows, sds((2 * slots, shard), bf16), gate_shape,
-         sds((shard, width), f32), sds((shard, width), f32)),
-        "own_units",
-        [pltpu.VMEM((slots * 2 * tiles, LANES), f32)],
-    )(mine, other, wi, wo)
-    dpre1, gate1, gi_m, go_m, gi_p, go_p = call(
-        near_body,
-        (sds((2 * slots, 2 * shard), bf16), gate_shape, grad, grad, grad, grad),
-        "near_units",
-    )(x, dy, wi_m, wo_m, wi_p, wo_p, gate0)
-    a_o = send(go_p, up)
-    a_i = send(gi_m, down)
-    dpre2, gate2, gi_f, go_f = call(
-        far_body,
-        (sds((2 * slots, shard), bf16), gate_shape, grad, grad),
-        "far_units",
-    )(x, dy, wi_f, wo_f, gate1)
-    b_i = send(gi_f, up)
-    b_o = send(go_f, down)
+    x, dy = call(
+        unpack_body, (rows, rows), "unpack", [pltpu.VMEM((slots * 2 * tiles, LANES), f32)]
+    )(mine, other)
+    x, dy, weights = lax.optimization_barrier((x, dy, weights))
+    blocks = replicas // 2
+    d_pre, gate, grads = call(
+        units_body,
+        (
+            sds((2 * slots, blocks * shard), bf16),
+            sds((2 * slots, LANES), f32),
+            sds((blocks, 2 * shard, width), bf16),
+        ),
+        "units",
+    )(x, dy, weights)
+    total = lax.psum_scatter(
+        grads, "dp", scatter_dimension=0, tiled=False, axis_index_groups=same_core
+    )
     keep, keep_gate, give = call(
         dx_body,
         (sds((slots, width), f32), sds((slots, LANES), f32), sds((slots, width + LANES), bf16)),
         "input_gradient",
-    )(dpre0, dpre1, dpre2, wi, wi_m, wi_p, wi_f, gate2)
+    )(d_pre, weights, gate)
     took = send(give, swap)
     back = call(
         lambda *refs: pack_body(experts, capacity, *refs),
@@ -312,9 +274,6 @@
         back.reshape(experts, (capacity + 1) * tiles, LANES),
         "expert", split_axis=0, concat_axis=0, tiled=True,
     ).reshape(experts * (capacity + 1) * tiles, LANES)
-    sum_i, sum_o = call(add_body, (grad, grad), "add_far")(gi_p, b_i, go_m, b_o)
-    c_i = send(sum_i, up)
-    c_o = send(sum_o, down)
     d_tokens, gate_grad = call(
         lambda *refs: combine_body(experts, capacity, *refs),
         (sds((tok_rows, width), bf16), sds((2, tok_rows), bf16)),
@@ -324,10 +283,9 @@
             pltpu.VMEM((tiles, slots, LANES), f32),
         ],
     )(ids, gates_row, back)
-    total = sds((width, shard), f32)
-    grad_in, grad_out = call(finish_body, (total, total), "finish")(
-        own_i, a_i, c_i, own_o, a_o, c_o
-    )
+    d_tokens, gate_grad, total = lax.optimization_barrier((d_tokens, gate_grad, total))
+    own = sds((width, shard), f32)
+    grad_in, grad_out = call(finish_body, (own, own), "finish")(total)
     return d_tokens, gate_grad.T, grad_in[None], grad_out[None]
 
 

time: 311 us -> 311 us (level)
  the two profiles are of different devices: /device:TPU:39 before, /device:TPU:83 now
where the time goes in v3:
time: 311 us
  waiting for transfers between devices  224 us (72%)
  Pallas kernels  41.1 us (13%)
  starting transfers between devices  26.7 us (9%)
  between operations  14.1 us (5%)
  local copies, waits for them, and re-layouts  3.64 us (1%)
    all_to_all x1, waiting for transfers between devices, shards(): lax.all_to_all(payload.reshape(experts, capacity * 2 * tiles, LANES), 'ex...  118 us
    all_to_all x1, waiting for transfers between devices, shards(): lax.all_to_all(back.reshape(experts, (capacity + 1) * tiles, LANES), 'exp...  74.2 us
    reduce_scatter x1, waiting for transfers between devices, shards(): lax.psum_scatter(grads, 'dp', scatter_dimension=0, tiled=False, axis_inde...  24.7 us
    pallas_call x1, Pallas kernels, shards(): call(units_body, (sds((2 * slots, blocks * shard), bf16), sds((2 * slots,...  11 us
    all_to_all x1, starting transfers between devices, shards(): lax.all_to_all(payload.reshape(experts, capacity * 2 * tiles, LANES), 'ex...  10.6 us
    all_to_all x1, starting transfers between devices, shards(): lax.all_to_all(back.reshape(experts, (capacity + 1) * tiles, LANES), 'exp...  9.92 us
    pallas_call x1, Pallas kernels, shards(): call(unpack_body, (rows, rows), 'unpack', [pltpu.VMEM((slots * 2 * tiles,...  9.49 us
    ppermute x2, waiting for transfers between devices, send(): return lax.ppermute(value, 'dp', perm)  6.61 us
  transfers between devices with their start and end apart: 6, of which 5 were waited for; matrix products, arithmetic and copies ran while one was open for 0% of the time, Pallas kernels for 4%

profile of v3, /device:TPU:83, one launch (start us, length us, event | category | flops | bytes accessed | tf_op | source)
XLA Modules:
  0.0 310.7 jit_solution(17201419448989606267)
XLA Ops:
  7.2 4.7 %dispatch.1 = bf16[9216,128]{1,0:T(8,128)(2,1)} custom-call(s32[2,192]{1,0:T(2,128)} %bitcast.23, bf16[2,192]{1,0:T(2,128)(2,1)} %bitcast.25, bf16[192,1024]{1,0:T(8,128)(2,1)} %refs_2_.1, bf16[192,1024]{1,0:T(8,128)(2,1)} %refs_3_.1), custom_call_target="tpu_custom_call" | custom-call | tf_op jit(solution)/shard_map/dispatch/pallas_call | solution.py:229
  11.8 0.0 copy-start.4
  11.8 0.0 copy-start.5
  11.8 10.6 %all-to-all-start = ((bf16[64,144,128]{2,1,0:T(8,128)(2,1)}), bf16[64,144,128]{2,1,0:T(8,128)(2,1)S(1)}, u32[]{:S(2)}, u32[]{:S(2)}) async-start(bf16[64,144,128]{2,1,0:T(8,128)(2,1)} %bitcast.15), calls=%async_computation | async-start | bytes 4718592 | tf_op jit(solution)/shard_map/all_to_all | solution.py:235
  22.4 0.0 all-gather.3.cloned.1.call-start
  22.5 0.0 copy-done.4
  22.5 0.0 copy-done.5
  22.5 0.8 pad_maximum_fusion
  23.3 0.0 all-gather.3.cloned.1.call-update
  23.3 118.1 %all-to-all-done = bf16[64,144,128]{2,1,0:T(8,128)(2,1)S(1)} async-done(((bf16[64,144,128]{2,1,0:T(8,128)(2,1)}), bf16[64,144,128]{2,1,0:T(8,128)(2,1)S(1)}, u32[]{:S(2)}, u32[]{:S(2)}) %all-to-all-start) | async-done | bytes 2359328 | tf_op jit(solution)/shard_map/all_to_all | solution.py:235
  141.5 0.0 copy-start
  141.5 3.6 %collective-permute-start = (bf16[9216,128]{1,0:T(8,128)(2,1)S(1)}, bf16[9216,128]{1,0:T(8,128)(2,1)S(1)}, u32[]{:S(2)}, u32[]{:S(2)}) collective-permute-start(bf16[9216,128]{1,0:T(8,128)(2,1)S(1)} %bitcast.13), channel_id=1, source_target_pairs={{0,64},{64,0},{128,192},{192,128},{256,320},{320,256},{384,448},{4... | collective-permute-start | bytes 7077896 | tf_op jit(solution)/shard_map/ppermute | solution.py:218
  145.1 4.0 %collective-permute-done.other_ref = bf16[9216,128]{1,0:T(8,128)(2,1)S(1)} collective-permute-done((bf16[9216,128]{1,0:T(8,128)(2,1)S(1)}, bf16[9216,128]{1,0:T(8,128)(2,1)S(1)}, u32[]{:S(2)}, u32[]{:S(2)}) %collective-permute-start) | collective-permute-done | bytes 2359328 | tf_op jit(solution)/shard_map/ppermute | solution.py:218
  149.1 0.0 copy-done
  149.1 0.0 copy-start.2
  149.1 1.5 copy-done.2
  150.5 9.5 %unpack.1 = (bf16[1152,1024]{1,0:T(8,128)(2,1)}, bf16[1152,1024]{1,0:T(8,128)(2,1)}) custom-call(bf16[9216,128]{1,0:T(8,128)(2,1)} %bitcast.14, bf16[9216,128]{1,0:T(8,128)(2,1)} %copy-done.2), custom_call_target="tpu_custom_call" | custom-call | tf_op jit(solution)/shard_map/unpack/pallas_call | solution.py:241
  160.0 0.0 all-gather.3.cloned.1.call-done
  160.0 11.0 %units.1 = (bf16[1152,512]{1,0:T(8,128)(2,1)}, f32[1152,128]{1,0:T(8,128)}, bf16[4,256,1024]{2,1,0:T(8,128)(2,1)}) custom-call(bf16[1152,1024]{1,0:T(8,128)(2,1)} %get-tuple-element.24.x_ref, bf16[1152,1024]{1,0:T(8,128)(2,1)} %get-tuple-element.25.dy_ref, bf16[4,2048,128]{2,1,0:T(8,128)(2,1)} %bitcast.16), custom_call_target="tpu_custom_call" | custom-call | tf_op jit(solution)/shard_map/units/pallas_call | solution.py:246
  171.1 5.2 %input_gradient.1 = (f32[576,1024]{1,0:T(8,128)}, f32[576,128]{1,0:T(8,128)}, bf16[576,1152]{1,0:T(8,128)(2,1)}) custom-call(bf16[1152,512]{1,0:T(8,128)(2,1)} %get-tuple-element.27.dpre_ref, bf16[4,2048,128]{2,1,0:T(8,128)(2,1)} %bitcast.17, f32[1152,128]{1,0:T(8,128)} %get-tuple-element.28.gate_ref), custom_call_target="tpu_custom_call" | custom-call | tf_op jit(solution)/shard_map/input_gradient/pallas_call | solution.py:258
  176.3 2.5 collective-permute-start.1
  178.8 2.7 collective-permute-done.1.refs_2_
  181.5 0.0 copy-start.3
  181.5 1.1 copy-done.3
  182.5 4.7 %pack.1 = bf16[5120,128]{1,0:T(8,128)(2,1)} custom-call(f32[576,1024]{1,0:T(8,128)} %get-tuple-element.29.refs_0_, f32[576,128]{1,0:T(8,128)} %get-tuple-element.30.refs_1_, bf16[576,1152]{1,0:T(8,128)(2,1)} %copy-done.3), custom_call_target="tpu_custom_call" | custom-call | tf_op jit(solution)/shard_map/pack/pallas_call | solution.py:264
  187.2 9.9 %all-to-all-start.1 = ((bf16[64,80,128]{2,1,0:T(8,128)(2,1)}), bf16[64,80,128]{2,1,0:T(8,128)(2,1)S(1)}, u32[]{:S(2)}, u32[]{:S(2)}) async-start(bf16[64,80,128]{2,1,0:T(8,128)(2,1)} %bitcast.18), calls=%async_computation.1 | async-start | bytes 2621440 | tf_op jit(solution)/shard_map/all_to_all | solution.py:273
  197.2 0.0 reduce-scatter.2.cloned.1.call-start
  197.2 0.7 reduce-scatter.2.cloned.1.call-update
  197.9 74.2 %all-to-all-done.1 = bf16[64,80,128]{2,1,0:T(8,128)(2,1)S(1)} async-done(((bf16[64,80,128]{2,1,0:T(8,128)(2,1)}), bf16[64,80,128]{2,1,0:T(8,128)(2,1)S(1)}, u32[]{:S(2)}, u32[]{:S(2)}) %all-to-all-start.1) | async-done | bytes 1310752 | tf_op jit(solution)/shard_map/all_to_all | solution.py:273
  272.1 0.0 copy-start.1
  272.2 1.1 copy-done.1
  273.2 3.8 %combine.1 = (bf16[192,1024]{1,0:T(8,128)(2,1)}, bf16[2,192]{1,0:T(2,128)(2,1)}) custom-call(s32[2,192]{1,0:T(2,128)} %bitcast.24, bf16[2,192]{1,0:T(2,128)(2,1)} %bitcast.26, bf16[5120,128]{1,0:T(8,128)(2,1)} %bitcast.19), custom_call_target="tpu_custom_call" | custom-call | tf_op jit(solution)/shard_map/combine/pallas_call | solution.py:277
  277.0 24.7 %reduce-scatter.2.cloned.1.call-done = bf16[1,256,1024]{2,1,0:T(8,128)(2,1)} async-done(((bf16[4,256,1024]{2,1,0:T(8,128)(2,1)}), bf16[1,256,1024]{2,1,0:T(8,128)(2,1)}) %reduce-scatter.2.cloned.1.call-update) | async-done | bytes 524304 | tf_op jit(solution)/shard_map/reduce_scatter | solution.py:255
  301.7 2.1 finish.1
Async XLA Ops:
  11.8 10.6 %copy-start.4 = (bf16[1,1024,128]{2,1,0:T(8,128)(2,1)S(1)}, bf16[1,1024,128]{2,1,0:T(8,128)(2,1)}, u32[]{:S(2)}) copy-start(bf16[1,1024,128]{2,1,0:T(8,128)(2,1)} %param.11) | copy-start | bytes 786436
  11.8 10.7 %copy-start.5 = (bf16[1,1024,128]{2,1,0:T(8,128)(2,1)S(1)}, bf16[1,1024,128]{2,1,0:T(8,128)(2,1)}, u32[]{:S(2)}) copy-start(bf16[1,1024,128]{2,1,0:T(8,128)(2,1)} %param.10) | copy-start | bytes 786436
  11.8 129.6 %all-to-all-start = ((bf16[64,144,128]{2,1,0:T(8,128)(2,1)}), bf16[64,144,128]{2,1,0:T(8,128)(2,1)S(1)}, u32[]{:S(2)}, u32[]{:S(2)}) async-start(bf16[64,144,128]{2,1,0:T(8,128)(2,1)} %bitcast.15), calls=%async_computation | async-start | bytes 4718592 | tf_op jit(solution)/shard_map/all_to_all | solution.py:235
  22.4 137.6 %all-gather.3.cloned.1.call-start = ((), (), s32[]{:S(2)}) async-start(), calls=%async_computation.4 | async-start | bytes 2621440 | tf_op jit(solution)/shard_map/all_gather | solution.py:225
  141.5 7.6 %copy-start = (bf16[64,144,128]{2,1,0:T(8,128)(2,1)}, bf16[64,144,128]{2,1,0:T(8,128)(2,1)S(1)}, u32[]{:S(2)}) copy-start(bf16[64,144,128]{2,1,0:T(8,128)(2,1)S(1)} %all-to-all-done) | copy-start | bytes 7077892
  141.5 7.6 %collective-permute-start = (bf16[9216,128]{1,0:T(8,128)(2,1)S(1)}, bf16[9216,128]{1,0:T(8,128)(2,1)S(1)}, u32[]{:S(2)}, u32[]{:S(2)}) collective-permute-start(bf16[9216,128]{1,0:T(8,128)(2,1)S(1)} %bitcast.13), channel_id=1, source_target_pairs={{0,64},{64,0},{128,192},{192,128},{256,320},{320,256},{384,448},{4... | collective-permute-start | bytes 7077896 | tf_op jit(solution)/shard_map/ppermute | solution.py:218
  149.1 1.5 copy-start.2
  176.3 5.2 %collective-permute-start.1 = (bf16[576,1152]{1,0:T(8,128)(2,1)}, bf16[576,1152]{1,0:T(8,128)(2,1)S(1)}, u32[]{:S(2)}, u32[]{:S(2)}) collective-permute-start(bf16[576,1152]{1,0:T(8,128)(2,1)} %get-tuple-element.31), channel_id=1, source_target_pairs={{0,64},{64,0},{128,192},{192,128},{256,320},{320,256},{384,448},{4... | collective-permute-start | bytes 3981320 | tf_op jit(solution)/shard_map/ppermute | solution.py:218
  181.5 1.1 copy-start.3
  187.2 84.9 %all-to-all-start.1 = ((bf16[64,80,128]{2,1,0:T(8,128)(2,1)}), bf16[64,80,128]{2,1,0:T(8,128)(2,1)S(1)}, u32[]{:S(2)}, u32[]{:S(2)}) async-start(bf16[64,80,128]{2,1,0:T(8,128)(2,1)} %bitcast.18), calls=%async_computation.1 | async-start | bytes 2621440 | tf_op jit(solution)/shard_map/all_to_all | solution.py:273
  197.2 104.5 %reduce-scatter.2.cloned.1.call-start = ((), (), s32[]{:S(2)}) async-start(), calls=%async_computation.3 | async-start | bytes 2621440 | tf_op jit(solution)/shard_map/reduce_scatter | solution.py:255
  272.1 1.1 copy-start.1
Sparse Core Ops, SparseCore 0:
  25.9 122.6 all-gather.2
  200.9 100.8 reduce-scatter.1

commit v4 on v3

--- a/solution.py
+++ b/solution.py
@@ -13,20 +13,31 @@
 VMEM_BYTES = 56 << 20
 
 
-def call(body, out_shape, name, scratch=()):
+def call(body, out_shape, name, scratch=(), scalars=0, arrays=0):
+    specs = {}
+    if scalars:
+        specs["in_specs"] = [pl.BlockSpec(memory_space=pltpu.SMEM)] * scalars + [
+            pl.BlockSpec(memory_space=pltpu.VMEM)
+        ] * arrays
     return pl.pallas_call(
         body,
         out_shape=out_shape,
+        **specs,
         scratch_shapes=scratch,
         name=name,
         compiler_params=pltpu.CompilerParams(vmem_limit_bytes=VMEM_BYTES),
     )
 
 
-def slot_targets(ids_ref, experts, capacity):
+def slot_targets(ids_ref, plane, experts, capacity):
     tokens = ids_ref.shape[1]
-    first = ids_ref[0:1, :]
-    second = ids_ref[1:2, :]
+
+    def near_order(expert):
+        up = (((expert >> 2) & 3) - plane) & 3
+        return up * 16 + (expert >> 4) * 4 + (expert & 3)
+
+    first = near_order(ids_ref[0:1, :])
+    second = near_order(ids_ref[1:2, :])
     expert = lax.broadcasted_iota(jnp.int32, (experts, tokens), 0)
     is_first = (expert == first).astype(f32)
     is_second = (expert == second).astype(f32)
@@ -42,17 +53,18 @@
     return first * capacity + slot_first, second * capacity + slot_second
 
 
-def one_hots(ids_ref, experts, capacity):
+def one_hots(ids_ref, plane, experts, capacity):
     tokens = ids_ref.shape[1]
-    first, second = slot_targets(ids_ref, experts, capacity)
+    first, second = slot_targets(ids_ref, plane, experts, capacity)
     slot = lax.broadcasted_iota(jnp.int32, (experts * capacity, tokens), 0)
     return (slot == first).astype(f32), (slot == second).astype(f32)
 
 
-def dispatch_body(experts, capacity, ids_ref, gates_ref, x_ref, dy_ref, out_ref, wide_ref):
+def dispatch_body(experts, capacity, plane_ref, ids_ref, gates_ref, x_ref, dy_ref, *refs):
+    out_refs, wide_ref = refs[:-1], refs[-1]
     width = x_ref.shape[1] // LANES
     slots = experts * capacity
-    pick_first, pick_second = one_hots(ids_ref, experts, capacity)
+    pick_first, pick_second = one_hots(ids_ref, plane_ref[0], experts, capacity)
     gates = gates_ref[...].astype(f32)
     pick = (pick_first + pick_second).astype(bf16)
     gated = (pick_first * gates[0:1, :] + pick_second * gates[1:2, :]).astype(bf16)
@@ -62,7 +74,9 @@
         cols = slice(j * LANES, (j + 1) * LANES)
         wide_ref[pl.ds(j, slots, stride=2 * width), :] = rows_x[:, cols]
         wide_ref[pl.ds(width + j, slots, stride=2 * width), :] = rows_dy[:, cols]
-    out_ref[...] = wide_ref[...].astype(bf16)
+    part = slots * 2 * width // len(out_refs)
+    for i, out_ref in enumerate(out_refs):
+        out_ref[...] = wide_ref[i * part : (i + 1) * part].astype(bf16)
 
 
 def gelu_parts(pre):
@@ -74,59 +88,76 @@
     return value, slope
 
 
-def unpack_body(mine_ref, other_ref, x_ref, dy_ref, wide_ref):
-    slots = x_ref.shape[0] // 2
+def unpack(got_ref, x_ref, dy_ref, wide_ref):
+    slots = x_ref.shape[0]
     width = x_ref.shape[1] // LANES
-    for half, ref in enumerate((mine_ref, other_ref)):
-        wide_ref[...] = ref[...].astype(f32)
-        rows = slice(half * slots, (half + 1) * slots)
-        for j in range(width):
-            cols = slice(j * LANES, (j + 1) * LANES)
-            x_ref[rows, cols] = wide_ref[pl.ds(j, slots, stride=2 * width), :].astype(bf16)
-            dy_ref[rows, cols] = wide_ref[pl.ds(width + j, slots, stride=2 * width), :].astype(bf16)
-
-
-def units_body(x_ref, dy_ref, w_ref, dpre_ref, gate_ref, grad_ref):
-    blocks = w_ref.shape[0]
-    width = x_ref.shape[1]
-    x = x_ref[...]
-    dy = dy_ref[...]
+    wide_ref[...] = got_ref[...].astype(f32)
+    for j in range(width):
+        cols = slice(j * LANES, (j + 1) * LANES)
+        x_ref[:, cols] = wide_ref[pl.ds(j, slots, stride=2 * width), :].astype(bf16)
+        dy_ref[:, cols] = wide_ref[pl.ds(width + j, slots, stride=2 * width), :].astype(bf16)
+
+
+def project(x, dy, w_ref, dpre_ref, act_ref, gate_ref):
+    width = x.shape[1]
     gates = []
-    for pair in range(0, blocks, 2):
+    for pair in range(0, w_ref.shape[0], 2):
+        cols = slice(pair * LANES, (pair + 2) * LANES)
         w_first = jnp.concatenate([w_ref[pair, :width], w_ref[pair + 1, :width]], axis=1)
         w_second = jnp.concatenate([w_ref[pair, width:], w_ref[pair + 1, width:]], axis=1)
         pre = jnp.dot(x, w_first, preferred_element_type=f32)
         dy_proj = jnp.dot(dy, w_second, preferred_element_type=f32)
         value, slope = gelu_parts(pre)
         activated = value.astype(bf16)
-        d_pre = (dy_proj * slope).astype(bf16)
         gate = activated.astype(f32) * dy_proj
         gates += [gate[:, :LANES], gate[:, LANES:]]
-        dpre_ref[:, pair * LANES : (pair + 2) * LANES] = d_pre
-        for row, left, right in ((0, d_pre, x), (LANES, activated, dy)):
-            grad = lax.dot_general(
-                left, right, (((0,), (0,)), ((), ())), preferred_element_type=f32
+        dpre_ref[:, cols] = (dy_proj * slope).astype(bf16)
+        act_ref[:, cols] = activated
+    gate_ref[...] = sum(gates[1:], gates[0])
+
+
+def mine_body(x_ref, dy_ref, w_ref, dpre_ref, act_ref, gate_ref):
+    project(x_ref[...], dy_ref[...], w_ref, dpre_ref, act_ref, gate_ref)
+
+
+def other_body(
+    got_ref, x_ref, dy_ref, dpre_in_ref, act_in_ref, w_ref,
+    dpre_ref, gate_ref, grad_ref, wide_ref, xo_ref, dyo_ref, act_ref,
+):
+    unpack(got_ref, xo_ref, dyo_ref, wide_ref)
+    project(xo_ref[...], dyo_ref[...], w_ref, dpre_ref, act_ref, gate_ref)
+    for row, sides in (
+        (0, ((dpre_in_ref, x_ref), (dpre_ref, xo_ref))),
+        (LANES, ((act_in_ref, dy_ref), (act_ref, dyo_ref))),
+    ):
+        for pair in range(0, w_ref.shape[0], 2):
+            cols = slice(pair * LANES, (pair + 2) * LANES)
+            grad = sum(
+                lax.dot_general(
+                    left[:, cols], right[...], (((0,), (0,)), ((), ())), preferred_element_type=f32
+                )
+                for left, right in sides
             ).astype(bf16)
             grad_ref[pair, row : row + LANES] = grad[:LANES]
             grad_ref[pair + 1, row : row + LANES] = grad[LANES:]
-    gate_ref[...] = sum(gates[1:], gates[0])
-
-
-def dx_body(dpre_ref, w_ref, gate_ref, keep_ref, keep_gate_ref, give_ref):
+
+
+def dx_body(dpre_m, dpre_o, w_ref, gate_m, gate_o, keep_ref, keep_gate_ref, give_ref):
     slots = keep_ref.shape[0]
     width = keep_ref.shape[1]
-    d_pre = dpre_ref[...]
     weights = jnp.concatenate([w_ref[i, :width] for i in range(w_ref.shape[0])], axis=1)
-    dx = lax.dot_general(d_pre, weights, (((1,), (1,)), ((), ())), preferred_element_type=f32)
-    gate = jnp.sum(gate_ref[...], axis=1, keepdims=True)
-    keep_ref[...] = dx[:slots]
-    keep_gate_ref[...] = jnp.broadcast_to(gate[:slots], keep_gate_ref.shape)
-    give_ref[:, :width] = dx[slots:].astype(bf16)
-    coarse = gate[slots:].astype(bf16)
-    fine = (gate[slots:] - coarse.astype(f32)).astype(bf16)
+    dims = (((1,), (1,)), ((), ()))
+    give = lax.dot_general(dpre_o[...], weights, dims, preferred_element_type=f32)
+    give_ref[:, :width] = give.astype(bf16)
+    keep_ref[...] = lax.dot_general(dpre_m[...], weights, dims, preferred_element_type=f32)
+    gate = jnp.sum(gate_m[...], axis=1, keepdims=True)
+    keep_gate_ref[...] = jnp.broadcast_to(gate, keep_gate_ref.shape)
+    gate = jnp.sum(gate_o[...], axis=1, keepdims=True)
+    coarse = gate.astype(bf16).astype(f32)
+    fine = (gate - coarse).astype(bf16).astype(f32)
     lane = lax.broadcasted_iota(jnp.int32, (slots, LANES), 1)
     give_ref[:, width:] = jnp.where(
-        lane == 0, coarse.astype(f32), jnp.where(lane == 1, fine.astype(f32), 0.0)
+        lane == 0, coarse, jnp.where(lane == 1, fine, 0.0)
     ).astype(bf16)
 
 
@@ -160,19 +191,22 @@
 
 
 def combine_body(
-    experts, capacity, ids_ref, gates_ref, back_ref, dtok_ref, dgate_ref, wide_ref, rows_ref
+    experts, capacity, plane_ref, ids_ref, gates_ref, b0, b1, b2, b3,
+    dtok_ref, dgate_ref, wide_ref, rows_ref,
 ):
     slots = experts * capacity
     tiles = dtok_ref.shape[1] // LANES
     step = (capacity + 1) * tiles
-    wide_ref[...] = back_ref[...].astype(f32)
+    for i, ref in enumerate((b0, b1, b2, b3)):
+        part = ref.shape[0]
+        wide_ref[i * part : (i + 1) * part] = ref[...].astype(f32)
     for c in range(capacity):
         for j in range(tiles):
             rows_ref[j, pl.ds(c, experts, stride=capacity), :] = wide_ref[
                 pl.ds(c * tiles + j, experts, stride=step), :
             ]
     table = wide_ref[pl.ds(capacity * tiles, experts, stride=step), :].astype(bf16)
-    pick_first, pick_second = one_hots(ids_ref, experts, capacity)
+    pick_first, pick_second = one_hots(ids_ref, plane_ref[0], experts, capacity)
     pick = (pick_first + pick_second).astype(bf16)
     for j in range(tiles):
         dtok_ref[:, j * LANES : (j + 1) * LANES] = lax.dot_general(
@@ -214,6 +248,27 @@
     swap = [(i, i ^ 1) for i in range(replicas)]
     sds = jax.ShapeDtypeStruct
 
+    plane = ((lax.axis_index("expert") >> 2) & 3).astype(jnp.int32).reshape(1)
+    in_plane = [[x * 16 + zl * 4 + y for x in range(4) for y in range(4)] for zl in range(4)]
+
+    def device(z, core, x, y):
+        return ((z >> 2) * 2 + core) * experts + x * 16 + (z & 3) * 4 + y
+
+    def along_z(hops):
+        length = 2 * replicas
+        return [
+            (device(z, c, x, y), device((z + hops(z)) % length, c, x, y))
+            for z in range(length) for c in range(2) for x in range(4) for y in range(4)
+        ]
+
+    out_perms = [along_z(lambda z: 1), along_z(lambda z: -2 if z % 2 else 2), along_z(lambda z: -1)]
+    home_perms = [[(b, a) for a, b in perm] for perm in out_perms]
+
+    def move(values, perms):
+        return values[:1] + [
+            lax.ppermute(v, ("dp", "expert"), perm) for v, perm in zip(values[1:], perms)
+        ]
+
     def send(value, perm):
         return lax.ppermute(value, "dp", perm)
 
@@ -226,32 +281,43 @@
         jnp.concatenate([wi, wo], axis=0), "dp", axis=0, tiled=False, axis_index_groups=same_core
     )
 
+    chunk = capacity * 2 * tiles
+    quarter = sds((slots * 2 * tiles // 4, LANES), bf16)
     payload = call(
         lambda *refs: dispatch_body(experts, capacity, *refs),
-        sds((slots * 2 * tiles, LANES), bf16),
+        (quarter,) * 4,
         "dispatch",
         [pltpu.VMEM((slots * 2 * tiles, LANES), f32)],
-    )(ids, gates_row, tokens, out_grad)
+        1,
+        4,
+    )(plane, ids, gates_row, tokens, out_grad)
+    payload = move(list(payload), out_perms)
     mine = lax.all_to_all(
-        payload.reshape(experts, capacity * 2 * tiles, LANES),
-        "expert", split_axis=0, concat_axis=0, tiled=True,
+        jnp.concatenate([v.reshape(experts // 4, chunk, LANES) for v in payload], axis=1),
+        "expert", split_axis=0, concat_axis=0, tiled=True, axis_index_groups=in_plane,
     ).reshape(slots * 2 * tiles, LANES)
+    rows = sds((slots, width), bf16)
+    wide = pltpu.VMEM((slots * 2 * tiles, LANES), f32)
+    x, dy = call(unpack, (rows, rows), "unpack", [wide])(mine)
+    mine, x, dy, weights = lax.optimization_barrier((mine, x, dy, weights))
     other = send(mine, swap)
-    rows = sds((2 * slots, width), bf16)
-    x, dy = call(
-        unpack_body, (rows, rows), "unpack", [pltpu.VMEM((slots * 2 * tiles, LANES), f32)]
-    )(mine, other)
-    x, dy, weights = lax.optimization_barrier((x, dy, weights))
     blocks = replicas // 2
-    d_pre, gate, grads = call(
-        units_body,
-        (
-            sds((2 * slots, blocks * shard), bf16),
-            sds((2 * slots, LANES), f32),
-            sds((blocks, 2 * shard, width), bf16),
-        ),
-        "units",
-    )(x, dy, weights)
+    hidden = sds((slots, blocks * shard), bf16)
+    gate_shape = sds((slots, LANES), f32)
+    dpre_mine, act_mine, gate_mine = call(mine_body, (hidden, hidden, gate_shape), "mine")(
+        x, dy, weights
+    )
+    dpre_other, gate_other, grads = call(
+        other_body,
+        (hidden, gate_shape, sds((blocks, 2 * shard, width), bf16)),
+        "other",
+        [
+            wide,
+            pltpu.VMEM((slots, width), bf16),
+            pltpu.VMEM((slots, width), bf16),
+            pltpu.VMEM((slots, blocks * shard), bf16),
+        ],
+    )(other, x, dy, dpre_mine, act_mine, weights)
     total = lax.psum_scatter(
         grads, "dp", scatter_dimension=0, tiled=False, axis_index_groups=same_core
     )
@@ -259,7 +325,7 @@
         dx_body,
         (sds((slots, width), f32), sds((slots, LANES), f32), sds((slots, width + LANES), bf16)),
         "input_gradient",
-    )(d_pre, weights, gate)
+    )(dpre_mine, dpre_other, weights, gate_mine, gate_other)
     took = send(give, swap)
     back = call(
         lambda *refs: pack_body(experts, capacity, *refs),
@@ -270,10 +336,18 @@
             pltpu.VMEM((experts * (capacity + 1) * tiles, LANES), f32),
         ],
     )(keep, keep_gate, took)
+    chunk = (capacity + 1) * tiles
     back = lax.all_to_all(
-        back.reshape(experts, (capacity + 1) * tiles, LANES),
-        "expert", split_axis=0, concat_axis=0, tiled=True,
-    ).reshape(experts * (capacity + 1) * tiles, LANES)
+        back.reshape(experts // 4, 4 * chunk, LANES),
+        "expert", split_axis=0, concat_axis=0, tiled=True, axis_index_groups=in_plane,
+    )
+    back = move(
+        [
+            back[:, i * chunk : (i + 1) * chunk].reshape(experts // 4 * chunk, LANES)
+            for i in range(4)
+        ],
+        home_perms,
+    )
     d_tokens, gate_grad = call(
         lambda *refs: combine_body(experts, capacity, *refs),
         (sds((tok_rows, width), bf16), sds((2, tok_rows), bf16)),
@@ -282,7 +356,9 @@
             pltpu.VMEM((experts * (capacity + 1) * tiles, LANES), f32),
             pltpu.VMEM((tiles, slots, LANES), f32),
         ],
-    )(ids, gates_row, back)
+        1,
+        6,
+    )(plane, ids, gates_row, *back)
     d_tokens, gate_grad, total = lax.optimization_barrier((d_tokens, gate_grad, total))
     own = sds((width, shard), f32)
     grad_in, grad_out = call(finish_body, (own, own), "finish")(total)

time: 311 us -> 282 us (0.907)
  the two profiles are of different devices: /device:TPU:83 before, /device:TPU:6 now
where the time goes in v4:
time: 282 us; the launch traced here: 281 us
  waiting for transfers between devices  124 us (44%)
  blocking collectives  59.2 us (21%)
  Pallas kernels  42.9 us (15%)
  starting transfers between devices  33.2 us (12%)
  between operations  14.1 us (5%)
  local copies, waits for them, and re-layouts  4.13 us (1%)
  other arithmetic  3.15 us (1%)
    ppermute x6, waiting for transfers between devices, move(): lax.ppermute(v, ('dp', 'expert'), perm)  119 us
    all_to_all x1, blocking collectives, shards(): lax.all_to_all(jnp.concatenate([v.reshape(experts // 4, chunk, LANES) for...  35.1 us
    ppermute x6, starting transfers between devices, move(): lax.ppermute(v, ('dp', 'expert'), perm)  28.6 us
    all_to_all x1, blocking collectives, shards(): lax.all_to_all(back.reshape(experts // 4, 4 * chunk, LANES), 'expert', sp...  24.1 us
    pallas_call x1, Pallas kernels, shards(): call(other_body, (hidden, gate_shape, sds((blocks, 2 * shard, width), bf1...  11.6 us
    pallas_call x1, Pallas kernels, shards(): x, dy = call(unpack, (rows, rows), 'unpack', [wide])(mine)  5.7 us
  transfers between devices with their start and end apart: 10, of which 7 were waited for; matrix products, arithmetic and copies ran while one was open for 1% of the time, Pallas kernels for 10%

profile of v4, /device:TPU:6, one launch (start us, length us, event | category | flops | bytes accessed | tf_op | source)
XLA Modules:
  0.0 281.1 jit_solution(13710628863632850279)
XLA Ops:
  7.2 0.0 all-gather.3.cloned.1.call-start
  7.2 1.9 pad_maximum_fusion.1
  9.1 0.0 all-gather.3.cloned.1.call-update
  9.1 0.0 reduce-scatter.2.cloned.1.call-start
  9.1 4.3 %dispatch.1 = (bf16[2304,128]{1,0:T(8,128)(2,1)}, bf16[2304,128]{1,0:T(8,128)(2,1)}, bf16[2304,128]{1,0:T(8,128)(2,1)}, bf16[2304,128]{1,0:T(8,128)(2,1)}) custom-call(s32[1]{0:T(128)} %bitcast.refs_0_, s32[2,192]{1,0:T(2,128)} %bitcast.37, bf16[2,192]{1,0:T(2,128)(2,1)} %bitcast.39, bf16[192,1024]{1,0:T(8,128)(2,1)} %refs_3_.1, bf16[192,1024]{1,0:T(8,128)(2,1)} %refs_4_.1), custom_call_target="tpu_custom_call" | custom-call | tf_op jit(solution)/shard_map/dispatch/pallas_call | solution.py:286
  13.5 3.8 %collective-permute-start = (bf16[2304,128]{1,0:T(8,128)(2,1)}, bf16[2304,128]{1,0:T(8,128)(2,1)S(1)}, u32[]{:S(2)}, u32[]{:S(2)}) collective-permute-start(bf16[2304,128]{1,0:T(8,128)(2,1)} %get-tuple-element.31), channel_id=1, source_target_pairs={{0,4},{1,5},{2,6},{3,7},{16,20},{17,21},{18,22},{19,23},{32,36},{3... | collective-permute-start | bytes 1769480 | tf_op jit(solution)/shard_map/ppermute | solution.py:269
  17.3 5.2 %collective-permute-start.1 = (bf16[2304,128]{1,0:T(8,128)(2,1)}, bf16[2304,128]{1,0:T(8,128)(2,1)S(1)}, u32[]{:S(2)}, u32[]{:S(2)}) collective-permute-start(bf16[2304,128]{1,0:T(8,128)(2,1)} %get-tuple-element.32), channel_id=1, source_target_pairs={{0,8},{1,9},{2,10},{3,11},{16,24},{17,25},{18,26},{19,27},{32,40},... | collective-permute-start | bytes 1769480 | tf_op jit(solution)/shard_map/ppermute | solution.py:269
  22.5 8.7 %collective-permute-start.2 = (bf16[2304,128]{1,0:T(8,128)(2,1)}, bf16[2304,128]{1,0:T(8,128)(2,1)S(1)}, u32[]{:S(2)}, u32[]{:S(2)}) collective-permute-start(bf16[2304,128]{1,0:T(8,128)(2,1)} %get-tuple-element.33), channel_id=1, source_target_pairs={{0,396},{1,397},{2,398},{3,399},{16,412},{17,413},{18,414},{19,415... | collective-permute-start | bytes 1769480 | tf_op jit(solution)/shard_map/ppermute | solution.py:269
  31.2 13.0 %collective-permute-done = bf16[2304,128]{1,0:T(8,128)(2,1)S(1)} collective-permute-done((bf16[2304,128]{1,0:T(8,128)(2,1)}, bf16[2304,128]{1,0:T(8,128)(2,1)S(1)}, u32[]{:S(2)}, u32[]{:S(2)}) %collective-permute-start) | collective-permute-done | bytes 589856 | tf_op jit(solution)/shard_map/ppermute | solution.py:269
  44.2 53.4 %collective-permute-done.1 = bf16[2304,128]{1,0:T(8,128)(2,1)S(1)} collective-permute-done((bf16[2304,128]{1,0:T(8,128)(2,1)}, bf16[2304,128]{1,0:T(8,128)(2,1)S(1)}, u32[]{:S(2)}, u32[]{:S(2)}) %collective-permute-start.1) | collective-permute-done | bytes 589856 | tf_op jit(solution)/shard_map/ppermute | solution.py:269
  97.6 6.2 %collective-permute-done.2 = bf16[2304,128]{1,0:T(8,128)(2,1)S(1)} collective-permute-done((bf16[2304,128]{1,0:T(8,128)(2,1)}, bf16[2304,128]{1,0:T(8,128)(2,1)S(1)}, u32[]{:S(2)}, u32[]{:S(2)}) %collective-permute-start.2) | collective-permute-done | bytes 589856 | tf_op jit(solution)/shard_map/ppermute | solution.py:269
  103.8 1.3 pad_maximum_fusion
  105.1 35.1 %all_to_all.10 = bf16[16,576,128]{2,1,0:T(8,128)(2,1)} all-to-all(bf16[16,576,128]{2,1,0:T(8,128)(2,1)S(1)} %pad_maximum_fusion), channel_id=1, replica_groups={{0,1,2,3,16,17,18,19,32,33,34,35,48,49,50,51},{4,5,6,7,20,21,22,23,36,3..., dimensions={0} | all-to-all | bytes 4718592 | tf_op jit(solution)/shard_map/all_to_all | solution.py:295
  140.2 0.0 copy-start
  140.2 5.7 %unpack.1 = (bf16[576,1024]{1,0:T(8,128)(2,1)}, bf16[576,1024]{1,0:T(8,128)(2,1)}) custom-call(bf16[9216,128]{1,0:T(8,128)(2,1)} %bitcast.23), custom_call_target="tpu_custom_call" | custom-call | tf_op jit(solution)/shard_map/unpack/pallas_call | solution.py:301
  145.9 0.0 all-gather.3.cloned.1.call-done
  145.9 0.0 copy-done
  145.9 2.1 collective-permute-start.3
  148.0 5.4 %mine.1 = (bf16[576,512]{1,0:T(8,128)(2,1)}, bf16[576,512]{1,0:T(8,128)(2,1)}, f32[576,128]{1,0:T(8,128)}) custom-call(bf16[576,1024]{1,0:T(8,128)(2,1)} %get-tuple-element.36.x_ref, bf16[576,1024]{1,0:T(8,128)(2,1)} %get-tuple-element.37.dy_ref, bf16[4,2048,128]{2,1,0:T(8,128)(2,1)} %bitcast.20), custom_call_target="tpu_custom_call" | custom-call | tf_op jit(solution)/shard_map/mine/pallas_call | solution.py:307
  153.4 0.0 collective-permute-done.3.got_ref
  153.4 0.0 copy-start.1
  153.4 1.4 copy-done.1
  154.8 11.6 %other.1 = (bf16[576,512]{1,0:T(8,128)(2,1)}, f32[576,128]{1,0:T(8,128)}, bf16[4,256,1024]{2,1,0:T(8,128)(2,1)}) custom-call(bf16[9216,128]{1,0:T(8,128)(2,1)} %copy-done.1, bf16[576,1024]{1,0:T(8,128)(2,1)} %get-tuple-element.36.x_ref, bf16[576,1024]{1,0:T(8,128)(2,1)} %get-tuple-element.37.dy_ref, bf16[576,512]{1,0:T(8,128)(2,1)} %get-tuple-element.39.dpre_in_ref.dpre_m, ...), custom_call_target="tpu_custom_call" | custom-call | tf_op jit(solution)/shard_map/other/pallas_call | solution.py:310
  166.4 0.0 reduce-scatter.2.cloned.1.call-update
  166.4 5.3 %input_gradient.1 = (f32[576,1024]{1,0:T(8,128)}, f32[576,128]{1,0:T(8,128)}, bf16[576,1152]{1,0:T(8,128)(2,1)}) custom-call(bf16[576,512]{1,0:T(8,128)(2,1)} %get-tuple-element.39.dpre_in_ref.dpre_m, bf16[576,512]{1,0:T(8,128)(2,1)} %get-tuple-element.42.dpre_o, bf16[4,2048,128]{2,1,0:T(8,128)(2,1)} %bitcast.22, f32[576,128]{1,0:T(8,128)} %get-tuple-element.43.gate_m, ...), custom_call_target="tpu_custom_call" | custom-call | tf_op jit(solution)/shard_map/input_gradient/pallas_call | solution.py:324
  171.7 2.4 collective-permute-start.4
  174.1 2.9 %collective-permute-done.4.refs_2_ = bf16[576,1152]{1,0:T(8,128)(2,1)S(1)} collective-permute-done((bf16[576,1152]{1,0:T(8,128)(2,1)}, bf16[576,1152]{1,0:T(8,128)(2,1)S(1)}, u32[]{:S(2)}, u32[]{:S(2)}) %collective-permute-start.4) | collective-permute-done | bytes 1327136 | tf_op jit(solution)/shard_map/ppermute | solution.py:273
  177.0 0.0 copy-start.2
  177.0 1.1 copy-done.2
  178.1 4.7 %pack.1 = bf16[5120,128]{1,0:T(8,128)(2,1)} custom-call(f32[576,1024]{1,0:T(8,128)} %get-tuple-element.45.refs_0_, f32[576,128]{1,0:T(8,128)} %get-tuple-element.46.refs_1_, bf16[576,1152]{1,0:T(8,128)(2,1)} %copy-done.2), custom_call_target="tpu_custom_call" | custom-call | tf_op jit(solution)/shard_map/pack/pallas_call | solution.py:330
  182.8 24.1 %all_to_all.11 = bf16[16,320,128]{2,1,0:T(8,128)(2,1)S(1)} all-to-all(bf16[16,320,128]{2,1,0:T(8,128)(2,1)} %bitcast.25), channel_id=1, replica_groups={{0,1,2,3,16,17,18,19,32,33,34,35,48,49,50,51},{4,5,6,7,20,21,22,23,36,3..., dimensions={0} | all-to-all | bytes 2621440 | tf_op jit(solution)/shard_map/all_to_all | solution.py:340
  206.9 0.8 fusion
  207.7 1.9 collective-permute-start.6
  209.6 5.4 %collective-permute-start.7 = (bf16[1280,128]{1,0:T(8,128)(2,1)S(1)}, bf16[1280,128]{1,0:T(8,128)(2,1)S(1)}, u32[]{:S(2)}, u32[]{:S(2)}) collective-permute-start(bf16[1280,128]{1,0:T(8,128)(2,1)S(1)} %bitcast.33), channel_id=1, source_target_pairs={{396,0},{397,1},{398,2},{399,3},{412,16},{413,17},{414,18},{415,19... | collective-permute-start | bytes 983048 | tf_op jit(solution)/shard_map/ppermute | solution.py:269
  215.0 3.7 %collective-permute-start.5 = (bf16[1280,128]{1,0:T(8,128)(2,1)S(1)}, bf16[1280,128]{1,0:T(8,128)(2,1)S(1)}, u32[]{:S(2)}, u32[]{:S(2)}) collective-permute-start(bf16[1280,128]{1,0:T(8,128)(2,1)S(1)} %bitcast.32), channel_id=1, source_target_pairs={{4,0},{5,1},{6,2},{7,3},{20,16},{21,17},{22,18},{23,19},{36,32},{3... | collective-permute-start | bytes 983048 | tf_op jit(solution)/shard_map/ppermute | solution.py:269
  218.6 21.1 %collective-permute-done.6.refs_5_ = bf16[1280,128]{1,0:T(8,128)(2,1)S(1)} collective-permute-done((bf16[1280,128]{1,0:T(8,128)(2,1)S(1)}, bf16[1280,128]{1,0:T(8,128)(2,1)S(1)}, u32[]{:S(2)}, u32[]{:S(2)}) %collective-permute-start.6) | collective-permute-done | bytes 327712 | tf_op jit(solution)/shard_map/ppermute | solution.py:269
  239.7 0.0 copy-start.3
  239.7 25.1 %collective-permute-done.7.refs_6_ = bf16[1280,128]{1,0:T(8,128)(2,1)S(1)} collective-permute-done((bf16[1280,128]{1,0:T(8,128)(2,1)S(1)}, bf16[1280,128]{1,0:T(8,128)(2,1)S(1)}, u32[]{:S(2)}, u32[]{:S(2)}) %collective-permute-start.7) | collective-permute-done | bytes 327712 | tf_op jit(solution)/shard_map/ppermute | solution.py:269
  264.8 0.0 copy-start.4
  264.8 0.0 collective-permute-done.5.refs_4_
  264.9 0.0 copy-start.5
  264.9 0.0 copy-done.3
  264.9 0.7 copy-done.4
  265.6 0.1 copy-done.5
  265.7 3.7 %combine.1 = (bf16[192,1024]{1,0:T(8,128)(2,1)}, bf16[2,192]{1,0:T(2,128)(2,1)}) custom-call(s32[1]{0:T(128)} %bitcast.refs_0_, s32[2,192]{1,0:T(2,128)} %bitcast.38, bf16[2,192]{1,0:T(2,128)(2,1)} %bitcast.40, bf16[1280,128]{1,0:T(8,128)(2,1)} %bitcast.26, bf16[1280,128]{1,0:T(8,128)(2,1)} %copy-done.5, bf16[1280,128]{1,0:T(8,128)(2,1)} %copy-done.3, ...), custom_call_target="tpu_custom_call" | custom-call | tf_op jit(solution)/shard_map/combine/pallas_call | solution.py:351
  269.4 2.7 reduce-scatter.2.cloned.1.call-done
  272.1 2.1 finish.1
Async XLA Ops:
  7.2 138.7 %all-gather.3.cloned.1.call-start = ((), (), s32[]{:S(2)}) async-start(), calls=%async_computation.4 | async-start | bytes 2621440 | tf_op jit(solution)/shard_map/all_gather | solution.py:280
  9.1 263.0 %reduce-scatter.2.cloned.1.call-start = ((), (), s32[]{:S(2)}) async-start(), calls=%async_computation.3 | async-start | bytes 2621440 | tf_op jit(solution)/shard_map/reduce_scatter | solution.py:321
  13.5 30.7 %collective-permute-start = (bf16[2304,128]{1,0:T(8,128)(2,1)}, bf16[2304,128]{1,0:T(8,128)(2,1)S(1)}, u32[]{:S(2)}, u32[]{:S(2)}) collective-permute-start(bf16[2304,128]{1,0:T(8,128)(2,1)} %get-tuple-element.31), channel_id=1, source_target_pairs={{0,4},{1,5},{2,6},{3,7},{16,20},{17,21},{18,22},{19,23},{32,36},{3... | collective-permute-start | bytes 1769480 | tf_op jit(solution)/shard_map/ppermute | solution.py:269
  17.3 80.3 %collective-permute-start.1 = (bf16[2304,128]{1,0:T(8,128)(2,1)}, bf16[2304,128]{1,0:T(8,128)(2,1)S(1)}, u32[]{:S(2)}, u32[]{:S(2)}) collective-permute-start(bf16[2304,128]{1,0:T(8,128)(2,1)} %get-tuple-element.32), channel_id=1, source_target_pairs={{0,8},{1,9},{2,10},{3,11},{16,24},{17,25},{18,26},{19,27},{32,40},... | collective-permute-start | bytes 1769480 | tf_op jit(solution)/shard_map/ppermute | solution.py:269
  22.5 81.3 %collective-permute-start.2 = (bf16[2304,128]{1,0:T(8,128)(2,1)}, bf16[2304,128]{1,0:T(8,128)(2,1)S(1)}, u32[]{:S(2)}, u32[]{:S(2)}) collective-permute-start(bf16[2304,128]{1,0:T(8,128)(2,1)} %get-tuple-element.33), channel_id=1, source_target_pairs={{0,396},{1,397},{2,398},{3,399},{16,412},{17,413},{18,414},{19,415... | collective-permute-start | bytes 1769480 | tf_op jit(solution)/shard_map/ppermute | solution.py:269
  140.2 5.7 %copy-start = (bf16[16,576,128]{2,1,0:T(8,128)(2,1)S(1)}, bf16[16,576,128]{2,1,0:T(8,128)(2,1)}, u32[]{:S(2)}) copy-start(bf16[16,576,128]{2,1,0:T(8,128)(2,1)} %all_to_all.10) | copy-start | bytes 7077892
  145.9 7.5 %collective-permute-start.3 = (bf16[9216,128]{1,0:T(8,128)(2,1)S(1)}, bf16[9216,128]{1,0:T(8,128)(2,1)S(1)}, u32[]{:S(2)}, u32[]{:S(2)}) collective-permute-start(bf16[9216,128]{1,0:T(8,128)(2,1)S(1)} %bitcast.24), channel_id=1, source_target_pairs={{0,64},{64,0},{128,192},{192,128},{256,320},{320,256},{384,448},{4... | collective-permute-start | bytes 7077896 | tf_op jit(solution)/shard_map/ppermute | solution.py:273
  153.4 1.4 copy-start.1
  171.7 5.3 %collective-permute-start.4 = (bf16[576,1152]{1,0:T(8,128)(2,1)}, bf16[576,1152]{1,0:T(8,128)(2,1)S(1)}, u32[]{:S(2)}, u32[]{:S(2)}) collective-permute-start(bf16[576,1152]{1,0:T(8,128)(2,1)} %get-tuple-element.47), channel_id=1, source_target_pairs={{0,64},{64,0},{128,192},{192,128},{256,320},{320,256},{384,448},{4... | collective-permute-start | bytes 3981320 | tf_op jit(solution)/shard_map/ppermute | solution.py:273
  177.0 1.1 copy-start.2
  207.7 32.1 %collective-permute-start.6 = (bf16[1280,128]{1,0:T(8,128)(2,1)S(1)}, bf16[1280,128]{1,0:T(8,128)(2,1)S(1)}, u32[]{:S(2)}, u32[]{:S(2)}) collective-permute-start(bf16[1280,128]{1,0:T(8,128)(2,1)S(1)} %bitcast.34), channel_id=1, source_target_pairs={{8,0},{9,1},{10,2},{11,3},{24,16},{25,17},{26,18},{27,19},{40,32},... | collective-permute-start | bytes 983048 | tf_op jit(solution)/shard_map/ppermute | solution.py:269
  209.6 55.3 %collective-permute-start.7 = (bf16[1280,128]{1,0:T(8,128)(2,1)S(1)}, bf16[1280,128]{1,0:T(8,128)(2,1)S(1)}, u32[]{:S(2)}, u32[]{:S(2)}) collective-permute-start(bf16[1280,128]{1,0:T(8,128)(2,1)S(1)} %bitcast.33), channel_id=1, source_target_pairs={{396,0},{397,1},{398,2},{399,3},{412,16},{413,17},{414,18},{415,19... | collective-permute-start | bytes 983048 | tf_op jit(solution)/shard_map/ppermute | solution.py:269
  215.0 49.9 %collective-permute-start.5 = (bf16[1280,128]{1,0:T(8,128)(2,1)S(1)}, bf16[1280,128]{1,0:T(8,128)(2,1)S(1)}, u32[]{:S(2)}, u32[]{:S(2)}) collective-permute-start(bf16[1280,128]{1,0:T(8,128)(2,1)S(1)} %bitcast.32), channel_id=1, source_target_pairs={{4,0},{5,1},{6,2},{7,3},{20,16},{21,17},{22,18},{23,19},{36,32},{3... | collective-permute-start | bytes 983048 | tf_op jit(solution)/shard_map/ppermute | solution.py:269
  239.7 25.1 %copy-start.3 = (bf16[1280,128]{1,0:T(8,128)(2,1)}, bf16[1280,128]{1,0:T(8,128)(2,1)S(1)}, u32[]{:S(2)}) copy-start(bf16[1280,128]{1,0:T(8,128)(2,1)S(1)} %collective-permute-done.6.refs_5_) | copy-start | bytes 983044
  264.8 0.7 copy-start.4
  264.9 0.8 copy-start.5
Sparse Core Ops, SparseCore 0:
  10.7 100.3 all-gather.2
  166.5 105.5 reduce-scatter.1

commit v5 on v4

--- a/solution.py
+++ b/solution.py
@@ -29,12 +29,13 @@
     )
 
 
-def slot_targets(ids_ref, plane, experts, capacity):
+def slot_targets(ids_ref, plane, experts, capacity, planes_first):
     tokens = ids_ref.shape[1]
 
     def near_order(expert):
         up = (((expert >> 2) & 3) - plane) & 3
-        return up * 16 + (expert >> 4) * 4 + (expert & 3)
+        place = (expert >> 4) * 4 + (expert & 3)
+        return up * 16 + place if planes_first else place * 4 + up
 
     first = near_order(ids_ref[0:1, :])
     second = near_order(ids_ref[1:2, :])
@@ -53,18 +54,17 @@
     return first * capacity + slot_first, second * capacity + slot_second
 
 
-def one_hots(ids_ref, plane, experts, capacity):
+def one_hots(ids_ref, plane, experts, capacity, planes_first):
     tokens = ids_ref.shape[1]
-    first, second = slot_targets(ids_ref, plane, experts, capacity)
+    first, second = slot_targets(ids_ref, plane, experts, capacity, planes_first)
     slot = lax.broadcasted_iota(jnp.int32, (experts * capacity, tokens), 0)
     return (slot == first).astype(f32), (slot == second).astype(f32)
 
 
-def dispatch_body(experts, capacity, plane_ref, ids_ref, gates_ref, x_ref, dy_ref, *refs):
-    out_refs, wide_ref = refs[:-1], refs[-1]
+def dispatch_body(experts, capacity, plane_ref, ids_ref, gates_ref, x_ref, dy_ref, out_ref, wide_ref):
     width = x_ref.shape[1] // LANES
     slots = experts * capacity
-    pick_first, pick_second = one_hots(ids_ref, plane_ref[0], experts, capacity)
+    pick_first, pick_second = one_hots(ids_ref, plane_ref[0], experts, capacity, False)
     gates = gates_ref[...].astype(f32)
     pick = (pick_first + pick_second).astype(bf16)
     gated = (pick_first * gates[0:1, :] + pick_second * gates[1:2, :]).astype(bf16)
@@ -74,9 +74,7 @@
         cols = slice(j * LANES, (j + 1) * LANES)
         wide_ref[pl.ds(j, slots, stride=2 * width), :] = rows_x[:, cols]
         wide_ref[pl.ds(width + j, slots, stride=2 * width), :] = rows_dy[:, cols]
-    part = slots * 2 * width // len(out_refs)
-    for i, out_ref in enumerate(out_refs):
-        out_ref[...] = wide_ref[i * part : (i + 1) * part].astype(bf16)
+    out_ref[...] = wide_ref[...].astype(bf16)
 
 
 def gelu_parts(pre):
@@ -88,18 +86,22 @@
     return value, slope
 
 
-def unpack(got_ref, x_ref, dy_ref, wide_ref):
-    slots = x_ref.shape[0]
-    width = x_ref.shape[1] // LANES
-    wide_ref[...] = got_ref[...].astype(f32)
-    for j in range(width):
-        cols = slice(j * LANES, (j + 1) * LANES)
-        x_ref[:, cols] = wide_ref[pl.ds(j, slots, stride=2 * width), :].astype(bf16)
-        dy_ref[:, cols] = wide_ref[pl.ds(width + j, slots, stride=2 * width), :].astype(bf16)
-
-
-def project(x, dy, w_ref, dpre_ref, act_ref, gate_ref):
-    width = x.shape[1]
+def unpack_body(r0, r1, r2, r3, rows_ref, wide_ref):
+    slots, width = rows_ref.shape
+    tiles = width // LANES
+    for i, ref in enumerate((r0, r1, r2, r3)):
+        part = ref.shape[0]
+        wide_ref[i * part : (i + 1) * part] = ref[...].astype(f32)
+    for j in range(tiles):
+        rows_ref[:, j * LANES : (j + 1) * LANES] = wide_ref[
+            pl.ds(j, slots, stride=tiles), :
+        ].astype(bf16)
+
+
+def project(rows_ref, w_ref, dpre_ref, act_ref, gate_ref):
+    width = rows_ref.shape[1] // 2
+    x = rows_ref[:, :width]
+    dy = rows_ref[:, width:]
     gates = []
     for pair in range(0, w_ref.shape[0], 2):
         cols = slice(pair * LANES, (pair + 2) * LANES)
@@ -116,25 +118,23 @@
     gate_ref[...] = sum(gates[1:], gates[0])
 
 
-def mine_body(x_ref, dy_ref, w_ref, dpre_ref, act_ref, gate_ref):
-    project(x_ref[...], dy_ref[...], w_ref, dpre_ref, act_ref, gate_ref)
-
-
 def other_body(
-    got_ref, x_ref, dy_ref, dpre_in_ref, act_in_ref, w_ref,
-    dpre_ref, gate_ref, grad_ref, wide_ref, xo_ref, dyo_ref, act_ref,
+    mine_ref, other_ref, dpre_in_ref, act_in_ref, w_ref, dpre_ref, gate_ref, grad_ref, act_ref
 ):
-    unpack(got_ref, xo_ref, dyo_ref, wide_ref)
-    project(xo_ref[...], dyo_ref[...], w_ref, dpre_ref, act_ref, gate_ref)
+    width = mine_ref.shape[1] // 2
+    project(other_ref, w_ref, dpre_ref, act_ref, gate_ref)
     for row, sides in (
-        (0, ((dpre_in_ref, x_ref), (dpre_ref, xo_ref))),
-        (LANES, ((act_in_ref, dy_ref), (act_ref, dyo_ref))),
+        (0, ((dpre_in_ref, mine_ref), (dpre_ref, other_ref))),
+        (LANES, ((act_in_ref, mine_ref), (act_ref, other_ref))),
     ):
         for pair in range(0, w_ref.shape[0], 2):
             cols = slice(pair * LANES, (pair + 2) * LANES)
             grad = sum(
                 lax.dot_general(
-                    left[:, cols], right[...], (((0,), (0,)), ((), ())), preferred_element_type=f32
+                    left[:, cols],
+                    right[:, width:] if row else right[:, :width],
+                    (((0,), (0,)), ((), ())),
+                    preferred_element_type=f32,
                 )
                 for left, right in sides
             ).astype(bf16)
@@ -187,7 +187,11 @@
         wide_ref[pl.ds(capacity * tiles + j, experts, stride=step), :] = (
             table if j == 0 else jnp.zeros_like(table)
         )
-    out_ref[...] = wide_ref[...].astype(bf16)
+    places = out_ref.shape[0]
+    planes = experts // places
+    for i in range(planes):
+        part = wide_ref[i * places * step : (i + 1) * places * step]
+        out_ref[:, i * step : (i + 1) * step] = part.reshape(places, step, LANES).astype(bf16)
 
 
 def combine_body(
@@ -206,7 +210,7 @@
                 pl.ds(c * tiles + j, experts, stride=step), :
             ]
     table = wide_ref[pl.ds(capacity * tiles, experts, stride=step), :].astype(bf16)
-    pick_first, pick_second = one_hots(ids_ref, plane_ref[0], experts, capacity)
+    pick_first, pick_second = one_hots(ids_ref, plane_ref[0], experts, capacity, True)
     pick = (pick_first + pick_second).astype(bf16)
     for j in range(tiles):
         dtok_ref[:, j * LANES : (j + 1) * LANES] = lax.dot_general(
@@ -269,6 +273,12 @@
             lax.ppermute(v, ("dp", "expert"), perm) for v, perm in zip(values[1:], perms)
         ]
 
+    def by_plane(array, rows):
+        return [
+            array[:, i * rows : (i + 1) * rows].reshape(experts // 4 * rows, LANES)
+            for i in range(4)
+        ]
+
     def send(value, perm):
         return lax.ppermute(value, "dp", perm)
 
@@ -282,42 +292,35 @@
     )
 
     chunk = capacity * 2 * tiles
-    quarter = sds((slots * 2 * tiles // 4, LANES), bf16)
+    wide = pltpu.VMEM((slots * 2 * tiles, LANES), f32)
     payload = call(
         lambda *refs: dispatch_body(experts, capacity, *refs),
-        (quarter,) * 4,
+        sds((slots * 2 * tiles, LANES), bf16),
         "dispatch",
-        [pltpu.VMEM((slots * 2 * tiles, LANES), f32)],
+        [wide],
         1,
         4,
     )(plane, ids, gates_row, tokens, out_grad)
-    payload = move(list(payload), out_perms)
-    mine = lax.all_to_all(
-        jnp.concatenate([v.reshape(experts // 4, chunk, LANES) for v in payload], axis=1),
+    got = lax.all_to_all(
+        payload.reshape(experts // 4, 4 * chunk, LANES),
         "expert", split_axis=0, concat_axis=0, tiled=True, axis_index_groups=in_plane,
-    ).reshape(slots * 2 * tiles, LANES)
-    rows = sds((slots, width), bf16)
-    wide = pltpu.VMEM((slots * 2 * tiles, LANES), f32)
-    x, dy = call(unpack, (rows, rows), "unpack", [wide])(mine)
-    mine, x, dy, weights = lax.optimization_barrier((mine, x, dy, weights))
+    )
+    got = move(by_plane(got, chunk), out_perms)
+    mine = call(unpack_body, sds((slots, 2 * width), bf16), "unpack", [wide])(*got)
+    mine, weights = lax.optimization_barrier((mine, weights))
     other = send(mine, swap)
     blocks = replicas // 2
     hidden = sds((slots, blocks * shard), bf16)
     gate_shape = sds((slots, LANES), f32)
-    dpre_mine, act_mine, gate_mine = call(mine_body, (hidden, hidden, gate_shape), "mine")(
-        x, dy, weights
+    dpre_mine, act_mine, gate_mine = call(project, (hidden, hidden, gate_shape), "mine")(
+        mine, weights
     )
     dpre_other, gate_other, grads = call(
         other_body,
         (hidden, gate_shape, sds((blocks, 2 * shard, width), bf16)),
         "other",
-        [
-            wide,
-            pltpu.VMEM((slots, width), bf16),
-            pltpu.VMEM((slots, width), bf16),
-            pltpu.VMEM((slots, blocks * shard), bf16),
-        ],
-    )(other, x, dy, dpre_mine, act_mine, weights)
+        [pltpu.VMEM((slots, blocks * shard), bf16)],
+    )(mine, other, dpre_mine, act_mine, weights)
     total = lax.psum_scatter(
         grads, "dp", scatter_dimension=0, tiled=False, axis_index_groups=same_core
     )
@@ -329,7 +332,7 @@
     took = send(give, swap)
     back = call(
         lambda *refs: pack_body(experts, capacity, *refs),
-        sds((experts * (capacity + 1) * tiles, LANES), bf16),
+        sds((experts // 4, 4 * (capacity + 1) * tiles, LANES), bf16),
         "pack",
         [
             pltpu.VMEM((tiles, slots, LANES), f32),
@@ -338,16 +341,10 @@
     )(keep, keep_gate, took)
     chunk = (capacity + 1) * tiles
     back = lax.all_to_all(
-        back.reshape(experts // 4, 4 * chunk, LANES),
+        back,
         "expert", split_axis=0, concat_axis=0, tiled=True, axis_index_groups=in_plane,
     )
-    back = move(
-        [
-            back[:, i * chunk : (i + 1) * chunk].reshape(experts // 4 * chunk, LANES)
-            for i in range(4)
-        ],
-        home_perms,
-    )
+    back = move(by_plane(back, chunk), home_perms)
     d_tokens, gate_grad = call(
         lambda *refs: combine_body(experts, capacity, *refs),
         (sds((tok_rows, width), bf16), sds((2, tok_rows), bf16)),

time: 282 us -> 270 us (0.957)
  waiting for transfers between devices: 124 us -> 113 us
    ppermute x6, waiting for transfers between devices: 119 us -> 107 us  [move(): lax.ppermute(v, ('dp', 'expert'), perm)]
  transfers between devices with their start and end apart: 10 -> 10, of which waited for: 7 -> 7; matrix products, arithmetic and copies ran while one was open for 1% -> 1% of each run, Pallas kernels for 10% -> 11%
where the time goes in v5:
time: 270 us; the launch traced here: 269 us
  waiting for transfers between devices  113 us (42%)
  blocking collectives  61.6 us (23%)
  Pallas kernels  41.6 us (15%)
  starting transfers between devices  31.2 us (12%)
  between operations  14.1 us (5%)
  local copies, waits for them, and re-layouts  5.92 us (2%)
    ppermute x6, waiting for transfers between devices, move(): lax.ppermute(v, ('dp', 'expert'), perm)  107 us
    all_to_all x1, blocking collectives, shards(): lax.all_to_all(payload.reshape(experts // 4, 4 * chunk, LANES), 'expert',...  36.3 us
    ppermute x6, starting transfers between devices, move(): lax.ppermute(v, ('dp', 'expert'), perm)  26.6 us
    all_to_all x1, blocking collectives, shards(): lax.all_to_all(back, 'expert', split_axis=0, concat_axis=0, tiled=True, a...  25.4 us
    pallas_call x1, Pallas kernels, shards(): call(other_body, (hidden, gate_shape, sds((blocks, 2 * shard, width), bf1...  9.98 us
    pallas_call x1, Pallas kernels, shards(): call(unpack_body, sds((slots, 2 * width), bf16), 'unpack', [wide])(*got)  5.61 us
  transfers between devices with their start and end apart: 10, of which 7 were waited for; matrix products, arithmetic and copies ran while one was open for 1% of the time, Pallas kernels for 11%

profile of v5, /device:TPU:6, one launch (start us, length us, event | category | flops | bytes accessed | tf_op | source)
XLA Modules:
  0.0 269.0 jit_solution(16609911096356248139)
XLA Ops:
  7.2 0.0 all-gather.3.cloned.1.call-start
  7.2 1.9 pad_maximum_fusion
  9.1 0.0 all-gather.3.cloned.1.call-update
  9.1 0.0 reduce-scatter.2.cloned.1.call-start
  9.1 4.7 %dispatch.1 = bf16[9216,128]{1,0:T(8,128)(2,1)} custom-call(s32[1]{0:T(128)} %bitcast.refs_0_, s32[2,192]{1,0:T(2,128)} %bitcast.34, bf16[2,192]{1,0:T(2,128)(2,1)} %bitcast.36, bf16[192,1024]{1,0:T(8,128)(2,1)} %refs_3_.1, bf16[192,1024]{1,0:T(8,128)(2,1)} %refs_4_.1), custom_call_target="tpu_custom_call" | custom-call | tf_op jit(solution)/shard_map/dispatch/pallas_call | solution.py:296
  13.8 36.3 %all_to_all.10 = bf16[16,576,128]{2,1,0:T(8,128)(2,1)S(1)} all-to-all(bf16[16,576,128]{2,1,0:T(8,128)(2,1)} %bitcast.22), channel_id=1, replica_groups={{0,1,2,3,16,17,18,19,32,33,34,35,48,49,50,51},{4,5,6,7,20,21,22,23,36,3..., dimensions={0} | all-to-all | bytes 4718592 | tf_op jit(solution)/shard_map/all_to_all | solution.py:304
  50.1 1.0 fusion
  51.1 5.4 %collective-permute-start.1 = (bf16[2304,128]{1,0:T(8,128)(2,1)S(1)}, bf16[2304,128]{1,0:T(8,128)(2,1)S(1)}, u32[]{:S(2)}, u32[]{:S(2)}) collective-permute-start(bf16[2304,128]{1,0:T(8,128)(2,1)S(1)} %bitcast.27), channel_id=1, source_target_pairs={{0,8},{1,9},{2,10},{3,11},{16,24},{17,25},{18,26},{19,27},{32,40},... | collective-permute-start | bytes 1769480 | tf_op jit(solution)/shard_map/ppermute | solution.py:273
  56.5 9.6 %collective-permute-start.2 = (bf16[2304,128]{1,0:T(8,128)(2,1)S(1)}, bf16[2304,128]{1,0:T(8,128)(2,1)S(1)}, u32[]{:S(2)}, u32[]{:S(2)}) collective-permute-start(bf16[2304,128]{1,0:T(8,128)(2,1)S(1)} %bitcast.26), channel_id=1, source_target_pairs={{0,396},{1,397},{2,398},{3,399},{16,412},{17,413},{18,414},{19,415... | collective-permute-start | bytes 1769480 | tf_op jit(solution)/shard_map/ppermute | solution.py:273
  66.1 1.9 collective-permute-start
  68.1 27.9 %collective-permute-done.1.r2 = bf16[2304,128]{1,0:T(8,128)(2,1)S(1)} collective-permute-done((bf16[2304,128]{1,0:T(8,128)(2,1)S(1)}, bf16[2304,128]{1,0:T(8,128)(2,1)S(1)}, u32[]{:S(2)}, u32[]{:S(2)}) %collective-permute-start.1) | collective-permute-done | bytes 589856 | tf_op jit(solution)/shard_map/ppermute | solution.py:273
  96.0 0.0 copy-start.2
  96.0 30.2 %collective-permute-done.2.r3 = bf16[2304,128]{1,0:T(8,128)(2,1)S(1)} collective-permute-done((bf16[2304,128]{1,0:T(8,128)(2,1)S(1)}, bf16[2304,128]{1,0:T(8,128)(2,1)S(1)}, u32[]{:S(2)}, u32[]{:S(2)}) %collective-permute-start.2) | collective-permute-done | bytes 589856 | tf_op jit(solution)/shard_map/ppermute | solution.py:273
  126.2 0.0 copy-start.3
  126.2 4.3 %collective-permute-done.r1 = bf16[2304,128]{1,0:T(8,128)(2,1)S(1)} collective-permute-done((bf16[2304,128]{1,0:T(8,128)(2,1)S(1)}, bf16[2304,128]{1,0:T(8,128)(2,1)S(1)}, u32[]{:S(2)}, u32[]{:S(2)}) %collective-permute-start) | collective-permute-done | bytes 589856 | tf_op jit(solution)/shard_map/ppermute | solution.py:273
  130.5 0.0 copy-start.4
  130.5 0.0 copy-done.2
  130.5 0.0 copy-done.3
  130.5 0.8 copy-done.4
  131.3 5.6 %unpack.1.rows_ref.mine_ref = bf16[576,2048]{1,0:T(8,128)(2,1)} custom-call(bf16[2304,128]{1,0:T(8,128)(2,1)} %bitcast.23, bf16[2304,128]{1,0:T(8,128)(2,1)} %copy-done.4, bf16[2304,128]{1,0:T(8,128)(2,1)} %copy-done.2, bf16[2304,128]{1,0:T(8,128)(2,1)} %copy-done.3), custom_call_target="tpu_custom_call" | custom-call | tf_op jit(solution)/shard_map/unpack/pallas_call | solution.py:309
  137.0 0.0 all-gather.3.cloned.1.call-done
  137.0 2.3 collective-permute-start.3
  139.3 5.4 %mine.1 = (bf16[576,512]{1,0:T(8,128)(2,1)}, bf16[576,512]{1,0:T(8,128)(2,1)}, f32[576,128]{1,0:T(8,128)}) custom-call(bf16[576,2048]{1,0:T(8,128)(2,1)} %unpack.1.rows_ref.mine_ref, bf16[4,2048,128]{2,1,0:T(8,128)(2,1)} %bitcast.19), custom_call_target="tpu_custom_call" | custom-call | tf_op jit(solution)/shard_map/mine/pallas_call | solution.py:315
  144.6 0.0 collective-permute-done.3.other_ref
  144.6 0.0 copy-start
  144.6 1.4 copy-done
  146.1 10.0 %other.1 = (bf16[576,512]{1,0:T(8,128)(2,1)}, f32[576,128]{1,0:T(8,128)}, bf16[4,256,1024]{2,1,0:T(8,128)(2,1)}) custom-call(bf16[576,2048]{1,0:T(8,128)(2,1)} %unpack.1.rows_ref.mine_ref, bf16[576,2048]{1,0:T(8,128)(2,1)} %copy-done, bf16[576,512]{1,0:T(8,128)(2,1)} %get-tuple-element.24.dpre_in_ref.dpre_m, bf16[576,512]{1,0:T(8,128)(2,1)} %get-tuple-element.25.act_in_ref, ...), custom_call_target="tpu_custom_call" | custom-call | tf_op jit(solution)/shard_map/other/pallas_call | solution.py:318
  156.1 0.0 reduce-scatter.2.cloned.1.call-update
  156.1 5.3 %input_gradient.1 = (f32[576,1024]{1,0:T(8,128)}, f32[576,128]{1,0:T(8,128)}, bf16[576,1152]{1,0:T(8,128)(2,1)}) custom-call(bf16[576,512]{1,0:T(8,128)(2,1)} %get-tuple-element.24.dpre_in_ref.dpre_m, bf16[576,512]{1,0:T(8,128)(2,1)} %get-tuple-element.26.dpre_o, bf16[4,2048,128]{2,1,0:T(8,128)(2,1)} %bitcast.21, f32[576,128]{1,0:T(8,128)} %get-tuple-element.27.gate_m, ...), custom_call_target="tpu_custom_call" | custom-call | tf_op jit(solution)/shard_map/input_gradient/pallas_call | solution.py:327
  161.4 2.2 collective-permute-start.4
  163.6 2.9 %collective-permute-done.4.refs_2_ = bf16[576,1152]{1,0:T(8,128)(2,1)S(1)} collective-permute-done((bf16[576,1152]{1,0:T(8,128)(2,1)}, bf16[576,1152]{1,0:T(8,128)(2,1)S(1)}, u32[]{:S(2)}, u32[]{:S(2)}) %collective-permute-start.4) | collective-permute-done | bytes 1327136 | tf_op jit(solution)/shard_map/ppermute | solution.py:283
  166.6 0.0 copy-start.1
  166.6 1.1 copy-done.1
  167.6 4.7 %pack.1 = bf16[16,320,128]{2,1,0:T(8,128)(2,1)} custom-call(f32[576,1024]{1,0:T(8,128)} %get-tuple-element.29.refs_0_, f32[576,128]{1,0:T(8,128)} %get-tuple-element.30.refs_1_, bf16[576,1152]{1,0:T(8,128)(2,1)} %copy-done.1), custom_call_target="tpu_custom_call" | custom-call | tf_op jit(solution)/shard_map/pack/pallas_call | solution.py:333
  172.3 25.4 %all_to_all.11 = bf16[16,320,128]{2,1,0:T(8,128)(2,1)S(1)} all-to-all(bf16[16,320,128]{2,1,0:T(8,128)(2,1)} %pack.1), channel_id=1, replica_groups={{0,1,2,3,16,17,18,19,32,33,34,35,48,49,50,51},{4,5,6,7,20,21,22,23,36,3..., dimensions={0} | all-to-all | bytes 2621440 | tf_op jit(solution)/shard_map/all_to_all | solution.py:343
  197.7 0.8 fusion.1
  198.5 2.6 collective-permute-start.6
  201.0 3.6 %collective-permute-start.7 = (bf16[1280,128]{1,0:T(8,128)(2,1)S(1)}, bf16[1280,128]{1,0:T(8,128)(2,1)S(1)}, u32[]{:S(2)}, u32[]{:S(2)}) collective-permute-start(bf16[1280,128]{1,0:T(8,128)(2,1)S(1)} %bitcast.30), channel_id=1, source_target_pairs={{396,0},{397,1},{398,2},{399,3},{412,16},{413,17},{414,18},{415,19... | collective-permute-start | bytes 983048 | tf_op jit(solution)/shard_map/ppermute | solution.py:273
  204.7 3.4 %collective-permute-start.5 = (bf16[1280,128]{1,0:T(8,128)(2,1)S(1)}, bf16[1280,128]{1,0:T(8,128)(2,1)S(1)}, u32[]{:S(2)}, u32[]{:S(2)}) collective-permute-start(bf16[1280,128]{1,0:T(8,128)(2,1)S(1)} %bitcast.29), channel_id=1, source_target_pairs={{4,0},{5,1},{6,2},{7,3},{20,16},{21,17},{22,18},{23,19},{36,32},{3... | collective-permute-start | bytes 983048 | tf_op jit(solution)/shard_map/ppermute | solution.py:273
  208.1 22.8 %collective-permute-done.6.refs_5_ = bf16[1280,128]{1,0:T(8,128)(2,1)S(1)} collective-permute-done((bf16[1280,128]{1,0:T(8,128)(2,1)S(1)}, bf16[1280,128]{1,0:T(8,128)(2,1)S(1)}, u32[]{:S(2)}, u32[]{:S(2)}) %collective-permute-start.6) | collective-permute-done | bytes 327712 | tf_op jit(solution)/shard_map/ppermute | solution.py:273
  230.9 0.0 copy-start.5
  230.9 21.8 %collective-permute-done.7.refs_6_ = bf16[1280,128]{1,0:T(8,128)(2,1)S(1)} collective-permute-done((bf16[1280,128]{1,0:T(8,128)(2,1)S(1)}, bf16[1280,128]{1,0:T(8,128)(2,1)S(1)}, u32[]{:S(2)}, u32[]{:S(2)}) %collective-permute-start.7) | collective-permute-done | bytes 327712 | tf_op jit(solution)/shard_map/ppermute | solution.py:273
  252.7 0.0 copy-start.6
  252.7 0.0 collective-permute-done.5.refs_4_
  252.7 0.0 copy-start.7
  252.7 0.0 copy-done.5
  252.7 0.7 copy-done.6
  253.4 0.1 copy-done.7
  253.5 3.8 %combine.1 = (bf16[192,1024]{1,0:T(8,128)(2,1)}, bf16[2,192]{1,0:T(2,128)(2,1)}) custom-call(s32[1]{0:T(128)} %bitcast.refs_0_, s32[2,192]{1,0:T(2,128)} %bitcast.35, bf16[2,192]{1,0:T(2,128)(2,1)} %bitcast.37, bf16[1280,128]{1,0:T(8,128)(2,1)} %bitcast.24, bf16[1280,128]{1,0:T(8,128)(2,1)} %copy-done.7, bf16[1280,128]{1,0:T(8,128)(2,1)} %copy-done.5, ...), custom_call_target="tpu_custom_call" | custom-call | tf_op jit(solution)/shard_map/combine/pallas_call | solution.py:348
  257.3 2.7 %reduce-scatter.2.cloned.1.call-done = bf16[1,256,1024]{2,1,0:T(8,128)(2,1)} async-done(((bf16[4,256,1024]{2,1,0:T(8,128)(2,1)}), bf16[1,256,1024]{2,1,0:T(8,128)(2,1)}) %reduce-scatter.2.cloned.1.call-update) | async-done | bytes 524304 | tf_op jit(solution)/shard_map/reduce_scatter | solution.py:324
  260.0 2.1 finish.1
Async XLA Ops:
  7.2 129.8 %all-gather.3.cloned.1.call-start = ((), (), s32[]{:S(2)}) async-start(), calls=%async_computation.4 | async-start | bytes 2621440 | tf_op jit(solution)/shard_map/all_gather | solution.py:290
  9.1 250.9 %reduce-scatter.2.cloned.1.call-start = ((), (), s32[]{:S(2)}) async-start(), calls=%async_computation.3 | async-start | bytes 2621440 | tf_op jit(solution)/shard_map/reduce_scatter | solution.py:324
  51.1 44.9 %collective-permute-start.1 = (bf16[2304,128]{1,0:T(8,128)(2,1)S(1)}, bf16[2304,128]{1,0:T(8,128)(2,1)S(1)}, u32[]{:S(2)}, u32[]{:S(2)}) collective-permute-start(bf16[2304,128]{1,0:T(8,128)(2,1)S(1)} %bitcast.27), channel_id=1, source_target_pairs={{0,8},{1,9},{2,10},{3,11},{16,24},{17,25},{18,26},{19,27},{32,40},... | collective-permute-start | bytes 1769480 | tf_op jit(solution)/shard_map/ppermute | solution.py:273
  56.5 69.6 %collective-permute-start.2 = (bf16[2304,128]{1,0:T(8,128)(2,1)S(1)}, bf16[2304,128]{1,0:T(8,128)(2,1)S(1)}, u32[]{:S(2)}, u32[]{:S(2)}) collective-permute-start(bf16[2304,128]{1,0:T(8,128)(2,1)S(1)} %bitcast.26), channel_id=1, source_target_pairs={{0,396},{1,397},{2,398},{3,399},{16,412},{17,413},{18,414},{19,415... | collective-permute-start | bytes 1769480 | tf_op jit(solution)/shard_map/ppermute | solution.py:273
  66.1 64.4 %collective-permute-start = (bf16[2304,128]{1,0:T(8,128)(2,1)S(1)}, bf16[2304,128]{1,0:T(8,128)(2,1)S(1)}, u32[]{:S(2)}, u32[]{:S(2)}) collective-permute-start(bf16[2304,128]{1,0:T(8,128)(2,1)S(1)} %bitcast.25), channel_id=1, source_target_pairs={{0,4},{1,5},{2,6},{3,7},{16,20},{17,21},{18,22},{19,23},{32,36},{3... | collective-permute-start | bytes 1769480 | tf_op jit(solution)/shard_map/ppermute | solution.py:273
  96.0 34.5 %copy-start.2 = (bf16[2304,128]{1,0:T(8,128)(2,1)}, bf16[2304,128]{1,0:T(8,128)(2,1)S(1)}, u32[]{:S(2)}) copy-start(bf16[2304,128]{1,0:T(8,128)(2,1)S(1)} %collective-permute-done.1.r2) | copy-start | bytes 1769476
  126.2 4.4 %copy-start.3 = (bf16[2304,128]{1,0:T(8,128)(2,1)}, bf16[2304,128]{1,0:T(8,128)(2,1)S(1)}, u32[]{:S(2)}) copy-start(bf16[2304,128]{1,0:T(8,128)(2,1)S(1)} %collective-permute-done.2.r3) | copy-start | bytes 1769476
  130.5 0.8 copy-start.4
  137.0 7.7 %collective-permute-start.3 = (bf16[576,2048]{1,0:T(8,128)(2,1)}, bf16[576,2048]{1,0:T(8,128)(2,1)S(1)}, u32[]{:S(2)}, u32[]{:S(2)}) collective-permute-start(bf16[576,2048]{1,0:T(8,128)(2,1)} %unpack.1.rows_ref.mine_ref), channel_id=1, source_target_pairs={{0,64},{64,0},{128,192},{192,128},{256,320},{320,256},{384,448},{4... | collective-permute-start | bytes 7077896 | tf_op jit(solution)/shard_map/ppermute | solution.py:283
  144.6 1.4 copy-start
  161.4 5.2 %collective-permute-start.4 = (bf16[576,1152]{1,0:T(8,128)(2,1)}, bf16[576,1152]{1,0:T(8,128)(2,1)S(1)}, u32[]{:S(2)}, u32[]{:S(2)}) collective-permute-start(bf16[576,1152]{1,0:T(8,128)(2,1)} %get-tuple-element.31), channel_id=1, source_target_pairs={{0,64},{64,0},{128,192},{192,128},{256,320},{320,256},{384,448},{4... | collective-permute-start | bytes 3981320 | tf_op jit(solution)/shard_map/ppermute | solution.py:283
  166.6 1.1 copy-start.1
  198.5 32.5 %collective-permute-start.6 = (bf16[1280,128]{1,0:T(8,128)(2,1)S(1)}, bf16[1280,128]{1,0:T(8,128)(2,1)S(1)}, u32[]{:S(2)}, u32[]{:S(2)}) collective-permute-start(bf16[1280,128]{1,0:T(8,128)(2,1)S(1)} %bitcast.31), channel_id=1, source_target_pairs={{8,0},{9,1},{10,2},{11,3},{24,16},{25,17},{26,18},{27,19},{40,32},... | collective-permute-start | bytes 983048 | tf_op jit(solution)/shard_map/ppermute | solution.py:273
  201.0 51.6 %collective-permute-start.7 = (bf16[1280,128]{1,0:T(8,128)(2,1)S(1)}, bf16[1280,128]{1,0:T(8,128)(2,1)S(1)}, u32[]{:S(2)}, u32[]{:S(2)}) collective-permute-start(bf16[1280,128]{1,0:T(8,128)(2,1)S(1)} %bitcast.30), channel_id=1, source_target_pairs={{396,0},{397,1},{398,2},{399,3},{412,16},{413,17},{414,18},{415,19... | collective-permute-start | bytes 983048 | tf_op jit(solution)/shard_map/ppermute | solution.py:273
  204.7 48.0 %collective-permute-start.5 = (bf16[1280,128]{1,0:T(8,128)(2,1)S(1)}, bf16[1280,128]{1,0:T(8,128)(2,1)S(1)}, u32[]{:S(2)}, u32[]{:S(2)}) collective-permute-start(bf16[1280,128]{1,0:T(8,128)(2,1)S(1)} %bitcast.29), channel_id=1, source_target_pairs={{4,0},{5,1},{6,2},{7,3},{20,16},{21,17},{22,18},{23,19},{36,32},{3... | collective-permute-start | bytes 983048 | tf_op jit(solution)/shard_map/ppermute | solution.py:273
  230.9 21.8 %copy-start.5 = (bf16[1280,128]{1,0:T(8,128)(2,1)}, bf16[1280,128]{1,0:T(8,128)(2,1)S(1)}, u32[]{:S(2)}) copy-start(bf16[1280,128]{1,0:T(8,128)(2,1)S(1)} %collective-permute-done.6.refs_5_) | copy-start | bytes 983044
  252.7 0.7 copy-start.6
  252.7 0.8 copy-start.7
Sparse Core Ops, SparseCore 0:
  10.7 122.0 all-gather.2
  156.2 103.7 reduce-scatter.1

commit v6 on v5

--- a/solution.py
+++ b/solution.py
@@ -86,73 +86,80 @@
     return value, slope
 
 
-def unpack_body(r0, r1, r2, r3, rows_ref, wide_ref):
-    slots, width = rows_ref.shape
+def unpack_body(r0, r1, r2, r3, x_ref, dy_ref, wide_ref):
+    slots, width = x_ref.shape
     tiles = width // LANES
     for i, ref in enumerate((r0, r1, r2, r3)):
         part = ref.shape[0]
         wide_ref[i * part : (i + 1) * part] = ref[...].astype(f32)
     for j in range(tiles):
-        rows_ref[:, j * LANES : (j + 1) * LANES] = wide_ref[
-            pl.ds(j, slots, stride=tiles), :
-        ].astype(bf16)
-
-
-def project(rows_ref, w_ref, dpre_ref, act_ref, gate_ref):
-    width = rows_ref.shape[1] // 2
-    x = rows_ref[:, :width]
-    dy = rows_ref[:, width:]
-    gates = []
-    for pair in range(0, w_ref.shape[0], 2):
+        cols = slice(j * LANES, (j + 1) * LANES)
+        x_ref[:, cols] = wide_ref[pl.ds(j, slots, stride=2 * tiles), :].astype(bf16)
+        dy_ref[:, cols] = wide_ref[pl.ds(tiles + j, slots, stride=2 * tiles), :].astype(bf16)
+
+
+def pair_of(w_ref, pair):
+    return jnp.concatenate([w_ref[pair], w_ref[pair + 1]], axis=1)
+
+
+def weight_gradient(units_ref, sides, grad_ref):
+    slots = sides[0].shape[0]
+    for pair in range(0, grad_ref.shape[0], 2):
         cols = slice(pair * LANES, (pair + 2) * LANES)
-        w_first = jnp.concatenate([w_ref[pair, :width], w_ref[pair + 1, :width]], axis=1)
-        w_second = jnp.concatenate([w_ref[pair, width:], w_ref[pair + 1, width:]], axis=1)
-        pre = jnp.dot(x, w_first, preferred_element_type=f32)
-        dy_proj = jnp.dot(dy, w_second, preferred_element_type=f32)
-        value, slope = gelu_parts(pre)
-        activated = value.astype(bf16)
-        gate = activated.astype(f32) * dy_proj
-        gates += [gate[:, :LANES], gate[:, LANES:]]
-        dpre_ref[:, cols] = (dy_proj * slope).astype(bf16)
-        act_ref[:, cols] = activated
-    gate_ref[...] = sum(gates[1:], gates[0])
-
-
-def other_body(
-    mine_ref, other_ref, dpre_in_ref, act_in_ref, w_ref, dpre_ref, gate_ref, grad_ref, act_ref
-):
-    width = mine_ref.shape[1] // 2
-    project(other_ref, w_ref, dpre_ref, act_ref, gate_ref)
-    for row, sides in (
-        (0, ((dpre_in_ref, mine_ref), (dpre_ref, other_ref))),
-        (LANES, ((act_in_ref, mine_ref), (act_ref, other_ref))),
-    ):
+        grad = sum(
+            lax.dot_general(
+                units_ref[half * slots : (half + 1) * slots, cols],
+                side,
+                (((0,), (0,)), ((), ())),
+                preferred_element_type=f32,
+            )
+            for half, side in enumerate(sides)
+        ).astype(bf16)
+        grad_ref[pair] = grad[:LANES]
+        grad_ref[pair + 1] = grad[LANES:]
+
+
+def first_body(xm_ref, xo_ref, dym_ref, dyo_ref, w_ref, act_ref, slope_ref, grad_ref):
+    slots = xm_ref.shape[0]
+    for half, x_ref in enumerate((xm_ref, xo_ref)):
+        rows = slice(half * slots, (half + 1) * slots)
         for pair in range(0, w_ref.shape[0], 2):
             cols = slice(pair * LANES, (pair + 2) * LANES)
-            grad = sum(
-                lax.dot_general(
-                    left[:, cols],
-                    right[:, width:] if row else right[:, :width],
-                    (((0,), (0,)), ((), ())),
-                    preferred_element_type=f32,
-                )
-                for left, right in sides
-            ).astype(bf16)
-            grad_ref[pair, row : row + LANES] = grad[:LANES]
-            grad_ref[pair + 1, row : row + LANES] = grad[LANES:]
-
-
-def dx_body(dpre_m, dpre_o, w_ref, gate_m, gate_o, keep_ref, keep_gate_ref, give_ref):
+            pre = jnp.dot(x_ref[...], pair_of(w_ref, pair), preferred_element_type=f32)
+            value, slope = gelu_parts(pre)
+            act_ref[rows, cols] = value.astype(bf16)
+            slope_ref[rows, cols] = slope
+    weight_gradient(act_ref, (dym_ref[...], dyo_ref[...]), grad_ref)
+
+
+def second_body(
+    xm_ref, xo_ref, dym_ref, dyo_ref, act_ref, slope_ref, w_ref, dpre_ref, gate_ref, grad_ref
+):
+    slots = xm_ref.shape[0]
+    for half, dy_ref in enumerate((dym_ref, dyo_ref)):
+        rows = slice(half * slots, (half + 1) * slots)
+        gates = []
+        for pair in range(0, w_ref.shape[0], 2):
+            cols = slice(pair * LANES, (pair + 2) * LANES)
+            dy_proj = jnp.dot(dy_ref[...], pair_of(w_ref, pair), preferred_element_type=f32)
+            dpre_ref[rows, cols] = (dy_proj * slope_ref[rows, cols]).astype(bf16)
+            gate = act_ref[rows, cols].astype(f32) * dy_proj
+            gates += [gate[:, :LANES], gate[:, LANES:]]
+        gate_ref[rows] = sum(gates[1:], gates[0])
+    weight_gradient(dpre_ref, (xm_ref[...], xo_ref[...]), grad_ref)
+
+
+def dx_body(dpre_ref, w_ref, gate_ref, keep_ref, keep_gate_ref, give_ref):
     slots = keep_ref.shape[0]
     width = keep_ref.shape[1]
-    weights = jnp.concatenate([w_ref[i, :width] for i in range(w_ref.shape[0])], axis=1)
+    weights = jnp.concatenate([w_ref[i] for i in range(w_ref.shape[0])], axis=1)
     dims = (((1,), (1,)), ((), ()))
-    give = lax.dot_general(dpre_o[...], weights, dims, preferred_element_type=f32)
+    give = lax.dot_general(dpre_ref[slots:], weights, dims, preferred_element_type=f32)
     give_ref[:, :width] = give.astype(bf16)
-    keep_ref[...] = lax.dot_general(dpre_m[...], weights, dims, preferred_element_type=f32)
-    gate = jnp.sum(gate_m[...], axis=1, keepdims=True)
+    keep_ref[...] = lax.dot_general(dpre_ref[:slots], weights, dims, preferred_element_type=f32)
+    gate = jnp.sum(gate_ref[:slots], axis=1, keepdims=True)
     keep_gate_ref[...] = jnp.broadcast_to(gate, keep_gate_ref.shape)
-    gate = jnp.sum(gate_o[...], axis=1, keepdims=True)
+    gate = jnp.sum(gate_ref[slots:], axis=1, keepdims=True)
     coarse = gate.astype(bf16).astype(f32)
     fine = (gate - coarse).astype(bf16).astype(f32)
     lane = lax.broadcasted_iota(jnp.int32, (slots, LANES), 1)
@@ -234,10 +241,8 @@
     dgate_ref[...] = (sums / gates).astype(bf16)
 
 
-def finish_body(total_ref, gi_ref, go_ref):
-    total = total_ref[...].astype(f32)
-    gi_ref[...] = total[:LANES].T
-    go_ref[...] = total[LANES:].T
+def finish_body(total_ref, out_ref):
+    out_ref[...] = total_ref[...].astype(f32).T
 
 
 def shards(tokens, out_grad, gates, expert_ids, w_in, w_out):
@@ -287,10 +292,15 @@
     ids = expert_ids.T
     gates_row = gates.T
 
-    weights = lax.all_gather(
-        jnp.concatenate([wi, wo], axis=0), "dp", axis=0, tiled=False, axis_index_groups=same_core
-    )
-
+    def gather(w):
+        return lax.all_gather(w, "dp", axis=0, tiled=False, axis_index_groups=same_core)
+
+    def reduce(grads):
+        return lax.psum_scatter(
+            grads, "dp", scatter_dimension=0, tiled=False, axis_index_groups=same_core
+        )
+
+    full_in = gather(wi)
     chunk = capacity * 2 * tiles
     wide = pltpu.VMEM((slots * 2 * tiles, LANES), f32)
     payload = call(
@@ -305,30 +315,29 @@
         payload.reshape(experts // 4, 4 * chunk, LANES),
         "expert", split_axis=0, concat_axis=0, tiled=True, axis_index_groups=in_plane,
     )
+    got, full_in = lax.optimization_barrier((got, full_in))
     got = move(by_plane(got, chunk), out_perms)
-    mine = call(unpack_body, sds((slots, 2 * width), bf16), "unpack", [wide])(*got)
-    mine, weights = lax.optimization_barrier((mine, weights))
-    other = send(mine, swap)
+    got, wo = lax.optimization_barrier((got, wo))
+    full_out = gather(wo)
+    rows = sds((slots, width), bf16)
+    x, dy = call(unpack_body, (rows, rows), "unpack", [wide])(*got)
+    sides = (x, send(x, swap), dy, send(dy, swap))
     blocks = replicas // 2
-    hidden = sds((slots, blocks * shard), bf16)
-    gate_shape = sds((slots, LANES), f32)
-    dpre_mine, act_mine, gate_mine = call(project, (hidden, hidden, gate_shape), "mine")(
-        mine, weights
-    )
-    dpre_other, gate_other, grads = call(
-        other_body,
-        (hidden, gate_shape, sds((blocks, 2 * shard, width), bf16)),
-        "other",
-        [pltpu.VMEM((slots, blocks * shard), bf16)],
-    )(mine, other, dpre_mine, act_mine, weights)
-    total = lax.psum_scatter(
-        grads, "dp", scatter_dimension=0, tiled=False, axis_index_groups=same_core
-    )
+    hidden = (2 * slots, blocks * shard)
+    grad = sds((blocks, shard, width), bf16)
+    act, slope, grads_out = call(
+        first_body, (sds(hidden, bf16), sds(hidden, f32), grad), "first"
+    )(*sides, full_in)
+    total_out = reduce(grads_out)
+    d_pre, gate, grads_in = call(
+        second_body, (sds(hidden, bf16), sds((2 * slots, LANES), f32), grad), "second"
+    )(*sides, act, slope, full_out)
+    total_in = reduce(grads_in)
     keep, keep_gate, give = call(
         dx_body,
         (sds((slots, width), f32), sds((slots, LANES), f32), sds((slots, width + LANES), bf16)),
         "input_gradient",
-    )(dpre_mine, dpre_other, weights, gate_mine, gate_other)
+    )(d_pre, full_in, gate)
     took = send(give, swap)
     back = call(
         lambda *refs: pack_body(experts, capacity, *refs),
@@ -356,9 +365,10 @@
         1,
         6,
     )(plane, ids, gates_row, *back)
-    d_tokens, gate_grad, total = lax.optimization_barrier((d_tokens, gate_grad, total))
+    d_tokens, gate_grad, total_in = lax.optimization_barrier((d_tokens, gate_grad, total_in))
     own = sds((width, shard), f32)
-    grad_in, grad_out = call(finish_body, (own, own), "finish")(total)
+    grad_in = call(finish_body, own, "finish_in")(total_in)
+    grad_out = call(finish_body, own, "finish_out")(total_out)
     return d_tokens, gate_grad.T, grad_in[None], grad_out[None]
 
 

time: 270 us -> 311 us (1.15)
  waiting for transfers between devices: 113 us -> 190 us
  blocking collectives: 61.6 us -> 25.8 us
    all_gather x1 -> x2, waiting for transfers between devices: 0.01 us -> 97.9 us  [gather(): lax.all_gather(w, 'dp', axis=0, tiled=False, axis_index_groups=same_core)]
    ppermute x6, waiting for transfers between devices: 107 us -> 30.5 us  [move(): lax.ppermute(v, ('dp', 'expert'), perm)]
    reduce_scatter x1 -> x2, waiting for transfers between devices: 2.73 us -> 54.5 us  [reduce(): lax.psum_scatter(grads, 'dp', scatter_dimension=0, tiled=False, axis_inde...]
    all_to_all x1 -> x0, blocking collectives: 36.3 us -> none  [shards(): lax.all_to_all(payload.reshape(experts // 4, 4 * chunk, LANES), 'expert',...]
    ppermute x6, starting transfers between devices: 26.6 us -> 16.7 us  [move(): lax.ppermute(v, ('dp', 'expert'), perm)]
    all_to_all x0 -> x1, starting transfers between devices: none -> 9.43 us  [shards(): lax.all_to_all(payload.reshape(experts // 4, 4 * chunk, LANES), 'expert',...]
    ppermute x2 -> x3, starting transfers between devices: 4.49 us -> 6.22 us  [send(): return lax.ppermute(value, 'dp', perm)]
    pallas_call x4 -> x5, Pallas kernels: 23.1 us -> 24.7 us  [the longest x1 7.81 us: shards(): call(second_body, (sds(hidden, bf16), sds((2 * slots, LANES), f32), grad)...]
  transfers between devices with their start and end apart: 10 -> 14, of which waited for: 7 -> 12; matrix products, arithmetic and copies ran while one was open for 1% -> 0% of each run, Pallas kernels for 11% -> 12%
where the time goes in v6:
time: 311 us; the launch traced here: 310 us
  waiting for transfers between devices  190 us (61%)
  Pallas kernels  42.8 us (14%)
  starting transfers between devices  32.7 us (11%)
  blocking collectives  25.8 us (8%)
  between operations  13.9 us (4%)
  local copies, waits for them, and re-layouts  5.55 us (2%)
    all_gather x2, waiting for transfers between devices, gather(): lax.all_gather(w, 'dp', axis=0, tiled=False, axis_index_groups=same_core)  97.9 us
    reduce_scatter x2, waiting for transfers between devices, reduce(): lax.psum_scatter(grads, 'dp', scatter_dimension=0, tiled=False, axis_inde...  54.5 us
    ppermute x6, waiting for transfers between devices, move(): lax.ppermute(v, ('dp', 'expert'), perm)  30.5 us
    all_to_all x1, blocking collectives, shards(): lax.all_to_all(back, 'expert', split_axis=0, concat_axis=0, tiled=True, a...  25.8 us
    ppermute x6, starting transfers between devices, move(): lax.ppermute(v, ('dp', 'expert'), perm)  16.7 us
    all_to_all x1, starting transfers between devices, shards(): lax.all_to_all(payload.reshape(experts // 4, 4 * chunk, LANES), 'expert',...  9.43 us
    pallas_call x1, Pallas kernels, shards(): call(second_body, (sds(hidden, bf16), sds((2 * slots, LANES), f32), grad)...  7.81 us
    pallas_call x1, Pallas kernels, shards(): call(first_body, (sds(hidden, bf16), sds(hidden, f32), grad), 'first')  7.65 us
  transfers between devices with their start and end apart: 14, of which 12 were waited for; matrix products, arithmetic and copies ran while one was open for 0% of the time, Pallas kernels for 12%

profile of v6, /device:TPU:6, one launch (start us, length us, event | category | flops | bytes accessed | tf_op | source)
XLA Modules:
  0.0 310.3 jit_solution(13629652492905767703)
XLA Ops:
  7.2 4.7 %dispatch.1 = bf16[9216,128]{1,0:T(8,128)(2,1)} custom-call(s32[1]{0:T(128)} %bitcast.refs_0_, s32[2,192]{1,0:T(2,128)} %bitcast.34, bf16[2,192]{1,0:T(2,128)(2,1)} %bitcast.36, bf16[192,1024]{1,0:T(8,128)(2,1)} %refs_3_.1, bf16[192,1024]{1,0:T(8,128)(2,1)} %refs_4_.1), custom_call_target="tpu_custom_call" | custom-call | tf_op jit(solution)/shard_map/dispatch/pallas_call | solution.py:306
  11.8 9.4 %all-to-all-start = ((bf16[16,576,128]{2,1,0:T(8,128)(2,1)}), bf16[16,576,128]{2,1,0:T(8,128)(2,1)S(1)}, u32[]{:S(2)}, u32[]{:S(2)}) async-start(bf16[16,576,128]{2,1,0:T(8,128)(2,1)} %bitcast.19), calls=%async_computation | async-start | bytes 4718592 | tf_op jit(solution)/shard_map/all_to_all | solution.py:314
  21.3 0.0 all-gather.4.cloned.1.call-start
  21.3 0.7 all-gather.4.cloned.1.call-update
  22.0 0.0 all-gather.6.cloned.1.call-start
  22.0 64.8 %all-gather.4.cloned.1.call-done.w_ref = bf16[4,1024,128]{2,1,0:T(8,128)(2,1)} async-done(((bf16[1,1024,128]{2,1,0:T(8,128)(2,1)}), bf16[4,1024,128]{2,1,0:T(8,128)(2,1)}) %all-gather.4.cloned.1.call-update) | async-done | bytes 1048592 | tf_op jit(solution)/shard_map/all_gather | solution.py:296
  86.8 0.0 all-to-all-done
  86.8 1.0 fusion
  87.8 1.9 collective-permute-start.1
  89.7 2.6 collective-permute-start.2
  92.4 3.2 %collective-permute-start = (bf16[2304,128]{1,0:T(8,128)(2,1)S(1)}, bf16[2304,128]{1,0:T(8,128)(2,1)S(1)}, u32[]{:S(2)}, u32[]{:S(2)}) collective-permute-start(bf16[2304,128]{1,0:T(8,128)(2,1)S(1)} %bitcast.23), channel_id=1, source_target_pairs={{0,4},{1,5},{2,6},{3,7},{16,20},{17,21},{18,22},{19,23},{32,36},{3... | collective-permute-start | bytes 1769480 | tf_op jit(solution)/shard_map/ppermute | solution.py:278
  95.6 12.5 %collective-permute-done.1.r2 = bf16[2304,128]{1,0:T(8,128)(2,1)S(1)} collective-permute-done((bf16[2304,128]{1,0:T(8,128)(2,1)S(1)}, bf16[2304,128]{1,0:T(8,128)(2,1)S(1)}, u32[]{:S(2)}, u32[]{:S(2)}) %collective-permute-start.1) | collective-permute-done | bytes 589856 | tf_op jit(solution)/shard_map/ppermute | solution.py:278
  108.1 0.0 copy-start.3
  108.1 7.3 %collective-permute-done.2.r3 = bf16[2304,128]{1,0:T(8,128)(2,1)S(1)} collective-permute-done((bf16[2304,128]{1,0:T(8,128)(2,1)S(1)}, bf16[2304,128]{1,0:T(8,128)(2,1)S(1)}, u32[]{:S(2)}, u32[]{:S(2)}) %collective-permute-start.2) | collective-permute-done | bytes 589856 | tf_op jit(solution)/shard_map/ppermute | solution.py:278
  115.3 0.0 copy-start.4
  115.3 4.0 %collective-permute-done.r1 = bf16[2304,128]{1,0:T(8,128)(2,1)S(1)} collective-permute-done((bf16[2304,128]{1,0:T(8,128)(2,1)S(1)}, bf16[2304,128]{1,0:T(8,128)(2,1)S(1)}, u32[]{:S(2)}, u32[]{:S(2)}) %collective-permute-start) | collective-permute-done | bytes 589856 | tf_op jit(solution)/shard_map/ppermute | solution.py:278
  119.4 0.0 copy-start.5
  119.4 0.0 all-gather.6.cloned.1.call-update
  119.4 0.0 reduce-scatter.5.cloned.1.call-start
  119.4 0.0 copy-done.3
  119.4 0.0 copy-done.4
  119.5 0.7 copy-done.5
  120.2 5.5 %unpack.1 = (bf16[576,1024]{1,0:T(8,128)(2,1)}, bf16[576,1024]{1,0:T(8,128)(2,1)}) custom-call(bf16[2304,128]{1,0:T(8,128)(2,1)} %bitcast.20, bf16[2304,128]{1,0:T(8,128)(2,1)} %copy-done.5, bf16[2304,128]{1,0:T(8,128)(2,1)} %copy-done.3, bf16[2304,128]{1,0:T(8,128)(2,1)} %copy-done.4), custom_call_target="tpu_custom_call" | custom-call | tf_op jit(solution)/shard_map/unpack/pallas_call | solution.py:323
  125.6 1.9 collective-permute-start.3
  127.6 2.4 collective-permute-start.4
  130.0 0.6 collective-permute-done.3.xo_ref
  130.6 0.0 copy-start
  130.6 2.0 collective-permute-done.4.dyo_ref
  132.6 0.0 copy-done
  132.6 0.0 copy-start.1
  132.6 1.1 copy-done.1
  133.8 7.7 %first.1 = (bf16[1152,512]{1,0:T(8,128)(2,1)}, f32[1152,512]{1,0:T(8,128)}, bf16[4,128,1024]{2,1,0:T(8,128)(2,1)}) custom-call(bf16[576,1024]{1,0:T(8,128)(2,1)} %get-tuple-element.32.xm_ref, bf16[576,1024]{1,0:T(8,128)(2,1)} %copy-done, bf16[576,1024]{1,0:T(8,128)(2,1)} %get-tuple-element.33.dym_ref, bf16[576,1024]{1,0:T(8,128)(2,1)} %copy-done.1, ...), custom_call_target="tpu_custom_call" | custom-call | tf_op jit(solution)/shard_map/first/pallas_call | solution.py:328
  141.4 0.0 reduce-scatter.5.cloned.1.call-update
  141.4 0.2 reduce-scatter.3.cloned.1.call-start
  141.7 33.1 %all-gather.6.cloned.1.call-done = bf16[4096,128]{1,0:T(8,128)(2,1)} async-done(((bf16[1024,128]{1,0:T(8,128)(2,1)}), bf16[4096,128]{1,0:T(8,128)(2,1)}) %all-gather.6.cloned.1.call-update) | async-done | bytes 1048592 | tf_op jit(solution)/shard_map/all_gather | solution.py:296
  174.8 7.8 %second.1 = (bf16[1152,512]{1,0:T(8,128)(2,1)}, f32[1152,128]{1,0:T(8,128)}, bf16[4,128,1024]{2,1,0:T(8,128)(2,1)}) custom-call(bf16[576,1024]{1,0:T(8,128)(2,1)} %get-tuple-element.32.xm_ref, bf16[576,1024]{1,0:T(8,128)(2,1)} %copy-done, bf16[576,1024]{1,0:T(8,128)(2,1)} %get-tuple-element.33.dym_ref, bf16[576,1024]{1,0:T(8,128)(2,1)} %copy-done.1, ...), custom_call_target="tpu_custom_call" | custom-call | tf_op jit(solution)/shard_map/second/pallas_call | solution.py:332
  182.6 5.0 %input_gradient.1 = (f32[576,1024]{1,0:T(8,128)}, f32[576,128]{1,0:T(8,128)}, bf16[576,1152]{1,0:T(8,128)(2,1)}) custom-call(bf16[1152,512]{1,0:T(8,128)(2,1)} %get-tuple-element.38.dpre_ref, bf16[4,1024,128]{2,1,0:T(8,128)(2,1)} %all-gather.4.cloned.1.call-done.w_ref, f32[1152,128]{1,0:T(8,128)} %get-tuple-element.39.gate_ref), custom_call_target="tpu_custom_call" | custom-call | tf_op jit(solution)/shard_map/input_gradient/pallas_call | solution.py:336
  187.5 1.9 collective-permute-start.5
  189.5 0.0 reduce-scatter.3.cloned.1.call-update
  189.5 3.2 %collective-permute-done.5.refs_2_ = bf16[576,1152]{1,0:T(8,128)(2,1)S(1)} collective-permute-done((bf16[576,1152]{1,0:T(8,128)(2,1)}, bf16[576,1152]{1,0:T(8,128)(2,1)S(1)}, u32[]{:S(2)}, u32[]{:S(2)}) %collective-permute-start.5) | collective-permute-done | bytes 1327136 | tf_op jit(solution)/shard_map/ppermute | solution.py:288
  192.7 0.0 copy-start.2
  192.7 1.1 copy-done.2
  193.8 4.7 %pack.1 = bf16[16,320,128]{2,1,0:T(8,128)(2,1)} custom-call(f32[576,1024]{1,0:T(8,128)} %get-tuple-element.40.refs_0_, f32[576,128]{1,0:T(8,128)} %get-tuple-element.41.refs_1_, bf16[576,1152]{1,0:T(8,128)(2,1)} %copy-done.2), custom_call_target="tpu_custom_call" | custom-call | tf_op jit(solution)/shard_map/pack/pallas_call | solution.py:342
  198.5 25.8 %all_to_all.10 = bf16[16,320,128]{2,1,0:T(8,128)(2,1)S(1)} all-to-all(bf16[16,320,128]{2,1,0:T(8,128)(2,1)} %pack.1), channel_id=1, replica_groups={{0,1,2,3,16,17,18,19,32,33,34,35,48,49,50,51},{4,5,6,7,20,21,22,23,36,3..., dimensions={0} | all-to-all | bytes 2621440 | tf_op jit(solution)/shard_map/all_to_all | solution.py:352
  224.3 0.8 fusion.1
  225.1 1.9 collective-permute-start.7
  227.0 5.1 %collective-permute-start.8 = (bf16[1280,128]{1,0:T(8,128)(2,1)S(1)}, bf16[1280,128]{1,0:T(8,128)(2,1)S(1)}, u32[]{:S(2)}, u32[]{:S(2)}) collective-permute-start(bf16[1280,128]{1,0:T(8,128)(2,1)S(1)} %bitcast.29), channel_id=1, source_target_pairs={{396,0},{397,1},{398,2},{399,3},{412,16},{413,17},{414,18},{415,19... | collective-permute-start | bytes 983048 | tf_op jit(solution)/shard_map/ppermute | solution.py:278
  232.2 1.9 collective-permute-start.6
  234.1 3.1 reduce-scatter.5.cloned.1.call-done
  237.2 1.9 finish_out.1
  239.0 0.2 collective-permute-done.7.refs_5_
  239.3 0.0 copy-start.6
  239.3 6.5 %collective-permute-done.8.refs_6_ = bf16[1280,128]{1,0:T(8,128)(2,1)S(1)} collective-permute-done((bf16[1280,128]{1,0:T(8,128)(2,1)S(1)}, bf16[1280,128]{1,0:T(8,128)(2,1)S(1)}, u32[]{:S(2)}, u32[]{:S(2)}) %collective-permute-start.8) | collective-permute-done | bytes 327712 | tf_op jit(solution)/shard_map/ppermute | solution.py:278
  245.8 0.0 copy-start.7
  245.8 0.0 collective-permute-done.6.refs_4_
  245.8 0.0 copy-start.8
  245.8 0.0 copy-done.6
  245.8 0.7 copy-done.7
  246.5 0.1 copy-done.8
  246.6 3.8 %combine.1 = (bf16[192,1024]{1,0:T(8,128)(2,1)}, bf16[2,192]{1,0:T(2,128)(2,1)}) custom-call(s32[1]{0:T(128)} %bitcast.refs_0_, s32[2,192]{1,0:T(2,128)} %bitcast.35, bf16[2,192]{1,0:T(2,128)(2,1)} %bitcast.37, bf16[1280,128]{1,0:T(8,128)(2,1)} %bitcast.21, bf16[1280,128]{1,0:T(8,128)(2,1)} %copy-done.8, bf16[1280,128]{1,0:T(8,128)(2,1)} %copy-done.6, ...), custom_call_target="tpu_custom_call" | custom-call | tf_op jit(solution)/shard_map/combine/pallas_call | solution.py:357
  250.4 51.5 %reduce-scatter.3.cloned.1.call-done = bf16[1,128,1024]{2,1,0:T(8,128)(2,1)} async-done(((bf16[4,128,1024]{2,1,0:T(8,128)(2,1)}), bf16[1,128,1024]{2,1,0:T(8,128)(2,1)}) %reduce-scatter.3.cloned.1.call-update) | async-done | bytes 262160 | tf_op jit(solution)/shard_map/reduce_scatter | solution.py:299
  301.9 1.9 finish_in.1
Async XLA Ops:
  11.8 75.0 %all-to-all-start = ((bf16[16,576,128]{2,1,0:T(8,128)(2,1)}), bf16[16,576,128]{2,1,0:T(8,128)(2,1)S(1)}, u32[]{:S(2)}, u32[]{:S(2)}) async-start(bf16[16,576,128]{2,1,0:T(8,128)(2,1)} %bitcast.19), calls=%async_computation | async-start | bytes 4718592 | tf_op jit(solution)/shard_map/all_to_all | solution.py:314
  21.3 65.6 %all-gather.4.cloned.1.call-start = ((), (), s32[]{:S(2)}) async-start(), calls=%async_computation.4 | async-start | bytes 1310720 | tf_op jit(solution)/shard_map/all_gather | solution.py:296
  22.0 152.8 %all-gather.6.cloned.1.call-start = ((), (), s32[]{:S(2)}) async-start(), calls=%async_computation.7 | async-start | bytes 1310720 | tf_op jit(solution)/shard_map/all_gather | solution.py:296
  87.8 20.3 %collective-permute-start.1 = (bf16[2304,128]{1,0:T(8,128)(2,1)S(1)}, bf16[2304,128]{1,0:T(8,128)(2,1)S(1)}, u32[]{:S(2)}, u32[]{:S(2)}) collective-permute-start(bf16[2304,128]{1,0:T(8,128)(2,1)S(1)} %bitcast.25), channel_id=1, source_target_pairs={{0,8},{1,9},{2,10},{3,11},{16,24},{17,25},{18,26},{19,27},{32,40},... | collective-permute-start | bytes 1769480 | tf_op jit(solution)/shard_map/ppermute | solution.py:278
  89.7 25.6 %collective-permute-start.2 = (bf16[2304,128]{1,0:T(8,128)(2,1)S(1)}, bf16[2304,128]{1,0:T(8,128)(2,1)S(1)}, u32[]{:S(2)}, u32[]{:S(2)}) collective-permute-start(bf16[2304,128]{1,0:T(8,128)(2,1)S(1)} %bitcast.24), channel_id=1, source_target_pairs={{0,396},{1,397},{2,398},{3,399},{16,412},{17,413},{18,414},{19,415... | collective-permute-start | bytes 1769480 | tf_op jit(solution)/shard_map/ppermute | solution.py:278
  92.4 27.0 %collective-permute-start = (bf16[2304,128]{1,0:T(8,128)(2,1)S(1)}, bf16[2304,128]{1,0:T(8,128)(2,1)S(1)}, u32[]{:S(2)}, u32[]{:S(2)}) collective-permute-start(bf16[2304,128]{1,0:T(8,128)(2,1)S(1)} %bitcast.23), channel_id=1, source_target_pairs={{0,4},{1,5},{2,6},{3,7},{16,20},{17,21},{18,22},{19,23},{32,36},{3... | collective-permute-start | bytes 1769480 | tf_op jit(solution)/shard_map/ppermute | solution.py:278
  108.1 11.4 %copy-start.3 = (bf16[2304,128]{1,0:T(8,128)(2,1)}, bf16[2304,128]{1,0:T(8,128)(2,1)S(1)}, u32[]{:S(2)}) copy-start(bf16[2304,128]{1,0:T(8,128)(2,1)S(1)} %collective-permute-done.1.r2) | copy-start | bytes 1769476
  115.3 4.1 %copy-start.4 = (bf16[2304,128]{1,0:T(8,128)(2,1)}, bf16[2304,128]{1,0:T(8,128)(2,1)S(1)}, u32[]{:S(2)}) copy-start(bf16[2304,128]{1,0:T(8,128)(2,1)S(1)} %collective-permute-done.2.r3) | copy-start | bytes 1769476
  119.4 0.8 copy-start.5
  119.4 117.8 %reduce-scatter.5.cloned.1.call-start = ((), (), s32[]{:S(2)}) async-start(), calls=%async_computation.6 | async-start | bytes 1310720 | tf_op jit(solution)/shard_map/reduce_scatter | solution.py:299
  125.6 4.9 %collective-permute-start.3 = (bf16[576,1024]{1,0:T(8,128)(2,1)}, bf16[576,1024]{1,0:T(8,128)(2,1)S(1)}, u32[]{:S(2)}, u32[]{:S(2)}) collective-permute-start(bf16[576,1024]{1,0:T(8,128)(2,1)} %get-tuple-element.32.xm_ref), channel_id=1, source_target_pairs={{0,64},{64,0},{128,192},{192,128},{256,320},{320,256},{384,448},{4... | collective-permute-start | bytes 3538952 | tf_op jit(solution)/shard_map/ppermute | solution.py:288
  127.6 5.1 %collective-permute-start.4 = (bf16[576,1024]{1,0:T(8,128)(2,1)}, bf16[576,1024]{1,0:T(8,128)(2,1)S(1)}, u32[]{:S(2)}, u32[]{:S(2)}) collective-permute-start(bf16[576,1024]{1,0:T(8,128)(2,1)} %get-tuple-element.33.dym_ref), channel_id=1, source_target_pairs={{0,64},{64,0},{128,192},{192,128},{256,320},{320,256},{384,448},{4... | collective-permute-start | bytes 3538952 | tf_op jit(solution)/shard_map/ppermute | solution.py:288
  130.6 2.1 copy-start
  132.6 1.1 copy-start.1
  141.4 160.4 %reduce-scatter.3.cloned.1.call-start = ((), (), s32[]{:S(2)}) async-start(), calls=%async_computation.5 | async-start | bytes 1310720 | tf_op jit(solution)/shard_map/reduce_scatter | solution.py:299
  187.5 5.2 %collective-permute-start.5 = (bf16[576,1152]{1,0:T(8,128)(2,1)}, bf16[576,1152]{1,0:T(8,128)(2,1)S(1)}, u32[]{:S(2)}, u32[]{:S(2)}) collective-permute-start(bf16[576,1152]{1,0:T(8,128)(2,1)} %get-tuple-element.42), channel_id=1, source_target_pairs={{0,64},{64,0},{128,192},{192,128},{256,320},{320,256},{384,448},{4... | collective-permute-start | bytes 3981320 | tf_op jit(solution)/shard_map/ppermute | solution.py:288
  192.7 1.1 copy-start.2
  225.1 14.1 %collective-permute-start.7 = (bf16[1280,128]{1,0:T(8,128)(2,1)S(1)}, bf16[1280,128]{1,0:T(8,128)(2,1)S(1)}, u32[]{:S(2)}, u32[]{:S(2)}) collective-permute-start(bf16[1280,128]{1,0:T(8,128)(2,1)S(1)} %bitcast.30), channel_id=1, source_target_pairs={{8,0},{9,1},{10,2},{11,3},{24,16},{25,17},{26,18},{27,19},{40,32},... | collective-permute-start | bytes 983048 | tf_op jit(solution)/shard_map/ppermute | solution.py:278
  227.0 18.8 %collective-permute-start.8 = (bf16[1280,128]{1,0:T(8,128)(2,1)S(1)}, bf16[1280,128]{1,0:T(8,128)(2,1)S(1)}, u32[]{:S(2)}, u32[]{:S(2)}) collective-permute-start(bf16[1280,128]{1,0:T(8,128)(2,1)S(1)} %bitcast.29), channel_id=1, source_target_pairs={{396,0},{397,1},{398,2},{399,3},{412,16},{413,17},{414,18},{415,19... | collective-permute-start | bytes 983048 | tf_op jit(solution)/shard_map/ppermute | solution.py:278
  232.2 13.6 %collective-permute-start.6 = (bf16[1280,128]{1,0:T(8,128)(2,1)S(1)}, bf16[1280,128]{1,0:T(8,128)(2,1)S(1)}, u32[]{:S(2)}, u32[]{:S(2)}) collective-permute-start(bf16[1280,128]{1,0:T(8,128)(2,1)S(1)} %bitcast.28), channel_id=1, source_target_pairs={{4,0},{5,1},{6,2},{7,3},{20,16},{21,17},{22,18},{23,19},{36,32},{3... | collective-permute-start | bytes 983048 | tf_op jit(solution)/shard_map/ppermute | solution.py:278
  239.3 6.5 %copy-start.6 = (bf16[1280,128]{1,0:T(8,128)(2,1)}, bf16[1280,128]{1,0:T(8,128)(2,1)S(1)}, u32[]{:S(2)}) copy-start(bf16[1280,128]{1,0:T(8,128)(2,1)S(1)} %collective-permute-done.7.refs_5_) | copy-start | bytes 983044
  245.8 0.7 copy-start.7
  245.8 0.9 copy-start.8
Sparse Core Ops, SparseCore 0:
  24.2 62.5 all-gather.3
  119.5 55.2 all-gather.5
  177.6 59.4 reduce-scatter.4
  240.1 61.7 reduce-scatter.2

commit v7 on v5

--- a/solution.py
+++ b/solution.py
@@ -13,8 +13,7 @@
 VMEM_BYTES = 56 << 20
 
 
-def call(body, out_shape, name, scratch=(), scalars=0, arrays=0):
-    specs = {}
+def call(body, out_shape, name, scratch=(), scalars=0, arrays=0, **specs):
     if scalars:
         specs["in_specs"] = [pl.BlockSpec(memory_space=pltpu.SMEM)] * scalars + [
             pl.BlockSpec(memory_space=pltpu.VMEM)
@@ -86,36 +85,41 @@
     return value, slope
 
 
-def unpack_body(r0, r1, r2, r3, rows_ref, wide_ref):
-    slots, width = rows_ref.shape
+def unpack_body(capacity, got_ref, r0, r1, r2, r3, wide_ref):
+    slots, width = r0.shape
+    places = slots // capacity
     tiles = width // LANES
+    step = 4 * capacity * tiles
+    wide_ref[...] = got_ref[...].astype(f32)
     for i, ref in enumerate((r0, r1, r2, r3)):
-        part = ref.shape[0]
-        wide_ref[i * part : (i + 1) * part] = ref[...].astype(f32)
-    for j in range(tiles):
-        rows_ref[:, j * LANES : (j + 1) * LANES] = wide_ref[
-            pl.ds(j, slots, stride=tiles), :
-        ].astype(bf16)
+        for c in range(capacity):
+            for j in range(tiles):
+                start = (i * capacity + c) * tiles + j
+                ref[c * places : (c + 1) * places, j * LANES : (j + 1) * LANES] = wide_ref[
+                    pl.ds(start, places, stride=step), :
+                ].astype(bf16)
 
 
 def project(rows_ref, w_ref, dpre_ref, act_ref, gate_ref):
     width = rows_ref.shape[1] // 2
-    x = rows_ref[:, :width]
-    dy = rows_ref[:, width:]
-    gates = []
-    for pair in range(0, w_ref.shape[0], 2):
-        cols = slice(pair * LANES, (pair + 2) * LANES)
-        w_first = jnp.concatenate([w_ref[pair, :width], w_ref[pair + 1, :width]], axis=1)
-        w_second = jnp.concatenate([w_ref[pair, width:], w_ref[pair + 1, width:]], axis=1)
-        pre = jnp.dot(x, w_first, preferred_element_type=f32)
-        dy_proj = jnp.dot(dy, w_second, preferred_element_type=f32)
-        value, slope = gelu_parts(pre)
-        activated = value.astype(bf16)
-        gate = activated.astype(f32) * dy_proj
-        gates += [gate[:, :LANES], gate[:, LANES:]]
-        dpre_ref[:, cols] = (dy_proj * slope).astype(bf16)
-        act_ref[:, cols] = activated
-    gate_ref[...] = sum(gates[1:], gates[0])
+    w_first = jnp.concatenate([w_ref[0, :width], w_ref[1, :width]], axis=1)
+    w_second = jnp.concatenate([w_ref[0, width:], w_ref[1, width:]], axis=1)
+    pre = jnp.dot(rows_ref[:, :width], w_first, preferred_element_type=f32)
+    dy_proj = jnp.dot(rows_ref[:, width:], w_second, preferred_element_type=f32)
+    value, slope = gelu_parts(pre)
+    activated = value.astype(bf16)
+    gate = activated.astype(f32) * dy_proj
+    dpre_ref[...] = (dy_proj * slope).astype(bf16)
+    act_ref[...] = activated
+    lanes = gate[:, :LANES] + gate[:, LANES:]
+
+    @pl.when(pl.program_id(0) == 0)
+    def _():
+        gate_ref[...] = lanes
+
+    @pl.when(pl.program_id(0) > 0)
+    def _():
+        gate_ref[...] += lanes
 
 
 def other_body(
@@ -123,23 +127,16 @@
 ):
     width = mine_ref.shape[1] // 2
     project(other_ref, w_ref, dpre_ref, act_ref, gate_ref)
-    for row, sides in (
-        (0, ((dpre_in_ref, mine_ref), (dpre_ref, other_ref))),
-        (LANES, ((act_in_ref, mine_ref), (act_ref, other_ref))),
+    dims = (((0,), (0,)), ((), ()))
+    for row, ours, theirs, cols in (
+        (0, dpre_in_ref, dpre_ref, slice(0, width)),
+        (LANES, act_in_ref, act_ref, slice(width, 2 * width)),
     ):
-        for pair in range(0, w_ref.shape[0], 2):
-            cols = slice(pair * LANES, (pair + 2) * LANES)
-            grad = sum(
-                lax.dot_general(
-                    left[:, cols],
-                    right[:, width:] if row else right[:, :width],
-                    (((0,), (0,)), ((), ())),
-                    preferred_element_type=f32,
-                )
-                for left, right in sides
-            ).astype(bf16)
-            grad_ref[pair, row : row + LANES] = grad[:LANES]
-            grad_ref[pair + 1, row : row + LANES] = grad[LANES:]
+        grad = lax.dot_general(ours[...], mine_ref[:, cols], dims, preferred_element_type=f32)
+        grad += lax.dot_general(theirs[...], other_ref[:, cols], dims, preferred_element_type=f32)
+        grad = grad.astype(bf16)
+        grad_ref[0, row : row + LANES] = grad[:LANES]
+        grad_ref[1, row : row + LANES] = grad[LANES:]
 
 
 def dx_body(dpre_m, dpre_o, w_ref, gate_m, gate_o, keep_ref, keep_gate_ref, give_ref):
@@ -171,27 +168,27 @@
         total = keep_ref[:, cols] + took_ref[:, cols].astype(f32)
         rows_ref[j] = total.astype(bf16).astype(f32)
     gate = keep_gate_ref[:, 0:1] + jnp.sum(took_ref[:, width:].astype(f32), axis=1, keepdims=True)
+    places = out_ref.shape[0]
+    planes = experts // places
     row = lax.broadcasted_iota(jnp.int32, (slots, LANES), 0)
     lane = lax.broadcasted_iota(jnp.int32, (slots, LANES), 1)
-    spread = jnp.where(row % capacity == lane, gate, 0.0).astype(bf16)
-    expert = lax.broadcasted_iota(jnp.int32, (experts, slots), 0)
+    spread = jnp.where((row // places) % capacity == lane, gate, 0.0).astype(bf16)
+    block = lax.broadcasted_iota(jnp.int32, (experts, slots), 0)
     slot = lax.broadcasted_iota(jnp.int32, (experts, slots), 1)
-    owner = (slot // capacity == expert).astype(f32).astype(bf16)
-    table = jnp.dot(owner, spread, preferred_element_type=f32)
-    for c in range(capacity):
-        for j in range(tiles):
-            wide_ref[pl.ds(c * tiles + j, experts, stride=step), :] = rows_ref[
-                j, pl.ds(c, experts, stride=capacity), :
-            ]
+    owner = (slot % places * planes + slot // (capacity * places) == block).astype(f32)
+    table = jnp.dot(owner.astype(bf16), spread, preferred_element_type=f32)
+    for i in range(planes):
+        for c in range(capacity):
+            first = (i * capacity + c) * places
+            for j in range(tiles):
+                wide_ref[pl.ds(i * step + c * tiles + j, places, stride=planes * step), :] = (
+                    rows_ref[j, first : first + places, :]
+                )
     for j in range(tiles):
         wide_ref[pl.ds(capacity * tiles + j, experts, stride=step), :] = (
             table if j == 0 else jnp.zeros_like(table)
         )
-    places = out_ref.shape[0]
-    planes = experts // places
-    for i in range(planes):
-        part = wide_ref[i * places * step : (i + 1) * places * step]
-        out_ref[:, i * step : (i + 1) * step] = part.reshape(places, step, LANES).astype(bf16)
+    out_ref[...] = wide_ref[...].reshape(out_ref.shape).astype(bf16)
 
 
 def combine_body(
@@ -305,21 +302,42 @@
         payload.reshape(experts // 4, 4 * chunk, LANES),
         "expert", split_axis=0, concat_axis=0, tiled=True, axis_index_groups=in_plane,
     )
-    got = move(by_plane(got, chunk), out_perms)
-    mine = call(unpack_body, sds((slots, 2 * width), bf16), "unpack", [wide])(*got)
+    got = call(
+        lambda *refs: unpack_body(capacity, *refs),
+        (sds((slots // 4, 2 * width), bf16),) * 4,
+        "unpack",
+        [wide],
+    )(got.reshape(slots * 2 * tiles, LANES))
+    mine = jnp.concatenate(move(list(got), out_perms), axis=0)
     mine, weights = lax.optimization_barrier((mine, weights))
     other = send(mine, swap)
     blocks = replicas // 2
     hidden = sds((slots, blocks * shard), bf16)
     gate_shape = sds((slots, LANES), f32)
-    dpre_mine, act_mine, gate_mine = call(project, (hidden, hidden, gate_shape), "mine")(
-        mine, weights
-    )
+
+    def whole(shape):
+        return pl.BlockSpec(shape, lambda i: (0,) * len(shape))
+
+    all_rows = whole((slots, 2 * width))
+    all_gates = whole((slots, LANES))
+    some_units = pl.BlockSpec((slots, 2 * shard), lambda i: (0, i))
+    some_weights = pl.BlockSpec((2, 2 * width, shard), lambda i: (i, 0, 0))
+    dpre_mine, act_mine, gate_mine = call(
+        project,
+        (hidden, hidden, gate_shape),
+        "mine",
+        grid=(blocks // 2,),
+        in_specs=[all_rows, some_weights],
+        out_specs=(some_units, some_units, all_gates),
+    )(mine, weights)
     dpre_other, gate_other, grads = call(
         other_body,
         (hidden, gate_shape, sds((blocks, 2 * shard, width), bf16)),
         "other",
-        [pltpu.VMEM((slots, blocks * shard), bf16)],
+        [pltpu.VMEM((slots, 2 * shard), bf16)],
+        grid=(blocks // 2,),
+        in_specs=[all_rows, all_rows, some_units, some_units, some_weights],
+        out_specs=(some_units, all_gates, pl.BlockSpec((2, 2 * shard, width), lambda i: (i, 0, 0))),
     )(mine, other, dpre_mine, act_mine, weights)
     total = lax.psum_scatter(
         grads, "dp", scatter_dimension=0, tiled=False, axis_index_groups=same_core

time: 270 us -> 265 us (0.981)
  waiting for transfers between devices: 113 us -> 104 us
    ppermute x6, waiting for transfers between devices: 107 us -> 98.1 us  [move(): lax.ppermute(v, ('dp', 'expert'), perm)]
  transfers between devices with their start and end apart: 10 -> 10, of which waited for: 7 -> 7; matrix products, arithmetic and copies ran while one was open for 1% -> 1% of each run, Pallas kernels for 11% -> 12%
where the time goes in v7:
time: 265 us; the launch traced here: 264 us
  waiting for transfers between devices  104 us (39%)
  blocking collectives  62.1 us (23%)
  Pallas kernels  43 us (16%)
  starting transfers between devices  33.3 us (13%)
  between operations  14.2 us (5%)
  local copies, waits for them, and re-layouts  4.13 us (2%)
  other arithmetic  3.08 us (1%)
    ppermute x6, waiting for transfers between devices, move(): lax.ppermute(v, ('dp', 'expert'), perm)  98.1 us
    all_to_all x1, blocking collectives, shards(): lax.all_to_all(payload.reshape(experts // 4, 4 * chunk, LANES), 'expert',...  36.6 us
    ppermute x6, starting transfers between devices, move(): lax.ppermute(v, ('dp', 'expert'), perm)  28.8 us
    all_to_all x1, blocking collectives, shards(): lax.all_to_all(back, 'expert', split_axis=0, concat_axis=0, tiled=True, a...  25.6 us
    pallas_call x1, Pallas kernels, shards(): call(other_body, (hidden, gate_shape, sds((blocks, 2 * shard, width), bf1...  9.99 us
    pallas_call x1, Pallas kernels, shards(): call(lambda *refs: pack_body(experts, capacity, *refs), sds((experts // 4...  5.97 us
    pallas_call x1, Pallas kernels, shards(): call(lambda *refs: unpack_body(capacity, *refs), (sds((slots // 4, 2 * wi...  5.94 us
    pallas_call x1, Pallas kernels, shards(): call(dx_body, (sds((slots, width), f32), sds((slots, LANES), f32), sds((s...  5.3 us
  transfers between devices with their start and end apart: 10, of which 7 were waited for; matrix products, arithmetic and copies ran while one was open for 1% of the time, Pallas kernels for 12%

profile of v7, /device:TPU:6, one launch (start us, length us, event | category | flops | bytes accessed | tf_op | source)
XLA Modules:
  0.0 263.7 jit_solution(15873242393336619694)
XLA Ops:
  7.2 0.0 all-gather.3.cloned.1.call-start
  7.2 1.9 pad_maximum_fusion.1
  9.1 0.0 all-gather.3.cloned.1.call-update
  9.1 0.0 reduce-scatter.2.cloned.1.call-start
  9.1 4.7 %dispatch.1 = bf16[9216,128]{1,0:T(8,128)(2,1)} custom-call(s32[1]{0:T(128)} %bitcast.refs_0_, s32[2,192]{1,0:T(2,128)} %bitcast.28, bf16[2,192]{1,0:T(2,128)(2,1)} %bitcast.30, bf16[192,1024]{1,0:T(8,128)(2,1)} %refs_3_.1, bf16[192,1024]{1,0:T(8,128)(2,1)} %refs_4_.1), custom_call_target="tpu_custom_call" | custom-call | tf_op jit(solution)/shard_map/dispatch/pallas_call | solution.py:293
  13.8 36.6 %all_to_all.10 = bf16[16,576,128]{2,1,0:T(8,128)(2,1)} all-to-all(bf16[16,576,128]{2,1,0:T(8,128)(2,1)} %bitcast.20), channel_id=1, replica_groups={{0,1,2,3,16,17,18,19,32,33,34,35,48,49,50,51},{4,5,6,7,20,21,22,23,36,3..., dimensions={0} | all-to-all | bytes 4718592 | tf_op jit(solution)/shard_map/all_to_all | solution.py:301
  50.4 5.9 %unpack.1 = (bf16[144,2048]{1,0:T(8,128)(2,1)}, bf16[144,2048]{1,0:T(8,128)(2,1)}, bf16[144,2048]{1,0:T(8,128)(2,1)}, bf16[144,2048]{1,0:T(8,128)(2,1)}) custom-call(bf16[9216,128]{1,0:T(8,128)(2,1)} %bitcast.19), custom_call_target="tpu_custom_call" | custom-call | tf_op jit(solution)/shard_map/unpack/pallas_call | solution.py:305
  56.3 3.9 %collective-permute-start = (bf16[144,2048]{1,0:T(8,128)(2,1)}, bf16[144,2048]{1,0:T(8,128)(2,1)S(1)}, u32[]{:S(2)}, u32[]{:S(2)}) collective-permute-start(bf16[144,2048]{1,0:T(8,128)(2,1)} %get-tuple-element.27), channel_id=1, source_target_pairs={{0,4},{1,5},{2,6},{3,7},{16,20},{17,21},{18,22},{19,23},{32,36},{3... | collective-permute-start | bytes 1769480 | tf_op jit(solution)/shard_map/ppermute | solution.py:270
  60.2 5.2 %collective-permute-start.1 = (bf16[144,2048]{1,0:T(8,128)(2,1)}, bf16[144,2048]{1,0:T(8,128)(2,1)S(1)}, u32[]{:S(2)}, u32[]{:S(2)}) collective-permute-start(bf16[144,2048]{1,0:T(8,128)(2,1)} %get-tuple-element.28), channel_id=1, source_target_pairs={{0,8},{1,9},{2,10},{3,11},{16,24},{17,25},{18,26},{19,27},{32,40},... | collective-permute-start | bytes 1769480 | tf_op jit(solution)/shard_map/ppermute | solution.py:270
  65.4 8.7 %collective-permute-start.2 = (bf16[144,2048]{1,0:T(8,128)(2,1)}, bf16[144,2048]{1,0:T(8,128)(2,1)S(1)}, u32[]{:S(2)}, u32[]{:S(2)}) collective-permute-start(bf16[144,2048]{1,0:T(8,128)(2,1)} %get-tuple-element.29), channel_id=1, source_target_pairs={{0,396},{1,397},{2,398},{3,399},{16,412},{17,413},{18,414},{19,415... | collective-permute-start | bytes 1769480 | tf_op jit(solution)/shard_map/ppermute | solution.py:270
  74.1 42.7 %collective-permute-done = bf16[144,2048]{1,0:T(8,128)(2,1)S(1)} collective-permute-done((bf16[144,2048]{1,0:T(8,128)(2,1)}, bf16[144,2048]{1,0:T(8,128)(2,1)S(1)}, u32[]{:S(2)}, u32[]{:S(2)}) %collective-permute-start) | collective-permute-done | bytes 589856 | tf_op jit(solution)/shard_map/ppermute | solution.py:270
  116.8 14.5 %collective-permute-done.1 = bf16[144,2048]{1,0:T(8,128)(2,1)S(1)} collective-permute-done((bf16[144,2048]{1,0:T(8,128)(2,1)}, bf16[144,2048]{1,0:T(8,128)(2,1)S(1)}, u32[]{:S(2)}, u32[]{:S(2)}) %collective-permute-start.1) | collective-permute-done | bytes 589856 | tf_op jit(solution)/shard_map/ppermute | solution.py:270
  131.3 0.0 collective-permute-done.2
  131.3 1.2 pad_maximum_fusion.rows_ref.mine_ref
  132.6 0.0 copy-start
  132.6 0.2 all-gather.3.cloned.1.call-done
  132.8 1.9 collective-permute-start.3
  134.7 0.0 copy-done
  134.7 5.2 %mine.1 = (bf16[576,512]{1,0:T(8,128)(2,1)}, bf16[576,512]{1,0:T(8,128)(2,1)}, f32[576,128]{1,0:T(8,128)}) custom-call(bf16[576,2048]{1,0:T(8,128)(2,1)} %copy-done, bf16[4,2048,128]{2,1,0:T(8,128)(2,1)} %bitcast.16), custom_call_target="tpu_custom_call" | custom-call | tf_op jit(solution)/shard_map/mine/pallas_call | solution.py:325
  140.0 0.0 collective-permute-done.3.other_ref
  140.0 0.0 copy-start.1
  140.0 1.4 copy-done.1
  141.4 10.0 %other.1 = (bf16[576,512]{1,0:T(8,128)(2,1)}, f32[576,128]{1,0:T(8,128)}, bf16[4,256,1024]{2,1,0:T(8,128)(2,1)}) custom-call(bf16[576,2048]{1,0:T(8,128)(2,1)} %copy-done, bf16[576,2048]{1,0:T(8,128)(2,1)} %copy-done.1, bf16[576,512]{1,0:T(8,128)(2,1)} %get-tuple-element.32.dpre_in_ref.dpre_m, bf16[576,512]{1,0:T(8,128)(2,1)} %get-tuple-element.33.act_in_ref, ...), custom_call_target="tpu_custom_call" | custom-call | tf_op jit(solution)/shard_map/other/pallas_call | solution.py:333
  151.4 0.0 reduce-scatter.2.cloned.1.call-update
  151.4 5.3 %input_gradient.1 = (f32[576,1024]{1,0:T(8,128)}, f32[576,128]{1,0:T(8,128)}, bf16[576,1152]{1,0:T(8,128)(2,1)}) custom-call(bf16[576,512]{1,0:T(8,128)(2,1)} %get-tuple-element.32.dpre_in_ref.dpre_m, bf16[576,512]{1,0:T(8,128)(2,1)} %get-tuple-element.34.dpre_o, bf16[4,2048,128]{2,1,0:T(8,128)(2,1)} %bitcast.18, f32[576,128]{1,0:T(8,128)} %get-tuple-element.35.gate_m, ...), custom_call_target="tpu_custom_call" | custom-call | tf_op jit(solution)/shard_map/input_gradient/pallas_call | solution.py:345
  156.7 2.6 collective-permute-start.4
  159.3 2.7 %collective-permute-done.4.refs_2_ = bf16[576,1152]{1,0:T(8,128)(2,1)S(1)} collective-permute-done((bf16[576,1152]{1,0:T(8,128)(2,1)}, bf16[576,1152]{1,0:T(8,128)(2,1)S(1)}, u32[]{:S(2)}, u32[]{:S(2)}) %collective-permute-start.4) | collective-permute-done | bytes 1327136 | tf_op jit(solution)/shard_map/ppermute | solution.py:280
  162.0 0.0 copy-start.2
  162.0 1.1 copy-done.2
  163.1 6.0 %pack.1 = bf16[16,320,128]{2,1,0:T(8,128)(2,1)} custom-call(f32[576,1024]{1,0:T(8,128)} %get-tuple-element.37.refs_0_, f32[576,128]{1,0:T(8,128)} %get-tuple-element.38.refs_1_, bf16[576,1152]{1,0:T(8,128)(2,1)} %copy-done.2), custom_call_target="tpu_custom_call" | custom-call | tf_op jit(solution)/shard_map/pack/pallas_call | solution.py:351
  169.1 25.6 %all_to_all.11 = bf16[16,320,128]{2,1,0:T(8,128)(2,1)S(1)} all-to-all(bf16[16,320,128]{2,1,0:T(8,128)(2,1)} %pack.1), channel_id=1, replica_groups={{0,1,2,3,16,17,18,19,32,33,34,35,48,49,50,51},{4,5,6,7,20,21,22,23,36,3..., dimensions={0} | all-to-all | bytes 2621440 | tf_op jit(solution)/shard_map/all_to_all | solution.py:361
  194.6 0.8 fusion
  195.4 4.0 %collective-permute-start.6 = (bf16[1280,128]{1,0:T(8,128)(2,1)S(1)}, bf16[1280,128]{1,0:T(8,128)(2,1)S(1)}, u32[]{:S(2)}, u32[]{:S(2)}) collective-permute-start(bf16[1280,128]{1,0:T(8,128)(2,1)S(1)} %bitcast.25), channel_id=1, source_target_pairs={{8,0},{9,1},{10,2},{11,3},{24,16},{25,17},{26,18},{27,19},{40,32},... | collective-permute-start | bytes 983048 | tf_op jit(solution)/shard_map/ppermute | solution.py:270
  199.4 1.9 collective-permute-start.7
  201.3 5.1 %collective-permute-start.5 = (bf16[1280,128]{1,0:T(8,128)(2,1)S(1)}, bf16[1280,128]{1,0:T(8,128)(2,1)S(1)}, u32[]{:S(2)}, u32[]{:S(2)}) collective-permute-start(bf16[1280,128]{1,0:T(8,128)(2,1)S(1)} %bitcast.23), channel_id=1, source_target_pairs={{4,0},{5,1},{6,2},{7,3},{20,16},{21,17},{22,18},{23,19},{36,32},{3... | collective-permute-start | bytes 983048 | tf_op jit(solution)/shard_map/ppermute | solution.py:270
  206.5 24.6 %collective-permute-done.6.refs_5_ = bf16[1280,128]{1,0:T(8,128)(2,1)S(1)} collective-permute-done((bf16[1280,128]{1,0:T(8,128)(2,1)S(1)}, bf16[1280,128]{1,0:T(8,128)(2,1)S(1)}, u32[]{:S(2)}, u32[]{:S(2)}) %collective-permute-start.6) | collective-permute-done | bytes 327712 | tf_op jit(solution)/shard_map/ppermute | solution.py:270
  231.0 0.0 copy-start.3
  231.0 16.3 %collective-permute-done.7.refs_6_ = bf16[1280,128]{1,0:T(8,128)(2,1)S(1)} collective-permute-done((bf16[1280,128]{1,0:T(8,128)(2,1)S(1)}, bf16[1280,128]{1,0:T(8,128)(2,1)S(1)}, u32[]{:S(2)}, u32[]{:S(2)}) %collective-permute-start.7) | collective-permute-done | bytes 327712 | tf_op jit(solution)/shard_map/ppermute | solution.py:270
  247.3 0.0 copy-start.4
  247.3 0.0 collective-permute-done.5.refs_4_
  247.3 0.0 copy-start.5
  247.3 0.0 copy-done.3
  247.3 0.7 copy-done.4
  248.0 0.1 copy-done.5
  248.1 3.8 %combine.1 = (bf16[192,1024]{1,0:T(8,128)(2,1)}, bf16[2,192]{1,0:T(2,128)(2,1)}) custom-call(s32[1]{0:T(128)} %bitcast.refs_0_, s32[2,192]{1,0:T(2,128)} %bitcast.29, bf16[2,192]{1,0:T(2,128)(2,1)} %bitcast.31, bf16[1280,128]{1,0:T(8,128)(2,1)} %bitcast.21, bf16[1280,128]{1,0:T(8,128)(2,1)} %copy-done.5, bf16[1280,128]{1,0:T(8,128)(2,1)} %copy-done.3, ...), custom_call_target="tpu_custom_call" | custom-call | tf_op jit(solution)/shard_map/combine/pallas_call | solution.py:366
  251.9 2.9 %reduce-scatter.2.cloned.1.call-done = bf16[1,256,1024]{2,1,0:T(8,128)(2,1)} async-done(((bf16[4,256,1024]{2,1,0:T(8,128)(2,1)}), bf16[1,256,1024]{2,1,0:T(8,128)(2,1)}) %reduce-scatter.2.cloned.1.call-update) | async-done | bytes 524304 | tf_op jit(solution)/shard_map/reduce_scatter | solution.py:342
  254.7 2.1 finish.1
Async XLA Ops:
  7.2 125.7 %all-gather.3.cloned.1.call-start = ((), (), s32[]{:S(2)}) async-start(), calls=%async_computation.4 | async-start | bytes 2621440 | tf_op jit(solution)/shard_map/all_gather | solution.py:287
  9.1 245.6 %reduce-scatter.2.cloned.1.call-start = ((), (), s32[]{:S(2)}) async-start(), calls=%async_computation.3 | async-start | bytes 2621440 | tf_op jit(solution)/shard_map/reduce_scatter | solution.py:342
  56.3 60.5 %collective-permute-start = (bf16[144,2048]{1,0:T(8,128)(2,1)}, bf16[144,2048]{1,0:T(8,128)(2,1)S(1)}, u32[]{:S(2)}, u32[]{:S(2)}) collective-permute-start(bf16[144,2048]{1,0:T(8,128)(2,1)} %get-tuple-element.27), channel_id=1, source_target_pairs={{0,4},{1,5},{2,6},{3,7},{16,20},{17,21},{18,22},{19,23},{32,36},{3... | collective-permute-start | bytes 1769480 | tf_op jit(solution)/shard_map/ppermute | solution.py:270
  60.2 71.1 %collective-permute-start.1 = (bf16[144,2048]{1,0:T(8,128)(2,1)}, bf16[144,2048]{1,0:T(8,128)(2,1)S(1)}, u32[]{:S(2)}, u32[]{:S(2)}) collective-permute-start(bf16[144,2048]{1,0:T(8,128)(2,1)} %get-tuple-element.28), channel_id=1, source_target_pairs={{0,8},{1,9},{2,10},{3,11},{16,24},{17,25},{18,26},{19,27},{32,40},... | collective-permute-start | bytes 1769480 | tf_op jit(solution)/shard_map/ppermute | solution.py:270
  65.4 65.9 %collective-permute-start.2 = (bf16[144,2048]{1,0:T(8,128)(2,1)}, bf16[144,2048]{1,0:T(8,128)(2,1)S(1)}, u32[]{:S(2)}, u32[]{:S(2)}) collective-permute-start(bf16[144,2048]{1,0:T(8,128)(2,1)} %get-tuple-element.29), channel_id=1, source_target_pairs={{0,396},{1,397},{2,398},{3,399},{16,412},{17,413},{18,414},{19,415... | collective-permute-start | bytes 1769480 | tf_op jit(solution)/shard_map/ppermute | solution.py:270
  132.6 2.2 copy-start
  132.8 7.2 %collective-permute-start.3 = (bf16[576,2048]{1,0:T(8,128)(2,1)S(1)}, bf16[576,2048]{1,0:T(8,128)(2,1)S(1)}, u32[]{:S(2)}, u32[]{:S(2)}) collective-permute-start(bf16[576,2048]{1,0:T(8,128)(2,1)S(1)} %pad_maximum_fusion.rows_ref.mine_ref), channel_id=1, source_target_pairs={{0,64},{64,0},{128,192},{192,128},{256,320},{320,256},{384,448},{4... | collective-permute-start | bytes 7077896 | tf_op jit(solution)/shard_map/ppermute | solution.py:280
  140.0 1.4 copy-start.1
  156.7 5.3 %collective-permute-start.4 = (bf16[576,1152]{1,0:T(8,128)(2,1)}, bf16[576,1152]{1,0:T(8,128)(2,1)S(1)}, u32[]{:S(2)}, u32[]{:S(2)}) collective-permute-start(bf16[576,1152]{1,0:T(8,128)(2,1)} %get-tuple-element.39), channel_id=1, source_target_pairs={{0,64},{64,0},{128,192},{192,128},{256,320},{320,256},{384,448},{4... | collective-permute-start | bytes 3981320 | tf_op jit(solution)/shard_map/ppermute | solution.py:280
  162.0 1.1 copy-start.2
  195.4 35.6 %collective-permute-start.6 = (bf16[1280,128]{1,0:T(8,128)(2,1)S(1)}, bf16[1280,128]{1,0:T(8,128)(2,1)S(1)}, u32[]{:S(2)}, u32[]{:S(2)}) collective-permute-start(bf16[1280,128]{1,0:T(8,128)(2,1)S(1)} %bitcast.25), channel_id=1, source_target_pairs={{8,0},{9,1},{10,2},{11,3},{24,16},{25,17},{26,18},{27,19},{40,32},... | collective-permute-start | bytes 983048 | tf_op jit(solution)/shard_map/ppermute | solution.py:270
  199.4 47.9 %collective-permute-start.7 = (bf16[1280,128]{1,0:T(8,128)(2,1)S(1)}, bf16[1280,128]{1,0:T(8,128)(2,1)S(1)}, u32[]{:S(2)}, u32[]{:S(2)}) collective-permute-start(bf16[1280,128]{1,0:T(8,128)(2,1)S(1)} %bitcast.24), channel_id=1, source_target_pairs={{396,0},{397,1},{398,2},{399,3},{412,16},{413,17},{414,18},{415,19... | collective-permute-start | bytes 983048 | tf_op jit(solution)/shard_map/ppermute | solution.py:270
  201.3 46.0 %collective-permute-start.5 = (bf16[1280,128]{1,0:T(8,128)(2,1)S(1)}, bf16[1280,128]{1,0:T(8,128)(2,1)S(1)}, u32[]{:S(2)}, u32[]{:S(2)}) collective-permute-start(bf16[1280,128]{1,0:T(8,128)(2,1)S(1)} %bitcast.23), channel_id=1, source_target_pairs={{4,0},{5,1},{6,2},{7,3},{20,16},{21,17},{22,18},{23,19},{36,32},{3... | collective-permute-start | bytes 983048 | tf_op jit(solution)/shard_map/ppermute | solution.py:270
  231.0 16.3 %copy-start.3 = (bf16[1280,128]{1,0:T(8,128)(2,1)}, bf16[1280,128]{1,0:T(8,128)(2,1)S(1)}, u32[]{:S(2)}) copy-start(bf16[1280,128]{1,0:T(8,128)(2,1)S(1)} %collective-permute-done.6.refs_5_) | copy-start | bytes 983044
  247.3 0.7 copy-start.4
  247.3 0.8 copy-start.5
Sparse Core Ops, SparseCore 0:
  10.7 122.0 all-gather.2
  151.6 103.1 reduce-scatter.1

commit v8 on v7

--- a/solution.py
+++ b/solution.py
@@ -104,22 +104,19 @@
     width = rows_ref.shape[1] // 2
     w_first = jnp.concatenate([w_ref[0, :width], w_ref[1, :width]], axis=1)
     w_second = jnp.concatenate([w_ref[0, width:], w_ref[1, width:]], axis=1)
-    pre = jnp.dot(rows_ref[:, :width], w_first, preferred_element_type=f32)
-    dy_proj = jnp.dot(rows_ref[:, width:], w_second, preferred_element_type=f32)
-    value, slope = gelu_parts(pre)
-    activated = value.astype(bf16)
-    gate = activated.astype(f32) * dy_proj
-    dpre_ref[...] = (dy_proj * slope).astype(bf16)
-    act_ref[...] = activated
-    lanes = gate[:, :LANES] + gate[:, LANES:]
-
-    @pl.when(pl.program_id(0) == 0)
-    def _():
-        gate_ref[...] = lanes
-
-    @pl.when(pl.program_id(0) > 0)
-    def _():
-        gate_ref[...] += lanes
+    first_step = pl.program_id(0) == 0
+    chunk = rows_ref.shape[0] // 3
+    for start in range(0, rows_ref.shape[0], chunk):
+        rows = slice(start, start + chunk)
+        pre = jnp.dot(rows_ref[rows, :width], w_first, preferred_element_type=f32)
+        dy_proj = jnp.dot(rows_ref[rows, width:], w_second, preferred_element_type=f32)
+        value, slope = gelu_parts(pre)
+        activated = value.astype(bf16)
+        gate = activated.astype(f32) * dy_proj
+        dpre_ref[rows] = (dy_proj * slope).astype(bf16)
+        act_ref[rows] = activated
+        before = jnp.where(first_step, 0.0, gate_ref[rows])
+        gate_ref[rows] = before + gate[:, :LANES] + gate[:, LANES:]
 
 
 def other_body(

time: 265 us -> 264 us (level)
  no operation moved by 1% of the time
where the time goes in v8:
time: 264 us
  waiting for transfers between devices  104 us (39%)
  blocking collectives  62.1 us (24%)
  Pallas kernels  42.9 us (16%)
  starting transfers between devices  33.3 us (13%)
  between operations  14.1 us (5%)
  local copies, waits for them, and re-layouts  4.13 us (2%)
  other arithmetic  3.08 us (1%)
    ppermute x6, waiting for transfers between devices, move(): lax.ppermute(v, ('dp', 'expert'), perm)  97.8 us
    all_to_all x1, blocking collectives, shards(): lax.all_to_all(payload.reshape(experts // 4, 4 * chunk, LANES), 'expert',...  36.6 us
    ppermute x6, starting transfers between devices, move(): lax.ppermute(v, ('dp', 'expert'), perm)  28.8 us
    all_to_all x1, blocking collectives, shards(): lax.all_to_all(back, 'expert', split_axis=0, concat_axis=0, tiled=True, a...  25.5 us
    pallas_call x1, Pallas kernels, shards(): call(other_body, (hidden, gate_shape, sds((blocks, 2 * shard, width), bf1...  9.78 us
    pallas_call x1, Pallas kernels, shards(): call(lambda *refs: pack_body(experts, capacity, *refs), sds((experts // 4...  5.98 us
    pallas_call x1, Pallas kernels, shards(): call(lambda *refs: unpack_body(capacity, *refs), (sds((slots // 4, 2 * wi...  5.94 us
    pallas_call x1, Pallas kernels, shards(): call(project, (hidden, hidden, gate_shape), 'mine', grid=(blocks // 2,),...  5.31 us
  transfers between devices with their start and end apart: 10, of which 7 were waited for; matrix products, arithmetic and copies ran while one was open for 1% of the time, Pallas kernels for 12%

profile of v8, /device:TPU:6, one launch (start us, length us, event | category | flops | bytes accessed | tf_op | source)
XLA Modules:
  0.0 263.5 jit_solution(4416167412309265430)
XLA Ops:
  7.2 0.0 all-gather.3.cloned.1.call-start
  7.2 1.9 pad_maximum_fusion.1
  9.1 0.0 all-gather.3.cloned.1.call-update
  9.1 0.0 reduce-scatter.2.cloned.1.call-start
  9.1 4.7 %dispatch.1 = bf16[9216,128]{1,0:T(8,128)(2,1)} custom-call(s32[1]{0:T(128)} %bitcast.refs_0_, s32[2,192]{1,0:T(2,128)} %bitcast.28, bf16[2,192]{1,0:T(2,128)(2,1)} %bitcast.30, bf16[192,1024]{1,0:T(8,128)(2,1)} %refs_3_.1, bf16[192,1024]{1,0:T(8,128)(2,1)} %refs_4_.1), custom_call_target="tpu_custom_call" | custom-call | tf_op jit(solution)/shard_map/dispatch/pallas_call | solution.py:290
  13.8 36.6 %all_to_all.10 = bf16[16,576,128]{2,1,0:T(8,128)(2,1)} all-to-all(bf16[16,576,128]{2,1,0:T(8,128)(2,1)} %bitcast.20), channel_id=1, replica_groups={{0,1,2,3,16,17,18,19,32,33,34,35,48,49,50,51},{4,5,6,7,20,21,22,23,36,3..., dimensions={0} | all-to-all | bytes 4718592 | tf_op jit(solution)/shard_map/all_to_all | solution.py:298
  50.4 5.9 %unpack.1 = (bf16[144,2048]{1,0:T(8,128)(2,1)}, bf16[144,2048]{1,0:T(8,128)(2,1)}, bf16[144,2048]{1,0:T(8,128)(2,1)}, bf16[144,2048]{1,0:T(8,128)(2,1)}) custom-call(bf16[9216,128]{1,0:T(8,128)(2,1)} %bitcast.19), custom_call_target="tpu_custom_call" | custom-call | tf_op jit(solution)/shard_map/unpack/pallas_call | solution.py:302
  56.3 3.9 %collective-permute-start = (bf16[144,2048]{1,0:T(8,128)(2,1)}, bf16[144,2048]{1,0:T(8,128)(2,1)S(1)}, u32[]{:S(2)}, u32[]{:S(2)}) collective-permute-start(bf16[144,2048]{1,0:T(8,128)(2,1)} %get-tuple-element.27), channel_id=1, source_target_pairs={{0,4},{1,5},{2,6},{3,7},{16,20},{17,21},{18,22},{19,23},{32,36},{3... | collective-permute-start | bytes 1769480 | tf_op jit(solution)/shard_map/ppermute | solution.py:267
  60.2 5.2 %collective-permute-start.1 = (bf16[144,2048]{1,0:T(8,128)(2,1)}, bf16[144,2048]{1,0:T(8,128)(2,1)S(1)}, u32[]{:S(2)}, u32[]{:S(2)}) collective-permute-start(bf16[144,2048]{1,0:T(8,128)(2,1)} %get-tuple-element.28), channel_id=1, source_target_pairs={{0,8},{1,9},{2,10},{3,11},{16,24},{17,25},{18,26},{19,27},{32,40},... | collective-permute-start | bytes 1769480 | tf_op jit(solution)/shard_map/ppermute | solution.py:267
  65.4 8.7 %collective-permute-start.2 = (bf16[144,2048]{1,0:T(8,128)(2,1)}, bf16[144,2048]{1,0:T(8,128)(2,1)S(1)}, u32[]{:S(2)}, u32[]{:S(2)}) collective-permute-start(bf16[144,2048]{1,0:T(8,128)(2,1)} %get-tuple-element.29), channel_id=1, source_target_pairs={{0,396},{1,397},{2,398},{3,399},{16,412},{17,413},{18,414},{19,415... | collective-permute-start | bytes 1769480 | tf_op jit(solution)/shard_map/ppermute | solution.py:267
  74.1 42.7 %collective-permute-done = bf16[144,2048]{1,0:T(8,128)(2,1)S(1)} collective-permute-done((bf16[144,2048]{1,0:T(8,128)(2,1)}, bf16[144,2048]{1,0:T(8,128)(2,1)S(1)}, u32[]{:S(2)}, u32[]{:S(2)}) %collective-permute-start) | collective-permute-done | bytes 589856 | tf_op jit(solution)/shard_map/ppermute | solution.py:267
  116.8 14.5 %collective-permute-done.1 = bf16[144,2048]{1,0:T(8,128)(2,1)S(1)} collective-permute-done((bf16[144,2048]{1,0:T(8,128)(2,1)}, bf16[144,2048]{1,0:T(8,128)(2,1)S(1)}, u32[]{:S(2)}, u32[]{:S(2)}) %collective-permute-start.1) | collective-permute-done | bytes 589856 | tf_op jit(solution)/shard_map/ppermute | solution.py:267
  131.3 0.0 collective-permute-done.2
  131.3 1.2 pad_maximum_fusion.rows_ref.mine_ref
  132.6 0.0 copy-start
  132.6 0.2 all-gather.3.cloned.1.call-done
  132.8 1.9 collective-permute-start.3
  134.7 0.0 copy-done
  134.7 5.3 %mine.1 = (bf16[576,512]{1,0:T(8,128)(2,1)}, bf16[576,512]{1,0:T(8,128)(2,1)}, f32[576,128]{1,0:T(8,128)}) custom-call(bf16[576,2048]{1,0:T(8,128)(2,1)} %copy-done, bf16[4,2048,128]{2,1,0:T(8,128)(2,1)} %bitcast.16), custom_call_target="tpu_custom_call" | custom-call | tf_op jit(solution)/shard_map/mine/pallas_call | solution.py:322
  140.1 0.0 collective-permute-done.3.other_ref
  140.1 0.0 copy-start.1
  140.1 1.4 copy-done.1
  141.5 9.8 %other.1 = (bf16[576,512]{1,0:T(8,128)(2,1)}, f32[576,128]{1,0:T(8,128)}, bf16[4,256,1024]{2,1,0:T(8,128)(2,1)}) custom-call(bf16[576,2048]{1,0:T(8,128)(2,1)} %copy-done, bf16[576,2048]{1,0:T(8,128)(2,1)} %copy-done.1, bf16[576,512]{1,0:T(8,128)(2,1)} %get-tuple-element.32.dpre_in_ref.dpre_m, bf16[576,512]{1,0:T(8,128)(2,1)} %get-tuple-element.33.act_in_ref, ...), custom_call_target="tpu_custom_call" | custom-call | tf_op jit(solution)/shard_map/other/pallas_call | solution.py:330
  151.3 0.0 reduce-scatter.2.cloned.1.call-update
  151.3 5.3 %input_gradient.1 = (f32[576,1024]{1,0:T(8,128)}, f32[576,128]{1,0:T(8,128)}, bf16[576,1152]{1,0:T(8,128)(2,1)}) custom-call(bf16[576,512]{1,0:T(8,128)(2,1)} %get-tuple-element.32.dpre_in_ref.dpre_m, bf16[576,512]{1,0:T(8,128)(2,1)} %get-tuple-element.34.dpre_o, bf16[4,2048,128]{2,1,0:T(8,128)(2,1)} %bitcast.18, f32[576,128]{1,0:T(8,128)} %get-tuple-element.35.gate_m, ...), custom_call_target="tpu_custom_call" | custom-call | tf_op jit(solution)/shard_map/input_gradient/pallas_call | solution.py:342
  156.6 2.6 collective-permute-start.4
  159.2 2.7 %collective-permute-done.4.refs_2_ = bf16[576,1152]{1,0:T(8,128)(2,1)S(1)} collective-permute-done((bf16[576,1152]{1,0:T(8,128)(2,1)}, bf16[576,1152]{1,0:T(8,128)(2,1)S(1)}, u32[]{:S(2)}, u32[]{:S(2)}) %collective-permute-start.4) | collective-permute-done | bytes 1327136 | tf_op jit(solution)/shard_map/ppermute | solution.py:277
  161.9 0.0 copy-start.2
  161.9 1.1 copy-done.2
  162.9 6.0 %pack.1 = bf16[16,320,128]{2,1,0:T(8,128)(2,1)} custom-call(f32[576,1024]{1,0:T(8,128)} %get-tuple-element.37.refs_0_, f32[576,128]{1,0:T(8,128)} %get-tuple-element.38.refs_1_, bf16[576,1152]{1,0:T(8,128)(2,1)} %copy-done.2), custom_call_target="tpu_custom_call" | custom-call | tf_op jit(solution)/shard_map/pack/pallas_call | solution.py:348
  168.9 25.5 %all_to_all.11 = bf16[16,320,128]{2,1,0:T(8,128)(2,1)S(1)} all-to-all(bf16[16,320,128]{2,1,0:T(8,128)(2,1)} %pack.1), channel_id=1, replica_groups={{0,1,2,3,16,17,18,19,32,33,34,35,48,49,50,51},{4,5,6,7,20,21,22,23,36,3..., dimensions={0} | all-to-all | bytes 2621440 | tf_op jit(solution)/shard_map/all_to_all | solution.py:358
  194.5 0.8 fusion
  195.3 4.0 %collective-permute-start.6 = (bf16[1280,128]{1,0:T(8,128)(2,1)S(1)}, bf16[1280,128]{1,0:T(8,128)(2,1)S(1)}, u32[]{:S(2)}, u32[]{:S(2)}) collective-permute-start(bf16[1280,128]{1,0:T(8,128)(2,1)S(1)} %bitcast.25), channel_id=1, source_target_pairs={{8,0},{9,1},{10,2},{11,3},{24,16},{25,17},{26,18},{27,19},{40,32},... | collective-permute-start | bytes 983048 | tf_op jit(solution)/shard_map/ppermute | solution.py:267
  199.2 1.9 collective-permute-start.7
  201.2 5.1 %collective-permute-start.5 = (bf16[1280,128]{1,0:T(8,128)(2,1)S(1)}, bf16[1280,128]{1,0:T(8,128)(2,1)S(1)}, u32[]{:S(2)}, u32[]{:S(2)}) collective-permute-start(bf16[1280,128]{1,0:T(8,128)(2,1)S(1)} %bitcast.23), channel_id=1, source_target_pairs={{4,0},{5,1},{6,2},{7,3},{20,16},{21,17},{22,18},{23,19},{36,32},{3... | collective-permute-start | bytes 983048 | tf_op jit(solution)/shard_map/ppermute | solution.py:267
  206.3 24.6 %collective-permute-done.6.refs_5_ = bf16[1280,128]{1,0:T(8,128)(2,1)S(1)} collective-permute-done((bf16[1280,128]{1,0:T(8,128)(2,1)S(1)}, bf16[1280,128]{1,0:T(8,128)(2,1)S(1)}, u32[]{:S(2)}, u32[]{:S(2)}) %collective-permute-start.6) | collective-permute-done | bytes 327712 | tf_op jit(solution)/shard_map/ppermute | solution.py:267
  230.9 0.0 copy-start.3
  230.9 16.0 %collective-permute-done.7.refs_6_ = bf16[1280,128]{1,0:T(8,128)(2,1)S(1)} collective-permute-done((bf16[1280,128]{1,0:T(8,128)(2,1)S(1)}, bf16[1280,128]{1,0:T(8,128)(2,1)S(1)}, u32[]{:S(2)}, u32[]{:S(2)}) %collective-permute-start.7) | collective-permute-done | bytes 327712 | tf_op jit(solution)/shard_map/ppermute | solution.py:267
  246.9 0.0 copy-start.4
  246.9 0.0 collective-permute-done.5.refs_4_
  246.9 0.0 copy-start.5
  246.9 0.0 copy-done.3
  246.9 0.7 copy-done.4
  247.6 0.1 copy-done.5
  247.7 3.8 %combine.1 = (bf16[192,1024]{1,0:T(8,128)(2,1)}, bf16[2,192]{1,0:T(2,128)(2,1)}) custom-call(s32[1]{0:T(128)} %bitcast.refs_0_, s32[2,192]{1,0:T(2,128)} %bitcast.29, bf16[2,192]{1,0:T(2,128)(2,1)} %bitcast.31, bf16[1280,128]{1,0:T(8,128)(2,1)} %bitcast.21, bf16[1280,128]{1,0:T(8,128)(2,1)} %copy-done.5, bf16[1280,128]{1,0:T(8,128)(2,1)} %copy-done.3, ...), custom_call_target="tpu_custom_call" | custom-call | tf_op jit(solution)/shard_map/combine/pallas_call | solution.py:363
  251.5 3.0 %reduce-scatter.2.cloned.1.call-done = bf16[1,256,1024]{2,1,0:T(8,128)(2,1)} async-done(((bf16[4,256,1024]{2,1,0:T(8,128)(2,1)}), bf16[1,256,1024]{2,1,0:T(8,128)(2,1)}) %reduce-scatter.2.cloned.1.call-update) | async-done | bytes 524304 | tf_op jit(solution)/shard_map/reduce_scatter | solution.py:339
  254.5 2.1 finish.1
Async XLA Ops:
  7.2 125.7 %all-gather.3.cloned.1.call-start = ((), (), s32[]{:S(2)}) async-start(), calls=%async_computation.4 | async-start | bytes 2621440 | tf_op jit(solution)/shard_map/all_gather | solution.py:284
  9.1 245.4 %reduce-scatter.2.cloned.1.call-start = ((), (), s32[]{:S(2)}) async-start(), calls=%async_computation.3 | async-start | bytes 2621440 | tf_op jit(solution)/shard_map/reduce_scatter | solution.py:339
  56.3 60.5 %collective-permute-start = (bf16[144,2048]{1,0:T(8,128)(2,1)}, bf16[144,2048]{1,0:T(8,128)(2,1)S(1)}, u32[]{:S(2)}, u32[]{:S(2)}) collective-permute-start(bf16[144,2048]{1,0:T(8,128)(2,1)} %get-tuple-element.27), channel_id=1, source_target_pairs={{0,4},{1,5},{2,6},{3,7},{16,20},{17,21},{18,22},{19,23},{32,36},{3... | collective-permute-start | bytes 1769480 | tf_op jit(solution)/shard_map/ppermute | solution.py:267
  60.2 71.1 %collective-permute-start.1 = (bf16[144,2048]{1,0:T(8,128)(2,1)}, bf16[144,2048]{1,0:T(8,128)(2,1)S(1)}, u32[]{:S(2)}, u32[]{:S(2)}) collective-permute-start(bf16[144,2048]{1,0:T(8,128)(2,1)} %get-tuple-element.28), channel_id=1, source_target_pairs={{0,8},{1,9},{2,10},{3,11},{16,24},{17,25},{18,26},{19,27},{32,40},... | collective-permute-start | bytes 1769480 | tf_op jit(solution)/shard_map/ppermute | solution.py:267
  65.4 65.9 %collective-permute-start.2 = (bf16[144,2048]{1,0:T(8,128)(2,1)}, bf16[144,2048]{1,0:T(8,128)(2,1)S(1)}, u32[]{:S(2)}, u32[]{:S(2)}) collective-permute-start(bf16[144,2048]{1,0:T(8,128)(2,1)} %get-tuple-element.29), channel_id=1, source_target_pairs={{0,396},{1,397},{2,398},{3,399},{16,412},{17,413},{18,414},{19,415... | collective-permute-start | bytes 1769480 | tf_op jit(solution)/shard_map/ppermute | solution.py:267
  132.6 2.2 copy-start
  132.8 7.2 %collective-permute-start.3 = (bf16[576,2048]{1,0:T(8,128)(2,1)S(1)}, bf16[576,2048]{1,0:T(8,128)(2,1)S(1)}, u32[]{:S(2)}, u32[]{:S(2)}) collective-permute-start(bf16[576,2048]{1,0:T(8,128)(2,1)S(1)} %pad_maximum_fusion.rows_ref.mine_ref), channel_id=1, source_target_pairs={{0,64},{64,0},{128,192},{192,128},{256,320},{320,256},{384,448},{4... | collective-permute-start | bytes 7077896 | tf_op jit(solution)/shard_map/ppermute | solution.py:277
  140.1 1.4 copy-start.1
  156.6 5.3 %collective-permute-start.4 = (bf16[576,1152]{1,0:T(8,128)(2,1)}, bf16[576,1152]{1,0:T(8,128)(2,1)S(1)}, u32[]{:S(2)}, u32[]{:S(2)}) collective-permute-start(bf16[576,1152]{1,0:T(8,128)(2,1)} %get-tuple-element.39), channel_id=1, source_target_pairs={{0,64},{64,0},{128,192},{192,128},{256,320},{320,256},{384,448},{4... | collective-permute-start | bytes 3981320 | tf_op jit(solution)/shard_map/ppermute | solution.py:277
  161.9 1.1 copy-start.2
  195.3 35.6 %collective-permute-start.6 = (bf16[1280,128]{1,0:T(8,128)(2,1)S(1)}, bf16[1280,128]{1,0:T(8,128)(2,1)S(1)}, u32[]{:S(2)}, u32[]{:S(2)}) collective-permute-start(bf16[1280,128]{1,0:T(8,128)(2,1)S(1)} %bitcast.25), channel_id=1, source_target_pairs={{8,0},{9,1},{10,2},{11,3},{24,16},{25,17},{26,18},{27,19},{40,32},... | collective-permute-start | bytes 983048 | tf_op jit(solution)/shard_map/ppermute | solution.py:267
  199.2 47.7 %collective-permute-start.7 = (bf16[1280,128]{1,0:T(8,128)(2,1)S(1)}, bf16[1280,128]{1,0:T(8,128)(2,1)S(1)}, u32[]{:S(2)}, u32[]{:S(2)}) collective-permute-start(bf16[1280,128]{1,0:T(8,128)(2,1)S(1)} %bitcast.24), channel_id=1, source_target_pairs={{396,0},{397,1},{398,2},{399,3},{412,16},{413,17},{414,18},{415,19... | collective-permute-start | bytes 983048 | tf_op jit(solution)/shard_map/ppermute | solution.py:267
  201.2 45.7 %collective-permute-start.5 = (bf16[1280,128]{1,0:T(8,128)(2,1)S(1)}, bf16[1280,128]{1,0:T(8,128)(2,1)S(1)}, u32[]{:S(2)}, u32[]{:S(2)}) collective-permute-start(bf16[1280,128]{1,0:T(8,128)(2,1)S(1)} %bitcast.23), channel_id=1, source_target_pairs={{4,0},{5,1},{6,2},{7,3},{20,16},{21,17},{22,18},{23,19},{36,32},{3... | collective-permute-start | bytes 983048 | tf_op jit(solution)/shard_map/ppermute | solution.py:267
  230.9 16.0 %copy-start.3 = (bf16[1280,128]{1,0:T(8,128)(2,1)}, bf16[1280,128]{1,0:T(8,128)(2,1)S(1)}, u32[]{:S(2)}) copy-start(bf16[1280,128]{1,0:T(8,128)(2,1)S(1)} %collective-permute-done.6.refs_5_) | copy-start | bytes 983044
  246.9 0.7 copy-start.4
  246.9 0.8 copy-start.5
Sparse Core Ops, SparseCore 0:
  10.7 122.0 all-gather.2
  151.4 103.0 reduce-scatter.1
